TPU v7x, 128 devices: a whole 4x4x4 slice. The times are simulated.
128 devices in a mesh: gx: 8 (over y, core), gy: 16 (over z, x).
Axes of the slice: x: 4, y: 4, z: 4, core: 2. Of those that a mesh axis runs over, the one named last changes fastest.
Arguments:
- slope_depth: float32 [2048, 8192], P('gx', 'gy'), may hold values from 0.2 to 2
- slope_momentum: float32 [2, 2048, 8192], P(None, 'gx', 'gy'), may hold values from -1.2 to 1.2
- bed_slope: float32 [2, 2048, 8192], P(None, 'gx', 'gy'), may hold values from -3 to 3
- friction: float32 [2048, 8192], P('gx', 'gy'), may hold values from 0.2 to 2
- slope_active: int32 [2048, 8192], P('gx', 'gy'), may hold values 0 or 1
- owners: int32 [8, 16, 256, 1], P('gx', 'gy'), may hold values from 0 to 127; in each aligned block of 256 rows (0 to 255, 256 to 511, ..., all dimensions but the last counted through in order) at most 4 rows name the same one
- offsets: int32 [8, 16, 256], P('gx', 'gy'), may hold values from 0 to 511
- lake_height: float32 [4096, 8192], P('gx', 'gy'), may hold values from -6 to 6
- lake_momentum: float32 [2, 4096, 8192], P(None, 'gx', 'gy'), may hold values from -16 to 16
- lake_diagonal: float32 [4096, 8192], P('gx', 'gy'), may hold values from 0.2 to 2
Outputs:
- slope_fields: float32 [3, 2048, 8192], P(None, 'gx', 'gy')
- new_height: float32 [4096, 8192], P('gx', 'gy')
- new_momentum: float32 [2, 4096, 8192], P(None, 'gx', 'gy')
Inputs may be any that keep to these rules, and one draw needn't show every extreme that they name: `owners`: among the 256 rows of one device, no owner is named by more than 4 rows, a bound that some block reaches.
All inputs are finite; a program needn't handle non-finite values. No bound on the sum of `slope_active` on one device may be relied on, other than what follows from the above.
Results may differ from a plain program's by a relative error of at most 0.0001.
Values sent between devices are 32-bit elements; how exact they have to be, the bound alone decides.
No kernel may reach another device: no remote copies, remote signals or barrier semaphores. Data moves between devices by JAX's collectives and lax.ppermute only.
A program may use at most 128 MiB of HBM per device.

v0:
```python
import jax
import jax.numpy as jnp
from jax import lax
from jax.sharding import PartitionSpec as P

SECTIONS = 2
ITERS = 3


courant = 0.15
depth_floor = 0.25
dispersion = 0.5


def with_halo(shard, sides, width):
    for axis, dim in sides:
        peers, length = (lax.axis_size(axis), shard.shape[dim])
        up = [(i, (i + 1) % peers) for i in range(peers - 1)]
        down = [(j, i) for i, j in up]
        last = lax.slice_in_dim(shard, length - width, length, axis=dim)
        first = lax.slice_in_dim(shard, 0, width, axis=dim)
        before = lax.ppermute(last, axis, up)
        after = lax.ppermute(first, axis, down)
        shard = jnp.concatenate([before, shard, after], axis=dim)
    return shard


def advance(fields, padded, bed_slope, friction, active):
    height = padded[0]
    floored = jnp.maximum(height, depth_floor)
    along_speed = padded[1] / floored
    across_speed = padded[2] / floored
    pressure = 0.5 * height * height
    flux_along = jnp.stack([padded[1], padded[1] * along_speed + pressure, padded[2] * along_speed])
    flux_across = jnp.stack(
        [padded[2], padded[1] * across_speed, padded[2] * across_speed + pressure]
    )
    average = 0.25 * (
        padded[:, 2:, 1:-1] + padded[:, :-2, 1:-1] + padded[:, 1:-1, 2:] + padded[:, 1:-1, :-2]
    )
    update = average - 0.5 * courant * (flux_along[:, 2:, 1:-1] - flux_along[:, :-2, 1:-1])
    update = update - 0.5 * courant * (flux_across[:, 1:-1, 2:] - flux_across[:, 1:-1, :-2])
    forcing = jnp.stack(
        [
            jnp.zeros_like(fields[0]),
            fields[0] * bed_slope[0] - friction * fields[1],
            fields[0] * bed_slope[1] - friction * fields[2],
        ]
    )
    return (update + courant * forcing) * active[None]


def operate(vectors, lake_diagonal):
    padded = with_halo(vectors, (("gx", 1), ("gy", 2)), 1)
    beside = padded[:, 2:, 1:-1] + padded[:, :-2, 1:-1] + padded[:, 1:-1, 2:] + padded[:, 1:-1, :-2]
    return (1.0 + 4.0 * dispersion + lake_diagonal)[None] * vectors - dispersion * beside


def squares(residual):
    return lax.psum(jnp.sum(residual * residual, axis=(1, 2)), ("gx", "gy"))


def per_device(
    slope_depth,
    slope_momentum,
    bed_slope,
    friction,
    slope_active,
    owners,
    offsets,
    lake_height,
    lake_momentum,
    lake_diagonal,
):
    active = slope_active.astype(jnp.float32)
    fields = jnp.concatenate([slope_depth[None], slope_momentum], axis=0)
    for section_index in range(SECTIONS):
        padded = with_halo(fields, (("gx", 1), ("gy", 2)), 1)
        fields = advance(fields, padded, bed_slope, friction, active)
    along_count = lax.axis_size("gx")
    across_count = lax.axis_size("gy")
    devices = along_count * across_count
    rows_here = fields.shape[1]
    columns = fields.shape[2]
    capacity = max(2, 2 * rows_here // devices)
    owner_list = owners.reshape(rows_here)
    offset_list = offsets.reshape(rows_here)
    matches = (owner_list[:, None] == jnp.arange(devices, dtype=jnp.int32)[None, :]).astype(
        jnp.int32
    )
    earlier = jnp.cumsum(matches, axis=0) - matches
    rank_in_owner = jnp.sum(earlier * matches, axis=1)
    slot_index = owner_list * capacity + rank_in_owner
    row_major = jnp.transpose(fields, (1, 0, 2))
    payload = jnp.zeros((devices * capacity, 3, columns), jnp.float32).at[slot_index].set(row_major)
    tags = (
        jnp.zeros((devices * capacity,), jnp.float32)
        .at[slot_index]
        .set((offset_list + 1).astype(jnp.float32))
    )
    payload = payload.reshape(devices, capacity, 3, columns)
    tags = tags.reshape(devices, capacity)
    received, got_tags = (
        lax.all_to_all(payload, ("gx", "gy"), split_axis=0, concat_axis=0, tiled=True),
        lax.all_to_all(tags, ("gx", "gy"), split_axis=0, concat_axis=0, tiled=True),
    )
    received = received.reshape(devices * capacity, 3, columns)
    got_tags = got_tags.reshape(devices * capacity).astype(jnp.int32)
    lake_rows = lake_height.shape[0]
    landing = jnp.where(got_tags > 0, got_tags - 1, lake_rows)
    placed = jnp.zeros((lake_rows + 1, 3, columns), jnp.float32).at[landing].add(received)
    inflow = jnp.transpose(placed[:lake_rows], (1, 0, 2))
    new_height = lake_height + inflow[0]
    right_side = lake_momentum + inflow[1:]
    solution = jnp.zeros_like(right_side)
    residual = right_side
    direction = right_side
    norm_now = squares(residual)
    for iteration in range(ITERS):
        applied = operate(direction, lake_diagonal)
        curvature_sum = lax.psum(jnp.sum(direction * applied, axis=(1, 2)), ("gx", "gy"))
        step_length = norm_now / curvature_sum
        solution = solution + step_length[:, None, None] * direction
        residual = residual - step_length[:, None, None] * applied
        norm_next = squares(residual)
        direction = residual + (norm_next / norm_now)[:, None, None] * direction
        norm_now = norm_next
    return (fields, new_height, solution)


def solution(mesh):
    return jax.shard_map(
        per_device,
        mesh=mesh,
        in_specs=(
            P("gx", "gy"),
            P(None, "gx", "gy"),
            P(None, "gx", "gy"),
            P("gx", "gy"),
            P("gx", "gy"),
            P("gx", "gy", None, None),
            P("gx", "gy", None),
            P("gx", "gy"),
            P(None, "gx", "gy"),
            P("gx", "gy"),
        ),
        out_specs=(P(None, "gx", "gy"), P("gx", "gy"), P(None, "gx", "gy")),
        check_vma=False,
    )
```

profile of v0, /device:TPU:1, one launch (start us, length us, event | category | flops | bytes accessed | tf_op | source)
XLA Modules:
  0.0 694.5 jit_solution(2772342991964344457)
XLA Ops:
  1.6 4.6 collective-permute-start.1
  6.2 1.9 collective-permute-start
  11.3 3.1 collective-permute-start.3
  15.9 6.4 collective-permute-done.3
  22.2 4.1 collective-permute-done.2
  27.9 4.1 fusion.30
  32.0 5.0 collective-permute-start.5
  37.1 1.9 collective-permute-start.4
  41.2 12.0 %all-to-all-start = ((f32[128,1,4]{2,1,0:T(1,128)}), f32[128,1,4]{2,1,0:T(1,128)S(1)}, u32[]{:S(2)}, u32[]{:S(2)}) async-start(f32[128,1,4]{2,1,0:T(1,128)} %bitcast.21), calls=%async_computation | async-start | bytes 131072 | tf_op jit(solution)/shard_map/all_to_all | solution.py:105
  53.4 3.3 collective-permute-start.7
  58.6 6.4 collective-permute-done.7
  65.0 3.9 collective-permute-done.6
  71.2 3.8 fusion.20
  77.2 2.5 broadcast_in_dim.16
  79.7 26.5 %scatter_fusion = f32[512,3,512]{2,1,0:T(4,128)} fusion(f32[512,3,512]{2,1,0:T(4,128)} %broadcast_in_dim.16, s32[256]{0:T(256)S(1)} %bitcast.105, f32[256,3,512]{2,1,0:T(4,128)S(1)} %copy.43), kind=kCustom, calls=%fused_computation.1 | custom fusion | bytes 4719616 | tf_op jit(solution)/shard_map/scatter | solution.py:95
  106.2 5.4 copy.44
  111.6 12.8 %all-to-all-start.1 = ((f32[128,4,3,512]{3,1,2,0:T(4,128)}), f32[128,4,3,512]{3,1,2,0:T(4,128)S(1)}, u32[]{:S(2)}, u32[]{:S(2)}) async-start(f32[128,4,3,512]{3,1,2,0:T(4,128)} %copy.44), calls=%async_computation.1 | async-start | bytes 6291456 | tf_op jit(solution)/shard_map/all_to_all | solution.py:104
  124.8 40.0 %all-to-all-done.1 = f32[128,4,3,512]{3,1,2,0:T(4,128)S(1)} async-done(((f32[128,4,3,512]{3,1,2,0:T(4,128)}), f32[128,4,3,512]{3,1,2,0:T(4,128)S(1)}, u32[]{:S(2)}, u32[]{:S(2)}) %all-to-all-start.1) | async-done | bytes 3145760 | tf_op jit(solution)/shard_map/all_to_all | solution.py:104
  164.8 3.8 copy.61
  168.6 2.5 broadcast_in_dim.13
  171.1 65.1 %scatter_fusion.1 = f32[513,3,512]{2,1,0:T(4,128)} fusion(f32[513,3,512]{2,1,0:T(4,128)} %broadcast_in_dim.13, s32[512]{0:T(512)S(1)} %bitcast.103, f32[512,3,512]{2,1,0:T(4,128)} %bitcast.92), kind=kCustom, calls=%fused_computation.2 | custom fusion | flops 786432 | bytes 9439232 | tf_op jit(solution)/shard_map/scatter-add | solution.py:111
  236.2 3.1 slice_bitcast_fusion
  239.3 2.3 slice_add_fusion
  241.6 3.1 collective-permute-start.9
  244.7 3.7 collective-permute-start.8
  250.9 2.6 collective-permute-start.11
  260.0 16.1 %multiply_reduce_fusion.3 = (f32[2]{0:T(128)S(1)}, f32[2]{0:T(128)S(1)}, f32[2,512,512]{2,0,1:T(2,128)}) fusion(f32[2,512,512]{2,0,1:T(2,128)S(1)} %slice_add_fusion, f32[2,1,512]{2,0,1:T(2,128)S(1)} %collective-permute-done.8, f32[2,1,512]{2,0,1:T(2,128)S(1)} %collective-permute-done.9, f32[2,514,1]{2,0,1:T(2,128)} %copy.51, f32[2,514,1]{2,0,1:T(2,128)} %copy.49, ...), kind=kLoop, calls=%fused_computation.53 | loop fusion | flops 9437180 | bytes 5259312 | tf_op jit(solution)/shard_map/reduce_sum | solution.py:121
  276.1 67.4 %all-reduce = (f32[2]{0:T(128)S(1)}, f32[2]{0:T(128)S(1)}) all-reduce(f32[2]{0:T(128)S(1)} %get-tuple-element.13, f32[2]{0:T(128)S(1)} %get-tuple-element.12), channel_id=1, replica_groups=mesh['gx'=8,'gy'=16] {'gx','gy'}, use_global_device_ids=true, to_apply=%region_7.8 | all-reduce | flops 4 | bytes 32 | tf_op jit(solution)/shard_map/psum | solution.py:60
  343.5 4.6 multiply_reduce_fusion.2
  348.1 62.9 %psum.44 = f32[2]{0:T(128)S(1)} all-reduce(f32[2]{0:T(128)S(1)} %get-tuple-element.20), channel_id=1, replica_groups=mesh['gx'=8,'gy'=16] {'gx','gy'}, use_global_device_ids=true, to_apply=%region_11.12 | all-reduce | flops 2 | bytes 16 | tf_op jit(solution)/shard_map/psum | solution.py:60
  411.1 2.7 multiply_add_fusion.2
  413.8 3.0 collective-permute-start.13
  416.8 1.9 collective-permute-start.12
  418.8 3.0 collective-permute-done.12
  421.8 1.8 pad_maximum_fusion.55
  427.3 4.0 collective-permute-start.15
  433.5 15.6 %multiply_reduce_fusion.1 = (f32[2]{0:T(128)S(1)}, f32[2,512,512]{2,0,1:T(2,128)}) fusion(f32[2,512,512]{2,0,1:T(2,128)} %copy-done, f32[2,1,512]{2,0,1:T(2,128)S(1)} %collective-permute-done.12, f32[2,1,512]{2,0,1:T(2,128)S(1)} %collective-permute-done.13, f32[2,514,1]{2,0,1:T(2,128)} %copy.55, f32[2,514,1]{2,0,1:T(2,128)} %copy.53, ...), kind=kLoop, calls=%fused_computation.49 | loop fusion | flops 8388606 | bytes 5259304 | tf_op jit(solution)/shard_map/reduce_sum | solution.py:121
  449.1 66.6 %psum.45 = f32[2]{0:T(128)S(1)} all-reduce(f32[2]{0:T(128)S(1)} %get-tuple-element.18), channel_id=1, replica_groups=mesh['gx'=8,'gy'=16] {'gx','gy'}, use_global_device_ids=true, to_apply=%region_13.14 | all-reduce | flops 2 | bytes 16 | tf_op jit(solution)/shard_map/psum | solution.py:121
  515.7 5.2 multiply_reduce_fusion
  520.9 62.8 %psum.46 = f32[2]{0:T(128)S(1)} all-reduce(f32[2]{0:T(128)S(1)} %get-tuple-element.16), channel_id=1, replica_groups=mesh['gx'=8,'gy'=16] {'gx','gy'}, use_global_device_ids=true, to_apply=%region_15.16 | all-reduce | flops 2 | bytes 16 | tf_op jit(solution)/shard_map/psum | solution.py:60
  583.7 3.4 multiply_add_fusion.1
  587.1 3.0 collective-permute-start.17
  590.2 1.9 collective-permute-start.16
  592.1 3.0 collective-permute-done.16
  600.7 4.0 collective-permute-start.19
  606.8 15.1 %fusion.16 = f32[2]{0:T(128)S(1)} fusion(f32[2,512,512]{2,0,1:T(2,128)} %copy-done.1, f32[2,1,512]{2,0,1:T(2,128)S(1)} %collective-permute-done.16, f32[2,1,512]{2,0,1:T(2,128)S(1)} %collective-permute-done.17, f32[2,514,1]{2,0,1:T(2,128)} %copy.59, f32[2,514,1]{2,0,1:T(2,128)} %copy.57, f32[512,512]{1,0:T(8,128)S(1)} %broadcast_add_fusion), kind=kLoop, calls=%fused_computation.55 | loop fusion | flops 8388606 | bytes 3162152 | tf_op jit(solution)/shard_map/reduce_sum | solution.py:121
  623.1 66.4 %psum.47 = f32[2]{0:T(128)S(1)} all-reduce(f32[2]{0:T(128)S(1)} %fusion.16), channel_id=1, replica_groups=mesh['gx'=8,'gy'=16] {'gx','gy'}, use_global_device_ids=true, to_apply=%region_17.18 | all-reduce | flops 2 | bytes 16 | tf_op jit(solution)/shard_map/psum | solution.py:121
  689.5 3.2 multiply_add_fusion
  (111 shorter events, 41.6 us)
Async XLA Ops:
  0.6 8.6 %copy-start.2 = (f32[2,256,512]{2,1,0:T(8,128)S(1)}, f32[2,256,512]{2,1,0:T(8,128)}, u32[]{:S(2)}) copy-start(f32[2,256,512]{2,1,0:T(8,128)} %param.11) | copy-start | bytes 3145732
  0.6 8.6 %copy-start.3 = (f32[256,512]{1,0:T(8,128)S(1)}, f32[256,512]{1,0:T(8,128)}, u32[]{:S(2)}) copy-start(f32[256,512]{1,0:T(8,128)} %param.10) | copy-start | bytes 1572868
  0.7 8.6 %copy-start.10 = (f32[256,512]{1,0:T(8,128)S(1)}, f32[256,512]{1,0:T(8,128)}, u32[]{:S(2)}) copy-start(f32[256,512]{1,0:T(8,128)} %param.13) | copy-start | bytes 1572868
  1.6 9.4 %collective-permute-start.1 = (f32[3,1,512]{2,1,0:T(1,128)S(1)}, f32[3,1,512]{2,1,0:T(1,128)S(1)}, u32[]{:S(2)}, u32[]{:S(2)}) collective-permute-start(f32[3,1,512]{2,1,0:T(1,128)S(1)} %get-tuple-element.57), channel_id=1, source_target_pairs={{0,16},{16,32},{32,48},{48,64},{64,80},{80,96},{96,112},{1,17},{17... | collective-permute-start | bytes 18440 | tf_op jit(solution)/shard_map/ppermute | solution.py:22
  6.2 4.9 collective-permute-start
  9.2 1.6 copy-start.14
  10.8 5.0 copy-start.13
  11.3 10.9 %collective-permute-start.3 = (f32[3,258,1]{2,1,0:T(8,128)S(1)}, f32[3,258,1]{2,1,0:T(8,128)S(1)}, u32[]{:S(2)}, u32[]{:S(2)}) collective-permute-start(f32[3,258,1]{2,1,0:T(8,128)S(1)} %get-tuple-element.53), channel_id=1, source_target_pairs={{0,1},{1,2},{2,3},{3,4},{4,5},{5,6},{6,7},{7,8},{8,9},{9,10},{10,1... | collective-permute-start | bytes 9296 | tf_op jit(solution)/shard_map/ppermute | solution.py:22
  14.5 11.9 %collective-permute-start.2 = (f32[3,258,1]{2,1,0:T(8,128)S(1)}, f32[3,258,1]{2,1,0:T(8,128)S(1)}, u32[]{:S(2)}, u32[]{:S(2)}) collective-permute-start(f32[3,258,1]{2,1,0:T(8,128)S(1)} %get-tuple-element.54), channel_id=1, source_target_pairs={{1,0},{2,1},{3,2},{4,3},{5,4},{6,5},{7,6},{8,7},{9,8},{10,9},{11,1... | collective-permute-start | bytes 9296 | tf_op jit(solution)/shard_map/ppermute | solution.py:23
  15.9 12.0 %copy-start.6 = (f32[256,512]{1,0:T(8,128)}, f32[256,512]{1,0:T(8,128)S(1)}, u32[]{:S(2)}) copy-start(f32[256,512]{1,0:T(8,128)S(1)} %convert_element_type.27) | copy-start | bytes 1572868
  27.8 11.2 %copy-start.15 = (s32[1,1,256]{2,1,0:T(1,128)S(1)}, s32[1,1,256]{2,1,0:T(1,128)}, u32[]{:S(2)}) copy-start(s32[1,1,256]{2,1,0:T(1,128)} %param.16) | copy-start | bytes 3076
  32.0 26.2 %copy-start.8 = (f32[2,256,512]{2,1,0:T(8,128)S(1)}, f32[2,256,512]{2,1,0:T(8,128)}, u32[]{:S(2)}) copy-start(f32[2,256,512]{2,1,0:T(8,128)} %param.12) | copy-start | bytes 3145732
  32.0 26.2 %copy-start.11 = (f32[256,512]{1,0:T(8,128)S(1)}, f32[256,512]{1,0:T(8,128)}, u32[]{:S(2)}) copy-start(f32[256,512]{1,0:T(8,128)} %param.13) | copy-start | bytes 1572868
  32.0 21.1 %collective-permute-start.5 = (f32[3,1,512]{2,1,0:T(1,128)S(1)}, f32[3,1,512]{2,1,0:T(1,128)S(1)}, u32[]{:S(2)}, u32[]{:S(2)}) collective-permute-start(f32[3,1,512]{2,1,0:T(1,128)S(1)} %get-tuple-element.55), channel_id=1, source_target_pairs={{0,16},{16,32},{32,48},{48,64},{64,80},{80,96},{96,112},{1,17},{17... | collective-permute-start | bytes 18440 | tf_op jit(solution)/shard_map/ppermute | solution.py:22
  37.1 16.1 %collective-permute-start.4 = (f32[3,1,512]{2,1,0:T(1,128)S(1)}, f32[3,1,512]{2,1,0:T(1,128)S(1)}, u32[]{:S(2)}, u32[]{:S(2)}) collective-permute-start(f32[3,1,512]{2,1,0:T(1,128)S(1)} %get-tuple-element.56), channel_id=1, source_target_pairs={{16,0},{32,16},{48,32},{64,48},{80,64},{96,80},{112,96},{17,1},{33... | collective-permute-start | bytes 18440 | tf_op jit(solution)/shard_map/ppermute | solution.py:23
  41.2 70.4 %all-to-all-start = ((f32[128,1,4]{2,1,0:T(1,128)}), f32[128,1,4]{2,1,0:T(1,128)S(1)}, u32[]{:S(2)}, u32[]{:S(2)}) async-start(f32[128,1,4]{2,1,0:T(1,128)} %bitcast.21), calls=%async_computation | async-start | bytes 131072 | tf_op jit(solution)/shard_map/all_to_all | solution.py:105
  53.4 11.6 %collective-permute-start.7 = (f32[3,258,1]{2,1,0:T(8,128)S(1)}, f32[3,258,1]{2,1,0:T(8,128)S(1)}, u32[]{:S(2)}, u32[]{:S(2)}) collective-permute-start(f32[3,258,1]{2,1,0:T(8,128)S(1)} %get-tuple-element.51), channel_id=1, source_target_pairs={{0,1},{1,2},{2,3},{3,4},{4,5},{5,6},{6,7},{7,8},{8,9},{9,10},{10,1... | collective-permute-start | bytes 9296 | tf_op jit(solution)/shard_map/ppermute | solution.py:22
  56.7 12.2 %collective-permute-start.6 = (f32[3,258,1]{2,1,0:T(8,128)S(1)}, f32[3,258,1]{2,1,0:T(8,128)S(1)}, u32[]{:S(2)}, u32[]{:S(2)}) collective-permute-start(f32[3,258,1]{2,1,0:T(8,128)S(1)} %get-tuple-element.52), channel_id=1, source_target_pairs={{1,0},{2,1},{3,2},{4,3},{5,4},{6,5},{7,6},{8,7},{9,8},{10,9},{11,1... | collective-permute-start | bytes 9296 | tf_op jit(solution)/shard_map/ppermute | solution.py:23
  70.1 1.0 copy-start.7
  75.0 1.1 copy-start.5
  111.6 53.2 %all-to-all-start.1 = ((f32[128,4,3,512]{3,1,2,0:T(4,128)}), f32[128,4,3,512]{3,1,2,0:T(4,128)S(1)}, u32[]{:S(2)}, u32[]{:S(2)}) async-start(f32[128,4,3,512]{3,1,2,0:T(4,128)} %copy.44), calls=%async_computation.1 | async-start | bytes 6291456 | tf_op jit(solution)/shard_map/all_to_all | solution.py:104
  236.2 3.1 copy-start.9
  239.3 2.3 copy-start.4
  241.6 6.8 collective-permute-start.9
  244.7 4.9 collective-permute-start.8
  250.9 8.1 %collective-permute-start.11 = (f32[2,514,1]{1,0,2:T(2,128)S(1)}, f32[2,514,1]{1,0,2:T(2,128)S(1)}, u32[]{:S(2)}, u32[]{:S(2)}) collective-permute-start(f32[2,514,1]{1,0,2:T(2,128)S(1)} %copy.50), channel_id=1, source_target_pairs={{0,1},{1,2},{2,3},{3,4},{4,5},{5,6},{6,7},{7,8},{8,9},{9,10},{10,1... | collective-permute-start | bytes 12344 | tf_op jit(solution)/shard_map/ppermute | solution.py:22
  253.5 4.4 collective-permute-start.10
  413.8 8.0 %copy-start = (f32[2,512,512]{2,0,1:T(2,128)}, f32[2,512,512]{2,0,1:T(2,128)S(1)}, u32[]{:S(2)}) copy-start(f32[2,512,512]{2,0,1:T(2,128)S(1)} %multiply_add_fusion.2) | copy-start | bytes 6291460
  413.8 4.9 collective-permute-start.13
  416.8 4.9 collective-permute-start.12
  424.8 6.6 collective-permute-start.14
  427.3 5.1 collective-permute-start.15
  587.1 8.0 %copy-start.1 = (f32[2,512,512]{2,0,1:T(2,128)}, f32[2,512,512]{2,0,1:T(2,128)S(1)}, u32[]{:S(2)}) copy-start(f32[2,512,512]{2,0,1:T(2,128)S(1)} %multiply_add_fusion.1) | copy-start | bytes 6291460
  587.1 4.9 collective-permute-start.17
  590.2 4.9 collective-permute-start.16
  598.1 6.6 collective-permute-start.18
  600.7 5.1 collective-permute-start.19
  606.8 15.1 %slice-start = ((f32[3,512,512]{2,0,1:T(4,128)}), f32[1,512,512]{2,0,1:T(1,128)S(1)}, s32[]{:S(2)}) async-start(f32[3,512,512]{2,0,1:T(4,128)} %copy-done.4), calls=%async_computation.2 | async-start | bytes 2097152 | tf_op jit(solution)/shard_map/slice | solution.py:113
  606.8 15.1 %copy-start.12 = (f32[512,512]{1,0:T(8,128)S(1)}, f32[512,512]{1,0:T(8,128)}, u32[]{:S(2)}) copy-start(f32[512,512]{1,0:T(8,128)} %param.17) | copy-start | bytes 3145732
where the time goes:
time: 704 us; the launch traced here: 695 us
  blocking collectives  326 us (46%)
  other arithmetic  155 us (22%)
  starting transfers between devices  78.6 us (11%)
  waiting for transfers between devices  69.8 us (10%)
  local copies, waits for them, and re-layouts  63.5 us (9%)
    psum x3, blocking collectives, squares(): return lax.psum(jnp.sum(residual * residual, axis=(1, 2)), ('gx', 'gy'))  193 us
    psum x2, blocking collectives, per_device(): lax.psum(jnp.sum(direction * applied, axis=(1, 2)), ('gx', 'gy'))  133 us
    scatter-add x1, other arithmetic, per_device(): jnp.zeros((lake_rows + 1, 3, columns), jnp.float32).at[landing]  65.1 us
    reduce_sum x3, other arithmetic, per_device(): jnp.sum(direction * applied, axis=(1, 2))  46.8 us
    all_to_all x1, waiting for transfers between devices, per_device(): lax.all_to_all(payload, ('gx', 'gy'), split_axis=0, concat_axis=0, tiled=...  40 us
    ppermute x10, starting transfers between devices, with_halo(): before = lax.ppermute(last, axis, up)  35.7 us
    scatter x1, local copies, waits for them, and re-layouts, per_device(): jnp.zeros((devices * capacity, 3, columns), jnp.float32).at[slot_index]  26.5 us
    ppermute x10, starting transfers between devices, with_halo(): after = lax.ppermute(first, axis, down)  18.1 us
  transfers between devices with their start and end apart: 22, of which 10 were waited for; matrix products, arithmetic and copies ran while one was open for 8% of the time, Pallas kernels for 0%

commit v1 on v0

v1 whole, which is shorter than its diff:
```python
import functools

import jax
import jax.numpy as jnp
from jax import lax
from jax.experimental import pallas as pl
from jax.experimental.pallas import tpu as pltpu
from jax.sharding import PartitionSpec as P

F32 = jnp.float32
BF16 = jnp.bfloat16
AXES = ("gx", "gy")
NX, NY = 8, 16
DEV = NX * NY
R, C, L = 256, 512, 512
CAP = 4
UNITS = 12 * CAP + 1
TAG = 12 * CAP
WIDE = C + 128
TOP = 16
SROWS = R + 3 * TOP
LROWS = L + 2 * TOP
MIB = 1 << 20


def params(limit):
    return pltpu.CompilerParams(vmem_limit_bytes=limit * MIB)


def lanes(shape):
    return lax.broadcasted_iota(jnp.int32, shape, len(shape) - 1)


def rows(shape):
    return lax.broadcasted_iota(jnp.int32, shape, len(shape) - 2)


def next_row(x, i, r, n, width):
    block = x[i, pl.ds(r, n + 8), 0:width]
    return pltpu.roll(block, n + 7, 0)[0:n, :]


def previous_row(x, i, r, n, width):
    block = x[i, pl.ds(pl.multiple_of(r - 8, 8), n + 8), 0:width]
    return pltpu.roll(block, 1, 0)[8 : n + 8, :]


def edge_rows_kernel(ht, hb, mt, mb, bt, bb, ft, fb, at, ab, dt, db, up, dn):
    for out, h, m, b, f, a, d, two, one in (
        (up, ht, mt, bt, ft, at, dt, slice(0, 2), slice(0, 1)),
        (dn, hb, mb, bb, fb, ab, db, slice(6, 8), slice(7, 8)),
    ):
        out[0:2, :] = h[two, :]
        out[2:4, :] = m[0, two, :]
        out[4:6, :] = m[1, two, :]
        out[6:7, :] = b[0, one, :]
        out[7:8, :] = b[1, one, :]
        out[8:9, :] = f[one, :]
        out[9:10, :] = a[one, :].astype(F32)
        out[10:12, :] = d[two, :]
        out[12:16, :] = jnp.zeros((4, C), F32)


def edge_rows(h, mom, bed, fric, act, d):
    last, lake_last = R // 8 - 1, L // 8 - 1
    two = lambda r: pl.BlockSpec((8, C), lambda i: (r, 0))
    three = lambda r: pl.BlockSpec((2, 8, C), lambda i: (0, r, 0))
    return pl.pallas_call(
        edge_rows_kernel,
        grid=(1,),
        in_specs=[two(0), two(last), three(0), three(last), three(0), three(last), two(0), two(last), two(0), two(last), two(0), two(lake_last)],
        out_specs=[pl.BlockSpec((16, C), lambda i: (0, 0))] * 2,
        out_shape=[jax.ShapeDtypeStruct((16, C), F32)] * 2,
        compiler_params=params(8),
        name="edge_rows",
    )(h, h, mom, mom, bed, bed, fric, fric, act, act, d, d)


def edge_columns_kernel(hl, hr, ml, mr, bl, br, fl, fr, al, ar, dl, dr, ll, lr, above, below, right, left, mat):
    slope = (
        (lambda s: hl[s, :], lambda s: hr[s, :]),
        (lambda s: ml[0, s, :], lambda s: mr[0, s, :]),
        (lambda s: ml[1, s, :], lambda s: mr[1, s, :]),
        (lambda s: bl[0, s, :], lambda s: br[0, s, :]),
        (lambda s: bl[1, s, :], lambda s: br[1, s, :]),
        (lambda s: fl[s, :], lambda s: fr[s, :]),
        (lambda s: al[s, :].astype(F32), lambda s: ar[s, :].astype(F32)),
    )
    lake = (
        (lambda s: dl[s, :], lambda s: dr[s, :]),
        (lambda s: ll[0, s, :], lambda s: lr[0, s, :]),
        (lambda s: ll[1, s, :], lambda s: lr[1, s, :]),
    )
    step = 64

    def put(acc, lane, first, last, i, wide):
        base, base_left = (2 * i, 64 + 2 * i) if wide == 2 else (16 + 3 * i, 80 + 3 * i)
        turned = pltpu.roll(last, (base + wide) % 128, 1)
        acc = jnp.where((lane >= base) & (lane < base + wide), turned, acc)
        turned = pltpu.roll(first, base_left, 1)
        return jnp.where((lane >= base_left) & (lane < base_left + wide), turned, acc)

    def both(t, _):
        s = pl.ds(pl.multiple_of(t * step, step), step)
        lane = lanes((step, 128))
        acc = jnp.zeros((step, 128), F32)
        for i, (first, last) in enumerate(slope):
            acc = put(acc, lane, first(s), last(s), i, 2)
        for i, (first, last) in enumerate(lake):
            acc = put(acc, lane, first(s), last(s), i, 3)
        mat[s, :] = acc
        return 0

    def lake_only(t, _):
        s = pl.ds(pl.multiple_of(t * step, step), step)
        lane = lanes((step, 128))
        acc = jnp.zeros((step, 128), F32)
        for i, (first, last) in enumerate(lake):
            acc = put(acc, lane, first(s), last(s), i, 3)
        mat[s, :] = acc
        return 0

    lax.fori_loop(0, R // step, both, 0)
    lax.fori_loop(R // step, L // step, lake_only, 0)
    lane, row = lanes((8, 128)), rows((8, 128))

    def corner(b_row, a_row, where):
        low = jnp.broadcast_to(below[b_row : b_row + 1, where], (8, 128))
        high = jnp.broadcast_to(above[a_row : a_row + 1, where], (8, 128))
        return jnp.where(row == 0, low, jnp.where(row == 7, high, 0.0))

    acc = mat[R : R + 8, :]
    for i in range(3):
        acc = put(acc, lane, corner(2 * i, 2 * i + 1, slice(0, 128)), corner(2 * i, 2 * i + 1, slice(C - 128, C)), i, 2)
    mat[R : R + 8, :] = acc
    acc = put(jnp.zeros((8, 128), F32), lane, corner(10, 11, slice(0, 128)), corner(10, 11, slice(C - 128, C)), 0, 3)
    mat[L : L + 8, :] = acc
    mat[L + 8 : L + 128, :] = jnp.zeros((120, 128), F32)
    for t in range(5):
        turned = mat[128 * t : 128 * t + 128, :].T
        right[:, 128 * t : 128 * t + 128] = turned[0:32, :]
        left[:, 128 * t : 128 * t + 128] = turned[64:96, :]


def edge_columns(h, mom, bed, fric, act, d, lm, above, below):
    last = C // 128 - 1
    two = lambda n, c: pl.BlockSpec((n, 128), lambda i: (0, c))
    three = lambda n, c: pl.BlockSpec((2, n, 128), lambda i: (0, 0, c))
    whole = pl.BlockSpec((16, C), lambda i: (0, 0))
    specs, args = [], []
    for spec, n, x in ((two, R, h), (three, R, mom), (three, R, bed), (two, R, fric), (two, R, act), (two, L, d), (three, L, lm)):
        specs += [spec(n, 0), spec(n, last)]
        args += [x, x]
    return pl.pallas_call(
        edge_columns_kernel,
        grid=(1,),
        in_specs=specs + [whole, whole],
        out_specs=[pl.BlockSpec((32, WIDE), lambda i: (0, 0))] * 2,
        out_shape=[jax.ShapeDtypeStruct((32, WIDE), F32)] * 2,
        scratch_shapes=[pltpu.VMEM((WIDE, 128), F32)],
        compiler_params=params(16),
        name="edge_columns",
    )(*args, above, below)


def split3(x):
    hi = x.astype(BF16)
    rest = x - hi.astype(F32)
    mid = rest.astype(BF16)
    return hi, mid, (rest - mid.astype(F32)).astype(BF16)


def slope_kernel(
    h_hbm, mom_hbm, bed_hbm, fric_hbm, act_hbm, above, below, from_left, from_right, own, off,
    out, payload,
    ext, act_ext, nxt, pa, qa, acc, turn, sems,
):
    srcs = (h_hbm, mom_hbm.at[0], mom_hbm.at[1], bed_hbm.at[0], bed_hbm.at[1], fric_hbm)
    tile = (pl.ds(TOP, R), pl.ds(0, C))
    copies = [pltpu.make_async_copy(s, ext.at[(i,) + tile], sems.at[i]) for i, s in enumerate(srcs)]
    copies.append(pltpu.make_async_copy(act_hbm, act_ext.at[tile], sems.at[6]))
    for c in copies:
        c.start()

    def arr(i):
        return ext.at[i] if i < 6 else act_ext

    for i in range(7):
        x = arr(i)
        x[0:TOP, :] = jnp.zeros((TOP, WIDE), x.dtype)
        x[TOP + R :, :] = jnp.zeros((2 * TOP, WIDE), x.dtype)
        if i < 3:
            x[TOP - 2 : TOP, 0:C] = above[2 * i : 2 * i + 2, :]
            x[TOP + R : TOP + R + 2, 0:C] = below[2 * i : 2 * i + 2, :]
        else:
            x[TOP - 1 : TOP, 0:C] = above[3 + i : 4 + i, :].astype(x.dtype)
            x[TOP + R : TOP + R + 1, 0:C] = below[3 + i : 4 + i, :].astype(x.dtype)
    for t in range(3):
        s = slice(128 * t, 128 * t + 128)
        both = jnp.concatenate(
            [from_left[:, s], jnp.zeros((32, 128), F32), from_right[:, s], jnp.zeros((32, 128), F32)], axis=0
        )
        turn[s, :] = both.T

    def halo(w, lane, i):
        left = pltpu.roll(w, 126 - 2 * i, 1)
        right = pltpu.roll(w, 64 - 2 * i, 1)
        return jnp.where(lane >= 126, left, jnp.where(lane < 2, right, 0.0))

    step = 64

    def columns(t, _):
        r = pl.multiple_of(t * step, step)
        w = turn[pl.ds(r, step), :]
        lane = lanes((step, 128))
        for i in range(7):
            x = arr(i)
            x[pl.ds(pl.multiple_of(TOP + r, 8), step), C:WIDE] = halo(w, lane, i).astype(x.dtype)
        return 0

    lax.fori_loop(0, R // step, columns, 0)
    w = turn[R : R + 8, :]
    row = rows((8, 128))
    for i in range(3):
        block = halo(w, lanes((8, 128)), i)
        ext[i, TOP - 8 : TOP, C:WIDE] = jnp.where(row == 7, block, 0.0)
        ext[i, TOP + R : TOP + R + 8, C:WIDE] = jnp.where(row == 0, block, 0.0)
    for c in copies:
        c.wait()

    k = 0.075
    chunk = 16

    def fluxes(src, begin, count):
        def body(t, _):
            s = pl.ds(pl.multiple_of(begin + t * chunk, 8), chunk)
            h, m, n = (src[i, s, :] for i in range(3))
            inv = 1.0 / jnp.maximum(h, 0.25)
            p = (0.5 * h) * h
            mi = m * inv
            cross = k * (mi * n)
            fm = k * (mi * m + p)
            gn = k * ((n * inv) * n + p)
            h4, m4, n4, mk, nk = 0.25 * h, 0.25 * m, 0.25 * n, k * m, k * n
            pa[0, s, :] = h4 - mk
            qa[0, s, :] = h4 + mk
            pa[1, s, :] = m4 - fm
            qa[1, s, :] = m4 + fm
            pa[2, s, :] = n4 - cross
            qa[2, s, :] = n4 + cross
            fr = ext[5, s, :]
            acc[0, s, :] = pltpu.roll(h4 - nk, WIDE - 1, 1) + pltpu.roll(h4 + nk, 1, 1)
            acc[1, s, :] = (
                pltpu.roll(m4 - cross, WIDE - 1, 1) + pltpu.roll(m4 + cross, 1, 1) + 0.15 * (h * ext[3, s, :] - fr * m)
            )
            acc[2, s, :] = (
                pltpu.roll(n4 - gn, WIDE - 1, 1) + pltpu.roll(n4 + gn, 1, 1) + 0.15 * (h * ext[4, s, :] - fr * n)
            )
            return 0

        lax.fori_loop(0, count, body, 0)

    def combine(begin, count, store, width):
        def body(t, _):
            r = pl.multiple_of(begin + t * chunk, 8)
            s = pl.ds(r, chunk)
            on = act_ext[s, 0:width].astype(F32)
            for i in range(3):
                store(
                    i,
                    t,
                    s,
                    on * (acc[i, s, 0:width] + next_row(pa, i, r, chunk, width) + previous_row(qa, i, r, chunk, width)),
                )
            return 0

        lax.fori_loop(0, count, body, 0)

    def to_next(i, t, s, value):
        nxt[i, s, :] = value

    def to_out(i, t, s, value):
        out[i, pl.ds(pl.multiple_of(t * chunk, 8), chunk), :] = value

    fluxes(ext, 0, SROWS // chunk)
    combine(8, (R + 16) // chunk, to_next, WIDE)
    fluxes(nxt, 8, (R + 16) // chunk)
    combine(TOP, R // chunk, to_out, C)

    owner = jnp.broadcast_to(own[...], (DEV, R))
    mine = rows((DEV, R)) == owner
    before = (rows((R, R)) < lanes((R, R))).astype(BF16)
    rank = jnp.dot(mine.astype(BF16), before, preferred_element_type=F32)
    picks = [mine & (rank == float(k_)) for k_ in range(CAP)]
    pickb = [p.astype(BF16) for p in picks]
    for i in range(3):
        parts = split3(out[i])
        for k_ in range(CAP):
            y = (
                jnp.dot(pickb[k_], parts[0], preferred_element_type=F32)
                + jnp.dot(pickb[k_], parts[1], preferred_element_type=F32)
                + jnp.dot(pickb[k_], parts[2], preferred_element_type=F32)
            )
            for j in range(4):
                payload[pl.ds(12 * k_ + 4 * i + j, DEV, stride=UNITS), :] = y[:, 128 * j : 128 * j + 128]

    lane, dest = lanes((DEV, 128)), rows((DEV, 128))
    tags = jnp.zeros((DEV, 128), F32)
    tag_value = jnp.broadcast_to((off[...] + 1).astype(F32), (DEV, R))
    edge_lane = lanes((R, 128))
    m_first, n_first = out[1, :, 0:128], out[2, :, 0:128]
    m_last, n_last = out[1, :, C - 128 : C], out[2, :, C - 128 : C]
    edges = jnp.where(edge_lane < 3, m_first, 0.0)
    edges = jnp.where((edge_lane >= 3) & (edge_lane < 6), pltpu.roll(n_first, 3, 1), edges)
    edges = jnp.where((edge_lane >= 8) & (edge_lane < 11), pltpu.roll(m_last, 11, 1), edges)
    edges = jnp.where((edge_lane >= 11) & (edge_lane < 14), pltpu.roll(n_last, 14, 1), edges)
    parts = split3(edges)
    to_right = jnp.zeros((DEV, 128), F32)
    to_left = jnp.zeros((DEV, 128), F32)
    for k_ in range(CAP):
        tag = jnp.sum(jnp.where(picks[k_], tag_value, 0.0), axis=1, keepdims=True)
        tags = jnp.where(lane == k_, tag, tags)
        g = (
            jnp.dot(pickb[k_], parts[0], preferred_element_type=F32)
            + jnp.dot(pickb[k_], parts[1], preferred_element_type=F32)
            + jnp.dot(pickb[k_], parts[2], preferred_element_type=F32)
        )
        at = 8 + 6 * k_
        to_right = jnp.where((lane >= at) & (lane < at + 6), pltpu.roll(g, at - 8, 1) if k_ else g, to_right)
        to_right = jnp.where(lane == 56 + k_, tag, to_right)
        at = 32 + 6 * k_
        to_left = jnp.where((lane >= at) & (lane < at + 6), pltpu.roll(g, at, 1), to_left)
        to_left = jnp.where(lane == 60 + k_, tag, to_left)
    column = lax.rem(dest, NY)
    to_right = jnp.where(column > 0, pltpu.roll(to_right, 1, 0), 0.0)
    to_left = jnp.where(column < NY - 1, pltpu.roll(to_left, DEV - 1, 0), 0.0)
    payload[pl.ds(TAG, DEV, stride=UNITS), :] = tags + to_right + to_left


def slope(h, mom, bed, fric, act, above, below, from_left, from_right, own, off):
    hbm = pl.BlockSpec(memory_space=pl.ANY)
    vmem = pl.BlockSpec(memory_space=pltpu.VMEM)
    return pl.pallas_call(
        slope_kernel,
        in_specs=[hbm] * 5 + [vmem] * 6,
        out_specs=[vmem, vmem],
        out_shape=[jax.ShapeDtypeStruct((3, R, C), F32), jax.ShapeDtypeStruct((DEV * UNITS, 128), F32)],
        scratch_shapes=[
            pltpu.VMEM((6, SROWS, WIDE), F32),
            pltpu.VMEM((SROWS, WIDE), jnp.int32),
            pltpu.VMEM((3, SROWS, WIDE), F32),
            pltpu.VMEM((3, SROWS, WIDE), F32),
            pltpu.VMEM((3, SROWS, WIDE), F32),
            pltpu.VMEM((3, SROWS, WIDE), F32),
            pltpu.VMEM((384, 128), F32),
            pltpu.SemaphoreType.DMA((7,)),
        ],
        compiler_params=params(40),
        name="slope",
    )(h, mom, bed, fric, act, above, below, from_left, from_right, own, off)


def prepare_kernel(d, lm, above, below, from_left, from_right, coef, momentum, turn):
    for t in range(5):
        s = slice(128 * t, 128 * t + 128)
        both = jnp.concatenate(
            [from_left[:, s], jnp.zeros((32, 128), F32), from_right[:, s], jnp.zeros((32, 128), F32)], axis=0
        )
        turn[s, :] = both.T
    third = 1.0 / 3.0

    def halo(w, lane, i):
        left = pltpu.roll(w, 109 - 3 * i, 1)
        right = pltpu.roll(w, 48 - 3 * i, 1)
        return jnp.where(lane >= 125, left, jnp.where(lane < 3, right, 0.0))

    step = 64

    def body(t, _):
        r = pl.multiple_of(t * step, step)
        s = pl.ds(r, step)
        w = turn[s, :]
        lane = lanes((step, 128))
        to = pl.ds(pl.multiple_of(TOP + r, 8), step)
        coef[to, 0:C] = (d[s, :] - 1.0) * third
        coef[to, C:WIDE] = (halo(w, lane, 0) - 1.0) * third
        for i in range(2):
            momentum[i, s, 0:C] = lm[i, s, :]
            momentum[i, s, C:WIDE] = halo(w, lane, i + 1)
        return 0

    lax.fori_loop(0, L // step, body, 0)
    coef[0:TOP, :] = jnp.zeros((TOP, WIDE), F32)
    coef[TOP + L :, :] = jnp.zeros((TOP, WIDE), F32)
    coef[TOP - 2 : TOP, 0:C] = (above[10:12, :] - 1.0) * third
    coef[TOP + L : TOP + L + 2, 0:C] = (below[10:12, :] - 1.0) * third
    block = (halo(turn[L : L + 8, :], lanes((8, 128)), 0) - 1.0) * third
    row = rows((8, 128))
    coef[TOP - 8 : TOP, C:WIDE] = jnp.where(row == 7, block, 0.0)
    coef[TOP + L : TOP + L + 8, C:WIDE] = jnp.where(row == 0, block, 0.0)


def prepare(d, lm, above, below, from_left, from_right):
    return pl.pallas_call(
        prepare_kernel,
        out_shape=[jax.ShapeDtypeStruct((LROWS, WIDE), F32), jax.ShapeDtypeStruct((2, L, WIDE), F32)],
        scratch_shapes=[pltpu.VMEM((WIDE, 128), F32)],
        compiler_params=params(24),
        cost_estimate=pl.CostEstimate(flops=4 * MIB, bytes_accessed=8 * MIB, transcendentals=0),
        name="prepare",
    )(d, lm, above, below, from_left, from_right)


def place_kernel(recv, momentum, height, b, first, last, new_height, hot, term):
    marks = recv[pl.ds(TAG, DEV, stride=UNITS), :]
    tags = marks.T
    here = (rows((L, DEV)) + 1).astype(F32)
    for group, at in enumerate((0, 56, 60)):
        for k in range(CAP):
            col = (group * CAP + k) * DEV
            hot[:, col : col + DEV] = (here == tags[at + k : at + k + 1, :]).astype(BF16)
    own = hot[:, 0 : CAP * DEV]
    for c in range(3):
        for k in range(CAP):
            for j in range(4):
                parts = split3(recv[pl.ds(12 * k + 4 * c + j, DEV, stride=UNITS), :])
                for t in range(3):
                    term[t, DEV * k : DEV * k + DEV, 128 * j : 128 * j + 128] = parts[t]
        flow = (
            jnp.dot(own, term[0], preferred_element_type=F32)
            + jnp.dot(own, term[1], preferred_element_type=F32)
            + jnp.dot(own, term[2], preferred_element_type=F32)
        )
        if c == 0:
            new_height[...] = height[...] + flow
        else:
            b[c - 1, :, 0:C] = momentum[c - 1, :, 0:C] + flow
    side = hot[:, CAP * DEV : 3 * CAP * DEV]
    lane = lanes((DEV, 128))
    for c in range(2):
        left, right = [], []
        for k in range(CAP):
            left.append(jnp.where(lane >= 125, pltpu.roll(marks, 117 - 6 * k - 3 * c, 1), 0.0))
            right.append(jnp.where(lane < 3, pltpu.roll(marks, 96 - 6 * k - 3 * c, 1), 0.0))
        parts = split3(jnp.concatenate(left + right, axis=0))
        b[c, :, C:WIDE] = (
            momentum[c, :, C:WIDE]
            + jnp.dot(side, parts[0], preferred_element_type=F32)
            + jnp.dot(side, parts[1], preferred_element_type=F32)
            + jnp.dot(side, parts[2], preferred_element_type=F32)
        )
    first[...] = b[:, 0:8, :]
    last[...] = b[:, L - 8 : L, :]


def place(recv, momentum, height):
    return pl.pallas_call(
        place_kernel,
        out_shape=[
            jax.ShapeDtypeStruct((2, L, WIDE), F32),
            jax.ShapeDtypeStruct((2, 8, WIDE), F32),
            jax.ShapeDtypeStruct((2, 8, WIDE), F32),
            jax.ShapeDtypeStruct((L, C), F32),
        ],
        scratch_shapes=[pltpu.VMEM((L, 3 * CAP * DEV), BF16), pltpu.VMEM((3, CAP * DEV, C), BF16)],
        compiler_params=params(40),
        name="place",
    )(recv, momentum, height)


def krylov_kernel(sides, b_in, above, below, coef, w1_out, w2_out, sums, b, w1, w2, sems):
    copies = [
        pltpu.make_async_copy(b_in.at[i], b.at[i, pl.ds(TOP, L), :], sems.at[i]) for i in range(2)
    ]
    for c in copies:
        c.start()
    for x in (b, w1, w2):
        for i in range(2):
            x[i, 0 : TOP - 8, :] = jnp.zeros((TOP - 8, WIDE), F32)
            x[i, TOP + L + 8 :, :] = jnp.zeros((TOP - 8, WIDE), F32)
    b[:, TOP - 8 : TOP, :] = above[...]
    b[:, TOP + L : TOP + L + 8, :] = below[...]
    up, down, left, right = (sides[i].astype(F32) for i in range(4))
    edge = jnp.where(lanes((1, 128)) < 64, right, left)
    for c in copies:
        c.wait()
    sixth = 1.0 / 6.0

    def image(x, i, r, n):
        s = pl.ds(r, n)
        v = x[i, s, :]
        around = (previous_row(x, i, r, n, WIDE) + next_row(x, i, r, n, WIDE)) + (
            pltpu.roll(v, 1, 1) + pltpu.roll(v, WIDE - 1, 1)
        )
        return v, coef[s, :] * v - sixth * around

    def store(x, i, s, w, scale=None):
        tail = w[:, C:WIDE] * edge
        if scale is not None:
            w, tail = w * scale, tail * scale
        x[i, s, 0:C] = w[:, 0:C]
        x[i, s, C:WIDE] = tail

    def dot(x, y):
        p = x[:, 0:C] * y[:, 0:C]
        p = (p[:, 0:128] + p[:, 128:256]) + (p[:, 256:384] + p[:, 384:512])
        return sum(p[8 * q : 8 * q + 8, :] for q in range(p.shape[0] // 8))

    chunk = 16
    zero = jnp.zeros((8, 128), F32)

    def sweep(src, dst, out, kinds):
        if dst is not None:
            for i in range(2):
                _, w = image(src, i, TOP - 8, 8)
                store(dst, i, slice(TOP - 8, TOP), w, up)
                _, w = image(src, i, TOP + L, 8)
                store(dst, i, slice(TOP + L, TOP + L + 8), w, down)

        def body(t, carry):
            r = pl.multiple_of(TOP + t * chunk, 8)
            carry = list(carry)
            for i in range(2):
                v, w = image(src, i, r, chunk)
                if dst is not None:
                    store(dst, i, pl.ds(r, chunk), w)
                    out[i, pl.ds(pl.multiple_of(t * chunk, 8), chunk), :] = w[:, 0:C]
                for q, kind in enumerate(kinds):
                    a, c = {"vv": (v, v), "vw": (v, w), "ww": (w, w)}[kind]
                    at = i * len(kinds) + q
                    carry[at] = carry[at] + dot(a, c)
            return tuple(carry)

        total = lax.fori_loop(0, L // chunk, body, (zero,) * (2 * len(kinds)))
        return total[: len(kinds)], total[len(kinds) :]

    s1 = sweep(b, w1, w1_out, ("vv", "vw", "ww"))
    s2 = sweep(w1, w2, w2_out, ("vw", "ww"))
    s3 = sweep(w2, None, None, ("vw",))
    flat = []
    for i in range(2):
        flat += list(s1[i]) + list(s2[i]) + list(s3[i]) + [zero, zero]
    stack = jnp.concatenate([jnp.sum(x, axis=0, keepdims=True) for x in flat], axis=0)
    total = jnp.sum(stack, axis=1, keepdims=True)
    line = jnp.sum(jnp.where(lanes((16, 128)) == rows((16, 128)), total, 0.0), axis=0, keepdims=True)
    sums[...] = jnp.broadcast_to(line, (DEV, 128))


def krylov(sides, b, above, below, coef):
    hbm = pl.BlockSpec(memory_space=pl.ANY)
    vmem = pl.BlockSpec(memory_space=pltpu.VMEM)
    return pl.pallas_call(
        krylov_kernel,
        in_specs=[pl.BlockSpec(memory_space=pltpu.SMEM), hbm, vmem, vmem, vmem],
        out_specs=[vmem] * 3,
        out_shape=[
            jax.ShapeDtypeStruct((2, L, C), F32),
            jax.ShapeDtypeStruct((2, L, C), F32),
            jax.ShapeDtypeStruct((DEV, 128), F32),
        ],
        scratch_shapes=[pltpu.VMEM((2, LROWS, WIDE), F32)] * 3 + [pltpu.SemaphoreType.DMA((2,))],
        compiler_params=params(40),
        name="krylov",
    )(sides, b, above, below, coef)


def steps(nu):
    def inner(u, v):
        return sum(u[i] * v[j] * nu[i + j] for i in range(len(u)) for j in range(len(v)))

    def times(u):
        lo = [4.0 * x for x in u] + [None]
        hi = [None] + [3.0 * x for x in u]
        return [a if b is None else b if a is None else a + b for a, b in zip(lo, hi)]

    def add(u, v, scale):
        u = list(u) + [None] * (len(v) - len(u))
        return [x + scale * y if x is not None and y is not None else scale * y if x is None else x
                for x, y in zip(u, list(v) + [None] * (len(u) - len(v)))]

    r = p = [jnp.ones_like(nu[0])]
    rr = nu[0]
    x = None
    for it in range(3):
        image = times(p)
        curve = inner(p, image)
        alpha = jnp.where(curve > 0.0, rr / curve, 0.25)
        alpha = jnp.minimum(jnp.maximum(alpha, 1.0 / 7.0), 1.0 / 1.2)
        x = [alpha * q for q in p] if x is None else add(x, p, alpha)
        if it == 2:
            return x
        r = add(r, image, -alpha)
        new = jnp.maximum(inner(r, r), 0.0)
        beta = jnp.minimum(jnp.where(rr > 0.0, new / rr, 0.0), 6.0)
        p = add(r, p, beta)
        rr = new


def finish_kernel(sums, b, w1, w2, x, coef):
    total = jnp.sum(sums[...], axis=0, keepdims=True)
    lane = lanes((1, 128))
    for c in range(2):
        nu = [
            jnp.sum(jnp.where(lane == 8 * c + k, total, 0.0), axis=1, keepdims=True) for k in range(6)
        ]
        e = steps(nu)
        for k in range(3):
            coef[3 * c + k : 3 * c + k + 1, :] = jnp.broadcast_to(e[k], (1, 128))
    step = 32

    for c in range(2):
        e = [jnp.broadcast_to(coef[3 * c + k : 3 * c + k + 1, 0:1], (step, C)) for k in range(3)]

        def body(t, _):
            s = pl.ds(pl.multiple_of(t * step, step), step)
            x[c, s, :] = e[0] * b[c, s, 0:C] + e[1] * w1[c, s, :] + e[2] * w2[c, s, :]
            return 0

        lax.fori_loop(0, L // step, body, 0)


def finish(sums, b, w1, w2):
    return pl.pallas_call(
        finish_kernel,
        out_shape=jax.ShapeDtypeStruct((2, L, C), F32),
        scratch_shapes=[pltpu.VMEM((8, 128), F32)],
        compiler_params=params(24),
        name="finish",
    )(sums, b, w1, w2)


def shift(x, axis, by):
    n = {"gx": NX, "gy": NY}[axis]
    return lax.ppermute(x, axis, [(i, i + by) for i in range(n) if 0 <= i + by < n])


def exchange(x):
    return lax.all_to_all(x, AXES, split_axis=0, concat_axis=0, tiled=True)


def per_device(h, mom, bed, fric, act, owners, offsets, height, lm, d):
    up, dn = edge_rows(h, mom, bed, fric, act, d)
    above, below = shift(dn, "gx", 1), shift(up, "gx", -1)
    to_right, to_left = edge_columns(h, mom, bed, fric, act, d, lm, above, below)
    from_left, from_right = shift(to_right, "gy", 1), shift(to_left, "gy", -1)
    own, off = owners.reshape(1, R), offsets.reshape(1, R)
    fields, payload = slope(h, mom, bed, fric, act, above, below, from_left, from_right, own, off)
    recv = exchange(payload.reshape(DEV, UNITS, 1, 128)).reshape(DEV * UNITS, 128)
    coef, momentum = prepare(d, lm, above, below, from_left, from_right)
    b, first, last, new_height = place(recv, momentum, height)
    b_above, b_below = shift(last, "gx", 1), shift(first, "gx", -1)
    i, j = lax.axis_index("gx"), lax.axis_index("gy")
    sides = jnp.stack([i > 0, i < NX - 1, j > 0, j < NY - 1]).astype(jnp.int32)
    w1, w2, sums = krylov(sides, b, b_above, b_below, coef)
    sums = exchange(sums.reshape(DEV, 1, 128)).reshape(DEV, 128)
    return fields, new_height, finish(sums, b, w1, w2)


def solution(mesh):
    return jax.shard_map(
        per_device,
        mesh=mesh,
        in_specs=(
            P("gx", "gy"),
            P(None, "gx", "gy"),
            P(None, "gx", "gy"),
            P("gx", "gy"),
            P("gx", "gy"),
            P("gx", "gy", None, None),
            P("gx", "gy", None),
            P("gx", "gy"),
            P(None, "gx", "gy"),
            P("gx", "gy"),
        ),
        out_specs=(P(None, "gx", "gy"), P("gx", "gy"), P(None, "gx", "gy")),
        check_vma=False,
    )
```

time: 704 us -> 142 us (0.20); the launches traced: 695 us -> 142 us
  blocking collectives: 326 us -> 14.6 us
  other arithmetic: 155 us -> 0.08 us
  local copies, waits for them, and re-layouts: 63.5 us -> 14.1 us
  starting transfers between devices: 78.6 us -> 29.2 us
  Pallas kernels: 0 us -> 35.5 us
  waiting for transfers between devices: 69.8 us -> 47.5 us
    psum x5 -> x0, blocking collectives: 326 us -> none  [the longest x3 193 us: squares(): return lax.psum(jnp.sum(residual * residual, axis=(1, 2)), ('gx', 'gy'))]
    scatter-add x1 -> x0, other arithmetic: 65.1 us -> none  [per_device(): jnp.zeros((lake_rows + 1, 3, columns), jnp.float32).at[landing]]
    reduce_sum x6 -> x0, other arithmetic: 56.9 us -> none  [the longest x3 46.8 us: per_device(): jnp.sum(direction * applied, axis=(1, 2))]
    ppermute x20 -> x6, starting transfers between devices: 53.8 us -> 16.1 us  [shift(): lax.ppermute(x, axis, [(i, i + by) for i in range(n) if 0 <= i + by < n])]
    pallas_call x0 -> x7, Pallas kernels: none -> 35.5 us  [the longest x1 13 us: krylov(): pl.pallas_call(krylov_kernel, in_specs=[pl.BlockSpec(memory_space=pltpu.S...]
    scatter x2 -> x0, local copies, waits for them, and re-layouts: 27.9 us -> none  [the longest x1 26.5 us: per_device(): jnp.zeros((devices * capacity, 3, columns), jnp.float32).at[slot_index]]
    ppermute x20 -> x6, waiting for transfers between devices: 29.8 us -> 10.5 us  [shift(): lax.ppermute(x, axis, [(i, i + by) for i in range(n) if 0 <= i + by < n])]
    all_to_all x0 -> x1, blocking collectives: none -> 14.6 us  [exchange(): return lax.all_to_all(x, AXES, split_axis=0, concat_axis=0, tiled=True)]
  transfers between devices with their start and end apart: 22 -> 7, of which waited for: 10 -> 5; matrix products, arithmetic and copies ran while one was open for 8% -> 0% of each run, Pallas kernels for 0% -> 1%
where the time goes in v1:
time: 142 us
  waiting for transfers between devices  47.5 us (33%)
  Pallas kernels  35.5 us (25%)
  starting transfers between devices  29.2 us (21%)
  blocking collectives  14.6 us (10%)
  local copies, waits for them, and re-layouts  14.1 us (10%)
    all_to_all x1, waiting for transfers between devices, exchange(): return lax.all_to_all(x, AXES, split_axis=0, concat_axis=0, tiled=True)  37 us
    ppermute x6, starting transfers between devices, shift(): lax.ppermute(x, axis, [(i, i + by) for i in range(n) if 0 <= i + by < n])  16.1 us
    all_to_all x1, blocking collectives, exchange(): return lax.all_to_all(x, AXES, split_axis=0, concat_axis=0, tiled=True)  14.6 us
    unnamed x42, local copies, waits for them, and re-layouts  14.1 us
    all_to_all x1, starting transfers between devices, exchange(): return lax.all_to_all(x, AXES, split_axis=0, concat_axis=0, tiled=True)  13.1 us
    pallas_call x1, Pallas kernels, krylov(): pl.pallas_call(krylov_kernel, in_specs=[pl.BlockSpec(memory_space=pltpu.S...  13 us
    ppermute x6, waiting for transfers between devices, shift(): lax.ppermute(x, axis, [(i, i + by) for i in range(n) if 0 <= i + by < n])  10.5 us
    pallas_call x1, Pallas kernels, slope(): pl.pallas_call(slope_kernel, in_specs=[hbm] * 5 + [vmem] * 6, out_specs=[...  9.66 us
  transfers between devices with their start and end apart: 7, of which 5 were waited for; matrix products, arithmetic and copies ran while one was open for 0% of the time, Pallas kernels for 1%

profile of v1, /device:TPU:1, one launch (start us, length us, event | category | flops | bytes accessed | tf_op | source)
XLA Modules:
  0.0 141.8 jit_solution(6345868226194495245)
XLA Ops:
  0.6 0.0 copy-start
  0.6 1.2 copy-done
  1.9 1.2 copy-done.2
  3.1 1.2 copy-done.4
  4.3 1.0 copy-done.7
  5.4 1.0 copy-done.9
  6.4 1.0 copy-done.11
  7.4 0.0 copy-start.8
  7.5 0.0 copy-start.10
  7.5 0.0 copy-start.12
  7.5 4.8 %collective-permute-start = (f32[16,512]{1,0:T(8,128)S(1)}, f32[16,512]{1,0:T(8,128)S(1)}, u32[]{:S(2)}, u32[]{:S(2)}) collective-permute-start(f32[16,512]{1,0:T(8,128)S(1)} %get-tuple-element.18), channel_id=1, source_target_pairs={{0,16},{16,32},{32,48},{48,64},{64,80},{80,96},{96,112},{1,17},{17... | collective-permute-start | bytes 98312 | tf_op jit(solution)/shard_map/ppermute | solution.py:634
  12.4 0.0 copy-start.19
  12.4 0.0 copy-start.20
  12.4 1.9 %collective-permute-start.1 = (f32[16,512]{1,0:T(8,128)S(1)}, f32[16,512]{1,0:T(8,128)S(1)}, u32[]{:S(2)}, u32[]{:S(2)}) collective-permute-start(f32[16,512]{1,0:T(8,128)S(1)} %get-tuple-element.19), channel_id=1, source_target_pairs={{16,0},{32,16},{48,32},{64,48},{80,64},{96,80},{112,96},{17,1},{33... | collective-permute-start | bytes 98312 | tf_op jit(solution)/shard_map/ppermute | solution.py:634
  14.3 0.0 collective-permute-done.above
  14.3 3.3 %collective-permute-done.1.below = f32[16,512]{1,0:T(8,128)S(1)} collective-permute-done((f32[16,512]{1,0:T(8,128)S(1)}, f32[16,512]{1,0:T(8,128)S(1)}, u32[]{:S(2)}, u32[]{:S(2)}) %collective-permute-start.1) | collective-permute-done | bytes 32800 | tf_op jit(solution)/shard_map/ppermute | solution.py:634
  17.6 0.0 copy-done.1
  17.6 0.0 copy-done.3
  17.6 0.0 copy-done.5
  17.6 0.0 copy-done.6
  17.6 0.0 copy-done.8
  17.7 0.0 copy-done.10
  17.7 0.0 copy-done.12
  17.7 1.9 %edge_columns.1 = (f32[32,640]{1,0:T(8,128)S(1)}, f32[32,640]{1,0:T(8,128)S(1)}) custom-call(f32[256,512]{1,0:T(8,128)S(1)} %copy-done.8, f32[256,512]{1,0:T(8,128)S(1)} %copy-done.8, f32[2,256,512]{2,1,0:T(8,128)S(1)} %copy-done.1, f32[2,256,512]{2,1,0:T(8,128)S(1)} %copy-done.1, f32[2,256,512]{2,1,0:T(8,128)S(1)} %copy-done.3, ...), custom_call_target="tpu_custom_call" | custom-call | tf_op jit(solution)/shard_map/edge_columns/pallas_call | solution.py:154
  19.5 3.1 %collective-permute-start.2 = (f32[32,640]{1,0:T(8,128)S(1)}, f32[32,640]{1,0:T(8,128)S(1)}, u32[]{:S(2)}, u32[]{:S(2)}) collective-permute-start(f32[32,640]{1,0:T(8,128)S(1)} %get-tuple-element.20), channel_id=1, source_target_pairs={{0,1},{1,2},{2,3},{3,4},{4,5},{5,6},{6,7},{7,8},{8,9},{9,10},{10,1... | collective-permute-start | bytes 245768 | tf_op jit(solution)/shard_map/ppermute | solution.py:634
  22.7 1.3 collective-permute-start.3
  24.0 0.2 collective-permute-done.2.from_left
  24.1 3.7 %collective-permute-done.3.from_right = f32[32,640]{1,0:T(8,128)S(1)} collective-permute-done((f32[32,640]{1,0:T(8,128)S(1)}, f32[32,640]{1,0:T(8,128)S(1)}, u32[]{:S(2)}, u32[]{:S(2)}) %collective-permute-start.3) | collective-permute-done | bytes 81952 | tf_op jit(solution)/shard_map/ppermute | solution.py:634
  27.9 0.0 copy-done.19
  27.9 9.7 %slope.1 = (f32[3,256,512]{2,1,0:T(8,128)}, f32[6272,128]{1,0:T(8,128)S(1)}) custom-call(f32[256,512]{1,0:T(8,128)S(1)} %copy-done.8, f32[2,256,512]{2,1,0:T(8,128)S(1)} %copy-done.1, f32[2,256,512]{2,1,0:T(8,128)S(1)} %copy-done.3, f32[256,512]{1,0:T(8,128)S(1)} %copy-done.10, s32[256,512]{1,0:T(8,128)S(1)} %copy-done.12, ...), custom_call_target="tpu_custom_call" | custom-call | tf_op jit(solution)/shard_map/slope/pallas_call | solution.py:343
  37.5 1.7 %copy-done.13 = f32[6272,128]{1,0:T(8,128)} copy-done((f32[6272,128]{1,0:T(8,128)}, f32[6272,128]{1,0:T(8,128)S(1)}, u32[]{:S(2)}) %copy-start.13) | copy-done | bytes 3211288
  39.2 13.1 %all-to-all-start = ((f32[128,49,1,128]{3,2,1,0:T(1,128)}), f32[128,49,1,128]{3,2,1,0:T(1,128)}, u32[]{:S(2)}, u32[]{:S(2)}) async-start(f32[128,49,1,128]{3,2,1,0:T(1,128)} %bitcast.12), calls=%async_computation | async-start | bytes 6422528 | tf_op jit(solution)/shard_map/all_to_all | solution.py:638
  52.3 1.2 prepare.1
  53.6 1.6 %copy-done.14 = f32[2,512,640]{2,1,0:T(8,128)} copy-done((f32[2,512,640]{2,1,0:T(8,128)}, f32[2,512,640]{2,1,0:T(8,128)S(1)}, u32[]{:S(2)}) %copy-start.14) | copy-done | bytes 2621464
  55.1 1.1 copy-done.16
  56.2 37.0 %all-to-all-done = f32[128,49,1,128]{3,2,1,0:T(1,128)} async-done(((f32[128,49,1,128]{3,2,1,0:T(1,128)}), f32[128,49,1,128]{3,2,1,0:T(1,128)}, u32[]{:S(2)}, u32[]{:S(2)}) %all-to-all-start) | async-done | bytes 3211296 | tf_op jit(solution)/shard_map/all_to_all | solution.py:638
  93.2 1.7 %copy-done.15 = f32[2,512,640]{2,1,0:T(8,128)S(1)} copy-done((f32[2,512,640]{2,1,0:T(8,128)S(1)}, f32[2,512,640]{2,1,0:T(8,128)}, u32[]{:S(2)}) %copy-start.15) | copy-done | bytes 2621464
  95.0 1.2 copy-done.18
  96.2 7.6 %place.1 = (f32[2,512,640]{2,1,0:T(8,128)S(1)}, f32[2,8,640]{2,1,0:T(8,128)S(1)}, f32[2,8,640]{2,1,0:T(8,128)S(1)}, f32[512,512]{1,0:T(8,128)}) custom-call(f32[6272,128]{1,0:T(8,128)} %bitcast.3.recv, f32[2,512,640]{2,1,0:T(8,128)S(1)} %copy-done.15, f32[512,512]{1,0:T(8,128)S(1)} %copy-done.18), custom_call_target="tpu_custom_call" | custom-call | tf_op jit(solution)/shard_map/place/pallas_call | solution.py:457
  103.9 3.0 %collective-permute-start.4 = (f32[2,8,640]{2,1,0:T(8,128)S(1)}, f32[2,8,640]{2,1,0:T(8,128)S(1)}, u32[]{:S(2)}, u32[]{:S(2)}) collective-permute-start(f32[2,8,640]{2,1,0:T(8,128)S(1)} %get-tuple-element.27), channel_id=1, source_target_pairs={{0,16},{16,32},{32,48},{48,64},{64,80},{80,96},{96,112},{1,17},{17... | collective-permute-start | bytes 122888 | tf_op jit(solution)/shard_map/ppermute | solution.py:634
  106.8 1.9 %collective-permute-start.5 = (f32[2,8,640]{2,1,0:T(8,128)S(1)}, f32[2,8,640]{2,1,0:T(8,128)S(1)}, u32[]{:S(2)}, u32[]{:S(2)}) collective-permute-start(f32[2,8,640]{2,1,0:T(8,128)S(1)} %get-tuple-element.28), channel_id=1, source_target_pairs={{16,0},{32,16},{48,32},{64,48},{80,64},{96,80},{112,96},{17,1},{33... | collective-permute-start | bytes 122888 | tf_op jit(solution)/shard_map/ppermute | solution.py:634
  108.8 0.1 add_convert_fusion.sides
  108.9 0.0 collective-permute-done.4.above
  108.9 3.3 %collective-permute-done.5.below = f32[2,8,640]{2,1,0:T(8,128)S(1)} collective-permute-done((f32[2,8,640]{2,1,0:T(8,128)S(1)}, f32[2,8,640]{2,1,0:T(8,128)S(1)}, u32[]{:S(2)}, u32[]{:S(2)}) %collective-permute-start.5) | collective-permute-done | bytes 40992 | tf_op jit(solution)/shard_map/ppermute | solution.py:634
  112.2 0.0 copy-done.17
  112.2 13.0 %krylov.1 = (f32[2,512,512]{2,1,0:T(8,128)S(1)}, f32[2,512,512]{2,1,0:T(8,128)S(1)}, f32[128,128]{1,0:T(8,128)S(1)}) custom-call(s32[4]{0:T(128)S(1)} %add_convert_fusion.sides, f32[2,512,640]{2,1,0:T(8,128)S(1)} %get-tuple-element.26.b_in.b, f32[2,8,640]{2,1,0:T(8,128)S(1)} %collective-permute-done.4.above, f32[2,8,640]{2,1,0:T(8,128)S(1)} %collective-permute-done.5.below, ...), custom_call_target="tpu_custom_call" | custom-call | tf_op jit(solution)/shard_map/krylov/pallas_call | solution.py:552
  125.1 14.6 %all_to_all.10 = f32[128,1,128]{2,1,0:T(1,128)S(1)} all-to-all(f32[128,1,128]{2,1,0:T(1,128)S(1)} %bitcast.14), channel_id=1, replica_groups=mesh['gx'=8,'gy'=16] {'gx','gy'}, dimensions={0} | all-to-all | bytes 131072 | tf_op jit(solution)/shard_map/all_to_all | solution.py:638
  139.7 2.1 %finish.1 = f32[2,512,512]{2,1,0:T(8,128)} custom-call(f32[128,128]{1,0:T(8,128)S(1)} %bitcast.13, f32[2,512,640]{2,1,0:T(8,128)S(1)} %get-tuple-element.26.b_in.b, f32[2,512,512]{2,1,0:T(8,128)S(1)} %get-tuple-element.31.w1, f32[2,512,512]{2,1,0:T(8,128)S(1)} %get-tuple-element.32.w2), custom_call_target="tpu_custom_call" | custom-call | tf_op jit(solution)/shard_map/finish/pallas_call | solution.py:623
  (17 shorter events, 0.1 us)
Async XLA Ops:
  0.6 1.2 copy-start
  1.9 1.2 copy-start.2
  3.1 1.2 copy-start.4
  4.3 1.0 copy-start.7
  5.4 1.0 copy-start.9
  6.4 1.0 copy-start.11
  7.4 10.2 %copy-start.1 = (f32[2,256,512]{2,1,0:T(8,128)S(1)}, f32[2,256,512]{2,1,0:T(8,128)}, u32[]{:S(2)}) copy-start(f32[2,256,512]{2,1,0:T(8,128)} %mom_hbm.1) | copy-start | bytes 3145732
  7.4 10.2 %copy-start.3 = (f32[2,256,512]{2,1,0:T(8,128)S(1)}, f32[2,256,512]{2,1,0:T(8,128)}, u32[]{:S(2)}) copy-start(f32[2,256,512]{2,1,0:T(8,128)} %bed_hbm.1) | copy-start | bytes 3145732
  7.4 10.2 %copy-start.5 = (f32[512,512]{1,0:T(8,128)S(1)}, f32[512,512]{1,0:T(8,128)}, u32[]{:S(2)}) copy-start(f32[512,512]{1,0:T(8,128)} %d.1) | copy-start | bytes 3145732
  7.4 10.2 %copy-start.6 = (f32[2,512,512]{2,1,0:T(8,128)S(1)}, f32[2,512,512]{2,1,0:T(8,128)}, u32[]{:S(2)}) copy-start(f32[2,512,512]{2,1,0:T(8,128)} %lm.1) | copy-start | bytes 6291460
  7.4 10.2 %copy-start.8 = (f32[256,512]{1,0:T(8,128)S(1)}, f32[256,512]{1,0:T(8,128)}, u32[]{:S(2)}) copy-start(f32[256,512]{1,0:T(8,128)} %h_hbm.1) | copy-start | bytes 1572868
  7.5 10.2 %copy-start.10 = (f32[256,512]{1,0:T(8,128)S(1)}, f32[256,512]{1,0:T(8,128)}, u32[]{:S(2)}) copy-start(f32[256,512]{1,0:T(8,128)} %fric_hbm.1) | copy-start | bytes 1572868
  7.5 10.2 %copy-start.12 = (s32[256,512]{1,0:T(8,128)S(1)}, s32[256,512]{1,0:T(8,128)}, u32[]{:S(2)}) copy-start(s32[256,512]{1,0:T(8,128)} %act_hbm.1) | copy-start | bytes 1572868
  7.5 6.8 %collective-permute-start = (f32[16,512]{1,0:T(8,128)S(1)}, f32[16,512]{1,0:T(8,128)S(1)}, u32[]{:S(2)}, u32[]{:S(2)}) collective-permute-start(f32[16,512]{1,0:T(8,128)S(1)} %get-tuple-element.18), channel_id=1, source_target_pairs={{0,16},{16,32},{32,48},{48,64},{64,80},{80,96},{96,112},{1,17},{17... | collective-permute-start | bytes 98312 | tf_op jit(solution)/shard_map/ppermute | solution.py:634
  12.4 15.5 %copy-start.19 = (s32[1,1,256,1]{2,3,1,0:T(1,128)S(1)}, s32[1,1,256,1]{2,3,1,0:T(1,128)}, u32[]{:S(2)}) copy-start(s32[1,1,256,1]{2,3,1,0:T(1,128)} %param.15) | copy-start | bytes 3076
  12.4 15.5 %copy-start.20 = (s32[1,1,256]{2,1,0:T(1,128)S(1)}, s32[1,1,256]{2,1,0:T(1,128)}, u32[]{:S(2)}) copy-start(s32[1,1,256]{2,1,0:T(1,128)} %param.16) | copy-start | bytes 3076
  12.4 5.2 %collective-permute-start.1 = (f32[16,512]{1,0:T(8,128)S(1)}, f32[16,512]{1,0:T(8,128)S(1)}, u32[]{:S(2)}, u32[]{:S(2)}) collective-permute-start(f32[16,512]{1,0:T(8,128)S(1)} %get-tuple-element.19), channel_id=1, source_target_pairs={{16,0},{32,16},{48,32},{64,48},{80,64},{96,80},{112,96},{17,1},{33... | collective-permute-start | bytes 98312 | tf_op jit(solution)/shard_map/ppermute | solution.py:634
  19.5 4.6 %collective-permute-start.2 = (f32[32,640]{1,0:T(8,128)S(1)}, f32[32,640]{1,0:T(8,128)S(1)}, u32[]{:S(2)}, u32[]{:S(2)}) collective-permute-start(f32[32,640]{1,0:T(8,128)S(1)} %get-tuple-element.20), channel_id=1, source_target_pairs={{0,1},{1,2},{2,3},{3,4},{4,5},{5,6},{6,7},{7,8},{8,9},{9,10},{10,1... | collective-permute-start | bytes 245768 | tf_op jit(solution)/shard_map/ppermute | solution.py:634
  22.7 5.2 %collective-permute-start.3 = (f32[32,640]{1,0:T(8,128)S(1)}, f32[32,640]{1,0:T(8,128)S(1)}, u32[]{:S(2)}, u32[]{:S(2)}) collective-permute-start(f32[32,640]{1,0:T(8,128)S(1)} %get-tuple-element.21), channel_id=1, source_target_pairs={{1,0},{2,1},{3,2},{4,3},{5,4},{6,5},{7,6},{8,7},{9,8},{10,9},{11,1... | collective-permute-start | bytes 245768 | tf_op jit(solution)/shard_map/ppermute | solution.py:634
  37.5 1.7 %copy-start.13 = (f32[6272,128]{1,0:T(8,128)}, f32[6272,128]{1,0:T(8,128)S(1)}, u32[]{:S(2)}) copy-start(f32[6272,128]{1,0:T(8,128)S(1)} %get-tuple-element.23) | copy-start | bytes 9633796
  39.2 54.0 %all-to-all-start = ((f32[128,49,1,128]{3,2,1,0:T(1,128)}), f32[128,49,1,128]{3,2,1,0:T(1,128)}, u32[]{:S(2)}, u32[]{:S(2)}) async-start(f32[128,49,1,128]{3,2,1,0:T(1,128)} %bitcast.12), calls=%async_computation | async-start | bytes 6422528 | tf_op jit(solution)/shard_map/all_to_all | solution.py:638
  53.6 1.6 %copy-start.14 = (f32[2,512,640]{2,1,0:T(8,128)}, f32[2,512,640]{2,1,0:T(8,128)S(1)}, u32[]{:S(2)}) copy-start(f32[2,512,640]{2,1,0:T(8,128)S(1)} %get-tuple-element.24.momentum) | copy-start | bytes 7864324
  55.1 1.1 copy-start.16
  93.2 1.7 %copy-start.15 = (f32[2,512,640]{2,1,0:T(8,128)S(1)}, f32[2,512,640]{2,1,0:T(8,128)}, u32[]{:S(2)}) copy-start(f32[2,512,640]{2,1,0:T(8,128)} %copy-done.14) | copy-start | bytes 7864324
  95.0 1.2 copy-start.18
  96.2 15.9 %copy-start.17 = (f32[544,640]{1,0:T(8,128)S(1)}, f32[544,640]{1,0:T(8,128)}, u32[]{:S(2)}) copy-start(f32[544,640]{1,0:T(8,128)} %copy-done.16) | copy-start | bytes 4177924
  103.9 5.0 %collective-permute-start.4 = (f32[2,8,640]{2,1,0:T(8,128)S(1)}, f32[2,8,640]{2,1,0:T(8,128)S(1)}, u32[]{:S(2)}, u32[]{:S(2)}) collective-permute-start(f32[2,8,640]{2,1,0:T(8,128)S(1)} %get-tuple-element.27), channel_id=1, source_target_pairs={{0,16},{16,32},{32,48},{48,64},{64,80},{80,96},{96,112},{1,17},{17... | collective-permute-start | bytes 122888 | tf_op jit(solution)/shard_map/ppermute | solution.py:634
  106.8 5.3 %collective-permute-start.5 = (f32[2,8,640]{2,1,0:T(8,128)S(1)}, f32[2,8,640]{2,1,0:T(8,128)S(1)}, u32[]{:S(2)}, u32[]{:S(2)}) collective-permute-start(f32[2,8,640]{2,1,0:T(8,128)S(1)} %get-tuple-element.28), channel_id=1, source_target_pairs={{16,0},{32,16},{48,32},{64,48},{80,64},{96,80},{112,96},{17,1},{33... | collective-permute-start | bytes 122888 | tf_op jit(solution)/shard_map/ppermute | solution.py:634

commit v2 on v1

v2 whole, which is shorter than its diff:
```python
import functools

import jax
import jax.numpy as jnp
from jax import lax
from jax.experimental import pallas as pl
from jax.experimental.pallas import tpu as pltpu
from jax.sharding import PartitionSpec as P

F32 = jnp.float32
BF16 = jnp.bfloat16
AXES = ("gx", "gy")
NX, NY = 8, 16
DEV = NX * NY
R, C, L = 256, 512, 512
CAP = 4
UNITS = 12 * CAP + 1
TAG = 12 * CAP
WIDE = C + 128
TOP = 16
SROWS = R + 2 * TOP
CHUNK = 32
LTOP = 16
LROWS = L + 2 * LTOP
LCHUNK = 64
LSUB = 16
MIB = 1 << 20


HBM = pl.BlockSpec(memory_space=pltpu.HBM)
VMEM = pl.BlockSpec(memory_space=pltpu.VMEM)


def params(limit=None):
    return pltpu.CompilerParams(vmem_limit_bytes=limit * MIB if limit else 60 * 1024 * 1024)


def lanes(shape):
    return lax.broadcasted_iota(jnp.int32, shape, len(shape) - 1)


def rows(shape):
    return lax.broadcasted_iota(jnp.int32, shape, len(shape) - 2)


def edge_rows_kernel(h, m, b, f, a, d, up, dn, hs, ms, bs, fs, as_, ds, sems):
    copies = []
    for q, (src, dst) in enumerate(((h, hs), (f, fs), (a, as_), (d, ds))):
        for side, r in enumerate((0, src.shape[0] - 8)):
            copies.append(pltpu.make_async_copy(src.at[pl.ds(r, 8), :], dst.at[side], sems.at[2 * q + side]))
    for q, (src, dst) in enumerate(((m, ms), (b, bs))):
        for side, r in enumerate((0, R - 8)):
            copies.append(pltpu.make_async_copy(src.at[:, pl.ds(r, 8), :], dst.at[side], sems.at[8 + 2 * q + side]))
    for c in copies:
        c.start()
    for c in copies:
        c.wait()
    for side, out, two, one in ((0, up, slice(0, 2), slice(0, 1)), (1, dn, slice(6, 8), slice(7, 8))):
        out[0:2, :] = hs[side, two, :]
        out[2:4, :] = ms[side, 0, two, :]
        out[4:6, :] = ms[side, 1, two, :]
        out[6:7, :] = bs[side, 0, one, :]
        out[7:8, :] = bs[side, 1, one, :]
        out[8:9, :] = fs[side, one, :]
        out[9:10, :] = as_[side, one, :].astype(F32)
        out[10:12, :] = ds[side, two, :]
        out[12:16, :] = jnp.zeros((4, C), F32)


def edge_rows(h, mom, bed, fric, act, d):
    return pl.pallas_call(
        edge_rows_kernel,
        in_specs=[HBM] * 6,
        out_specs=[VMEM] * 2,
        out_shape=[jax.ShapeDtypeStruct((16, C), F32)] * 2,
        scratch_shapes=[
            pltpu.VMEM((2, 8, C), F32),
            pltpu.VMEM((2, 2, 8, C), F32),
            pltpu.VMEM((2, 2, 8, C), F32),
            pltpu.VMEM((2, 8, C), F32),
            pltpu.VMEM((2, 8, C), jnp.int32),
            pltpu.VMEM((2, 8, C), F32),
            pltpu.SemaphoreType.DMA((12,)),
        ],
        compiler_params=params(),
        name="edge_rows",
    )(h, mom, bed, fric, act, d)


def edge_columns_kernel(h, m, b, f, a, d, l, above, below, right, left, mat):
    sides = (slice(0, 128), slice(C - 128, C))

    def pair(read):
        return tuple(functools.partial(read, lane) for lane in sides)

    slope = (
        pair(lambda lane, s: h[s, lane]),
        pair(lambda lane, s: m[0, s, lane]),
        pair(lambda lane, s: m[1, s, lane]),
        pair(lambda lane, s: b[0, s, lane]),
        pair(lambda lane, s: b[1, s, lane]),
        pair(lambda lane, s: f[s, lane]),
        pair(lambda lane, s: a[s, lane].astype(F32)),
    )
    lake = (
        pair(lambda lane, s: d[s, lane]),
        pair(lambda lane, s: l[0, s, lane]),
        pair(lambda lane, s: l[1, s, lane]),
    )
    step = 64

    def put(acc, lane, first, last, i, wide):
        base, base_left = (2 * i, 64 + 2 * i) if wide == 2 else (16 + 3 * i, 80 + 3 * i)
        turned = pltpu.roll(last, (base + wide) % 128, 1)
        acc = jnp.where((lane >= base) & (lane < base + wide), turned, acc)
        turned = pltpu.roll(first, base_left, 1)
        return jnp.where((lane >= base_left) & (lane < base_left + wide), turned, acc)

    def both(t, _):
        s = pl.ds(pl.multiple_of(t * step, step), step)
        lane = lanes((step, 128))
        acc = jnp.zeros((step, 128), F32)
        for i, (first, last) in enumerate(slope):
            acc = put(acc, lane, first(s), last(s), i, 2)
        for i, (first, last) in enumerate(lake):
            acc = put(acc, lane, first(s), last(s), i, 3)
        mat[s, :] = acc
        return 0

    def lake_only(t, _):
        s = pl.ds(pl.multiple_of(t * step, step), step)
        lane = lanes((step, 128))
        acc = jnp.zeros((step, 128), F32)
        for i, (first, last) in enumerate(lake):
            acc = put(acc, lane, first(s), last(s), i, 3)
        mat[s, :] = acc
        return 0

    lax.fori_loop(0, R // step, both, 0)
    lax.fori_loop(R // step, L // step, lake_only, 0)
    lane, row = lanes((8, 128)), rows((8, 128))

    def corner(b_row, a_row, where):
        low = jnp.broadcast_to(below[b_row : b_row + 1, where], (8, 128))
        high = jnp.broadcast_to(above[a_row : a_row + 1, where], (8, 128))
        return jnp.where(row == 0, low, jnp.where(row == 7, high, 0.0))

    acc = mat[R : R + 8, :]
    for i in range(3):
        acc = put(acc, lane, corner(2 * i, 2 * i + 1, slice(0, 128)), corner(2 * i, 2 * i + 1, slice(C - 128, C)), i, 2)
    mat[R : R + 8, :] = acc
    acc = put(jnp.zeros((8, 128), F32), lane, corner(10, 11, slice(0, 128)), corner(10, 11, slice(C - 128, C)), 0, 3)
    mat[L : L + 8, :] = acc
    mat[L + 8 : L + 128, :] = jnp.zeros((120, 128), F32)
    for t in range(5):
        turned = mat[128 * t : 128 * t + 128, :].T
        right[:, 128 * t : 128 * t + 128] = turned[0:32, :]
        left[:, 128 * t : 128 * t + 128] = turned[64:96, :]


def edge_columns(h, mom, bed, fric, act, d, lm, above, below):
    return pl.pallas_call(
        edge_columns_kernel,
        in_specs=[VMEM] * 9,
        out_specs=[VMEM] * 2,
        out_shape=[jax.ShapeDtypeStruct((32, WIDE), F32)] * 2,
        scratch_shapes=[pltpu.VMEM((WIDE, 128), F32)],
        compiler_params=params(16),
        name="edge_columns",
    )(h, mom, bed, fric, act, d, lm, above, below)


def split2(x):
    hi = x.astype(BF16)
    return hi, (x - hi.astype(F32)).astype(BF16)


def pick(hot, parts):
    return jnp.dot(hot, parts[0], preferred_element_type=F32) + jnp.dot(hot, parts[1], preferred_element_type=F32)


def beside(xs):
    lane = lanes(xs[0].shape)
    r = [pltpu.roll(x, 1, 1) for x in xs]
    left = [jnp.where(lane == 0, r[j - 1], r[j]) for j in range(5)]
    r = [pltpu.roll(x, 127, 1) for x in xs]
    right = [jnp.where(lane == 127, r[(j + 1) % 5], r[j]) for j in range(5)]
    return left, right


def slope_kernel(
    h_in, mom, bed, fric, act, above, below, from_left, from_right, own, off,
    out, payload,
    ends, side, pa, qa, acc, turn,
):
    tile = (
        lambda s, lane: h_in[s, lane],
        lambda s, lane: mom[0, s, lane],
        lambda s, lane: mom[1, s, lane],
        lambda s, lane: bed[0, s, lane],
        lambda s, lane: bed[1, s, lane],
        lambda s, lane: fric[s, lane],
        lambda s, lane: act[s, lane].astype(F32),
    )
    ends[...] = jnp.zeros(ends.shape, F32)
    for i in range(7):
        for j in range(4):
            s = slice(128 * j, 128 * j + 128)
            if i < 3:
                ends[0, i, j, 6:8, :] = above[2 * i : 2 * i + 2, s]
                ends[1, i, j, 0:2, :] = below[2 * i : 2 * i + 2, s]
            else:
                ends[0, i, j, 7:8, :] = above[3 + i : 4 + i, s]
                ends[1, i, j, 0:1, :] = below[3 + i : 4 + i, s]
    for t in range(3):
        s = slice(128 * t, 128 * t + 128)
        both = jnp.concatenate(
            [from_left[:, s], jnp.zeros((32, 128), F32), from_right[:, s], jnp.zeros((32, 128), F32)], axis=0
        )
        turn[s, :] = both.T

    def halo(w, lane, i):
        left = pltpu.roll(w, 126 - 2 * i, 1)
        right = pltpu.roll(w, 64 - 2 * i, 1)
        return jnp.where(lane >= 126, left, jnp.where(lane < 2, right, 0.0))

    step = 64

    def columns(t, _):
        r = pl.multiple_of(t * step, step)
        w = turn[pl.ds(r, step), :]
        lane = lanes((step, 128))
        for i in range(7):
            side[i, pl.ds(r, step), :] = halo(w, lane, i)
        return 0

    lax.fori_loop(0, R // step, columns, 0)
    w = turn[R : R + 8, :]
    row = rows((8, 128))
    for i in range(3):
        block = halo(w, lanes((8, 128)), i)
        ends[0, i, 4, :, :] = jnp.where(row == 7, block, 0.0)
        ends[1, i, 4, :, :] = jnp.where(row == 0, block, 0.0)

    k, q = 0.075, 0.25 / 0.075

    def fluxes(u, s, get, h, m, n):
        pairs = [[], [], []]
        for j in range(5):
            inv = 1.0 / jnp.maximum(h[j], 0.25)
            p = (0.5 * h[j]) * h[j]
            mi = m[j] * inv
            cross = mi * n[j]
            fm = mi * m[j] + p
            gn = (n[j] * inv) * n[j] + p
            h4, m4, n4 = q * h[j], q * m[j], q * n[j]
            pa[u, 0, j, s, :] = h4 - m[j]
            qa[u, 0, j, s, :] = h4 + m[j]
            pa[u, 1, j, s, :] = m4 - fm
            qa[u, 1, j, s, :] = m4 + fm
            pa[u, 2, j, s, :] = n4 - cross
            qa[u, 2, j, s, :] = n4 + cross
            fr = get(5, j)
            pairs[0].append((h4 - n[j], h4 + n[j], None))
            pairs[1].append((m4 - cross, m4 + cross, 2.0 * (h[j] * get(3, j) - fr * m[j])))
            pairs[2].append((n4 - gn, n4 + gn, 2.0 * (h[j] * get(4, j) - fr * n[j])))
        for i in range(3):
            _, right = beside([x[0] for x in pairs[i]])
            left, _ = beside([x[1] for x in pairs[i]])
            for j in range(5):
                x = left[j] + right[j]
                acc[u, i, j, s, :] = x if i == 0 else x + pairs[i][j][2]

    def combine(u, i, j, r, n, on):
        return (k * on) * (
            acc[u, i, j, pl.ds(r, n), :] + pa[u, i, j, pl.ds(r + 1, n), :] + qa[u, i, j, pl.ds(r - 1, n), :]
        )

    def reader(s):
        def get(i, j):
            return side[i, s, :] if j == 4 else tile[i](s, slice(128 * j, 128 * j + 128))

        return get

    def end_reader(e):
        return lambda i, j: ends[e, i, j, :, :]

    def section(u, to, n, get):
        if u == 0:
            new = [[get(i, j) for j in range(5)] for i in range(3)]
        else:
            new = [[combine(0, i, j, to, n, get(6, j)) for j in range(5)] for i in range(3)]
        fluxes(u, pl.ds(to, n), get, *new)

    def body(u):
        def run(t, _):
            r = pl.multiple_of(t * CHUNK, CHUNK)
            section(u, pl.multiple_of(TOP + r, 8), CHUNK, reader(pl.ds(r, CHUNK)))
            return 0

        return run

    def last(t, _):
        r = pl.multiple_of(t * CHUNK, CHUNK)
        to = pl.ds(r, CHUNK)
        for j in range(4):
            s = slice(128 * j, 128 * j + 128)
            on = tile[6](to, s)
            for i in range(3):
                out[i, to, s] = combine(1, i, j, pl.multiple_of(TOP + r, 8), CHUNK, on)
        return 0

    pa[0, :, :, TOP + R + 8 :, :] = jnp.zeros((3, 5, 8, 128), F32)
    qa[0, :, :, 0:8, :] = jnp.zeros((3, 5, 8, 128), F32)
    for u in range(2):
        section(u, TOP - 8, 8, end_reader(0))
        section(u, TOP + R, 8, end_reader(1))
        lax.fori_loop(0, R // CHUNK, body(u), 0)
    lax.fori_loop(0, R // CHUNK, last, 0)

    owner = jnp.broadcast_to(own[...], (DEV, R))
    mine = rows((DEV, R)) == owner
    before = (rows((R, R)) < lanes((R, R))).astype(BF16)
    rank = jnp.dot(mine.astype(BF16), before, preferred_element_type=F32)
    picks = [mine & (rank == float(k_)) for k_ in range(CAP)]
    pickb = [p.astype(BF16) for p in picks]
    for i in range(3):
        parts = split2(out[i])
        for k_ in range(CAP):
            y = pick(pickb[k_], parts)
            for j in range(4):
                payload[pl.ds(12 * k_ + 4 * i + j, DEV, stride=UNITS), :] = y[:, 128 * j : 128 * j + 128]

    lane, dest = lanes((DEV, 128)), rows((DEV, 128))
    tags = jnp.zeros((DEV, 128), F32)
    tag_value = jnp.broadcast_to((off[...] + 1).astype(F32), (DEV, R))
    edge_lane = lanes((R, 128))
    m_first, n_first = out[1, :, 0:128], out[2, :, 0:128]
    m_last, n_last = out[1, :, C - 128 : C], out[2, :, C - 128 : C]
    edges = jnp.where(edge_lane < 3, m_first, 0.0)
    edges = jnp.where((edge_lane >= 3) & (edge_lane < 6), pltpu.roll(n_first, 3, 1), edges)
    edges = jnp.where((edge_lane >= 8) & (edge_lane < 11), pltpu.roll(m_last, 11, 1), edges)
    edges = jnp.where((edge_lane >= 11) & (edge_lane < 14), pltpu.roll(n_last, 14, 1), edges)
    parts = split2(edges)
    to_right = jnp.zeros((DEV, 128), F32)
    to_left = jnp.zeros((DEV, 128), F32)
    for k_ in range(CAP):
        tag = jnp.sum(jnp.where(picks[k_], tag_value, 0.0), axis=1, keepdims=True)
        tags = jnp.where(lane == k_, tag, tags)
        g = pick(pickb[k_], parts)
        at = 8 + 6 * k_
        to_right = jnp.where((lane >= at) & (lane < at + 6), pltpu.roll(g, at - 8, 1) if k_ else g, to_right)
        to_right = jnp.where(lane == 56 + k_, tag, to_right)
        at = 32 + 6 * k_
        to_left = jnp.where((lane >= at) & (lane < at + 6), pltpu.roll(g, at, 1), to_left)
        to_left = jnp.where(lane == 60 + k_, tag, to_left)
    column = lax.rem(dest, NY)
    to_right = jnp.where(column > 0, pltpu.roll(to_right, 1, 0), 0.0)
    to_left = jnp.where(column < NY - 1, pltpu.roll(to_left, DEV - 1, 0), 0.0)
    payload[pl.ds(TAG, DEV, stride=UNITS), :] = tags + to_right + to_left


def slope(h, mom, bed, fric, act, above, below, from_left, from_right, own, off):
    return pl.pallas_call(
        slope_kernel,
        in_specs=[VMEM] * 11,
        out_specs=[VMEM] * 2,
        out_shape=[jax.ShapeDtypeStruct((3, R, C), F32), jax.ShapeDtypeStruct((DEV * UNITS, 128), F32)],
        scratch_shapes=[
            pltpu.VMEM((2, 7, 5, 8, 128), F32),
            pltpu.VMEM((7, R, 128), F32),
            pltpu.VMEM((2, 3, 5, SROWS, 128), F32),
            pltpu.VMEM((2, 3, 5, SROWS, 128), F32),
            pltpu.VMEM((2, 3, 5, SROWS, 128), F32),
            pltpu.VMEM((384, 128), F32),
        ],
        compiler_params=params(34),
        name="slope",
    )(h, mom, bed, fric, act, above, below, from_left, from_right, own, off)


def prepare_kernel(d, lm, above, below, from_left, from_right, coef, momentum, first, last, turn):
    for t in range(5):
        s = slice(128 * t, 128 * t + 128)
        both = jnp.concatenate(
            [from_left[:, s], jnp.zeros((32, 128), F32), from_right[:, s], jnp.zeros((32, 128), F32)], axis=0
        )
        turn[s, :] = both.T

    def halo(w, lane, i):
        left = pltpu.roll(w, 109 - 3 * i, 1)
        right = pltpu.roll(w, 48 - 3 * i, 1)
        return jnp.where(lane >= 125, left, jnp.where(lane < 3, right, 0.0))

    step = 64

    def body(t, _):
        r = pl.multiple_of(t * step, step)
        s = pl.ds(r, step)
        w = turn[s, :]
        lane = lanes((step, 128))
        to = pl.ds(pl.multiple_of(LTOP + r, 8), step)
        for j in range(4):
            coef[j, to, :] = 2.0 * d[s, 128 * j : 128 * j + 128] - 2.0
        coef[4, to, :] = 2.0 * halo(w, lane, 0) - 2.0
        for i in range(2):
            for j in range(4):
                momentum[i, j, s, :] = lm[i, s, 128 * j : 128 * j + 128]
            momentum[i, 4, s, :] = halo(w, lane, i + 1)
        return 0

    lax.fori_loop(0, L // step, body, 0)
    for j in range(5):
        coef[j, 0:LTOP, :] = jnp.zeros((LTOP, 128), F32)
        coef[j, LTOP + L :, :] = jnp.zeros((LTOP, 128), F32)
        if j < 4:
            s = slice(128 * j, 128 * j + 128)
            coef[j, LTOP - 2 : LTOP, :] = 2.0 * above[10:12, s] - 2.0
            coef[j, LTOP + L : LTOP + L + 2, :] = 2.0 * below[10:12, s] - 2.0
    block = 2.0 * halo(turn[L : L + 8, :], lanes((8, 128)), 0) - 2.0
    row = rows((8, 128))
    coef[4, LTOP - 8 : LTOP, :] = jnp.where(row == 7, block, 0.0)
    coef[4, LTOP + L : LTOP + L + 8, :] = jnp.where(row == 0, block, 0.0)
    first[...] = momentum[:, :, 0:8, :]
    last[...] = momentum[:, :, L - 8 : L, :]


def prepare(d, lm, above, below, from_left, from_right):
    return pl.pallas_call(
        prepare_kernel,
        out_shape=[jax.ShapeDtypeStruct(x, F32) for x in ((5, LROWS, 128), (2, 5, L, 128), (2, 5, 8, 128), (2, 5, 8, 128))],
        scratch_shapes=[pltpu.VMEM((WIDE, 128), F32)],
        compiler_params=params(16),
        cost_estimate=pl.CostEstimate(flops=4 * MIB, bytes_accessed=8 * MIB, transcendentals=0),
        name="prepare",
    )(d, lm, above, below, from_left, from_right)


def one_hot(hot, tags, first):
    here = (rows((L, DEV)) + 1).astype(F32)
    for group, at in enumerate(first):
        for k in range(CAP):
            col = (group * CAP + k) * DEV
            hot[:, col : col + DEV] = (here == tags[at + k : at + k + 1, :]).astype(BF16)


def gather(recv, term, c):
    for k in range(CAP):
        for j in range(4):
            parts = split2(recv[pl.ds(12 * k + 4 * c + j, DEV, stride=UNITS), :])
            for t in range(2):
                term[t, DEV * k : DEV * k + DEV, 128 * j : 128 * j + 128] = parts[t]


def place_kernel(recv, first_momentum, last_momentum, flow, first, last, hot, term):
    marks = recv[pl.ds(TAG, DEV, stride=UNITS), :]
    one_hot(hot, marks.T, (0, 56, 60))
    own = hot[:, 0 : CAP * DEV]
    side = hot[:, CAP * DEV : 3 * CAP * DEV]
    lane = lanes((DEV, 128))
    for c in range(2):
        gather(recv, term, c + 1)
        sums = pick(own, (term[0], term[1]))
        for j in range(4):
            flow[c, j, :, :] = sums[:, 128 * j : 128 * j + 128]
        left, right = [], []
        for k in range(CAP):
            left.append(jnp.where(lane >= 125, pltpu.roll(marks, 117 - 6 * k - 3 * c, 1), 0.0))
            right.append(jnp.where(lane < 3, pltpu.roll(marks, 96 - 6 * k - 3 * c, 1), 0.0))
        flow[c, 4, :, :] = pick(side, split2(jnp.concatenate(left + right, axis=0)))
    first[...] = first_momentum[...] + flow[:, :, 0:8, :]
    last[...] = last_momentum[...] + flow[:, :, L - 8 : L, :]


def place(recv, first_momentum, last_momentum):
    return pl.pallas_call(
        place_kernel,
        out_shape=[jax.ShapeDtypeStruct((2, 5, n, 128), F32) for n in (L, 8, 8)],
        scratch_shapes=[pltpu.VMEM((L, 3 * CAP * DEV), BF16), pltpu.VMEM((2, CAP * DEV, C), BF16)],
        compiler_params=params(20),
        name="place",
    )(recv, first_momentum, last_momentum)


def raise_kernel(recv, height, new_height, hot, term):
    one_hot(hot, recv[pl.ds(TAG, DEV, stride=UNITS), :].T, (0,))
    gather(recv, term, 0)
    new_height[...] = height[...] + pick(hot[...], (term[0], term[1]))


def raise_lake(recv, height):
    return pl.pallas_call(
        raise_kernel,
        in_specs=[VMEM] * 2,
        out_specs=VMEM,
        out_shape=jax.ShapeDtypeStruct((L, C), F32),
        scratch_shapes=[pltpu.VMEM((L, CAP * DEV), BF16), pltpu.VMEM((2, CAP * DEV, C), BF16)],
        compiler_params=params(8),
        cost_estimate=pl.CostEstimate(flops=600 * MIB, bytes_accessed=6 * MIB, transcendentals=0),
        name="raise_lake",
    )(recv, height)


def krylov_kernel(sides, flow, momentum, above, below, coef, b, w1, w2, sums):
    for x in (b, w1, w2):
        x[:, :, 0 : LTOP - 8, :] = jnp.zeros((2, 5, LTOP - 8, 128), F32)
        x[:, :, LTOP + L + 8 :, :] = jnp.zeros((2, 5, LTOP - 8, 128), F32)
    b[:, :, LTOP - 8 : LTOP, :] = above[...]
    b[:, :, LTOP + L : LTOP + L + 8, :] = below[...]
    up, down, left, right = (sides[i].astype(F32) for i in range(4))
    edge = jnp.where(lanes((1, 128)) < 64, right, left)

    def total_side(t, _):
        r = pl.multiple_of(t * 64, 64)
        for i in range(2):
            for j in range(5):
                b[i, j, pl.ds(pl.multiple_of(LTOP + r, 8), 64), :] = (
                    flow[i, j, pl.ds(r, 64), :] + momentum[i, j, pl.ds(r, 64), :]
                )
        return 0

    lax.fori_loop(0, L // 64, total_side, 0)

    def image(x, i, r, n):
        v = [x[i, j, pl.ds(r, n), :] for j in range(5)]
        west, east = beside(v)
        w = []
        for j in range(5):
            around = (x[i, j, pl.ds(r - 1, n), :] + x[i, j, pl.ds(r + 1, n), :]) + (west[j] + east[j])
            w.append(coef[j, pl.ds(r, n), :] * v[j] - around)
        w[4] = w[4] * edge
        return v, w

    def dot(x, y):
        p = (x[0] * y[0] + x[1] * y[1]) + (x[2] * y[2] + x[3] * y[3])
        p = [p[8 * q : 8 * q + 8, :] for q in range(p.shape[0] // 8)]
        while len(p) > 1:
            p = [a + c for a, c in zip(p[::2], p[1::2])]
        return p[0]

    zero = jnp.zeros((8, 128), F32)

    def sweep(src, dst, kinds):
        for i in range(2):
            for r, scale in ((LTOP - 8, up), (LTOP + L, down)):
                _, w = image(src, i, r, 8)
                for j in range(5):
                    dst[i, j, r : r + 8, :] = w[j] * scale

        def body(t, carry):
            r = pl.multiple_of(LTOP + t * LCHUNK, 8)
            carry = list(carry)
            for q0 in range(0, LCHUNK, LSUB):
                rq = pl.multiple_of(r + q0, 8)
                for i in range(2):
                    v, w = image(src, i, rq, LSUB)
                    for j in range(5):
                        dst[i, j, pl.ds(rq, LSUB), :] = w[j]
                    for q, kind in enumerate(kinds):
                        x, y = {"vv": (v, v), "vw": (v, w), "ww": (w, w)}[kind]
                        at = i * len(kinds) + q
                        carry[at] = carry[at] + dot(x, y)
            return tuple(carry)

        total = lax.fori_loop(0, L // LCHUNK, body, (zero,) * (2 * len(kinds)))
        return total[: len(kinds)], total[len(kinds) :]

    def last_sum(x):
        lane = lanes((LSUB, 128))

        def body(t, carry):
            r = pl.multiple_of(LTOP + t * LCHUNK, 8)
            carry = list(carry)
            for q0 in range(0, LCHUNK, LSUB):
                rq = pl.multiple_of(r + q0, 8)
                for i in range(2):
                    v = [x[i, j, pl.ds(rq, LSUB), :] for j in range(5)]
                    turned = [pltpu.roll(y, 127, 1) for y in v]
                    w = []
                    for j in range(4):
                        pair = jnp.where(lane == 127, turned[j + 1], turned[j]) + x[i, j, pl.ds(rq + 1, LSUB), :]
                        w.append(coef[j, pl.ds(rq, LSUB), :] * v[j] - 2.0 * pair)
                    carry[i] = carry[i] + dot(v, w)
            return tuple(carry)

        total = lax.fori_loop(0, L // LCHUNK, body, (zero,) * 2)
        return total[:1], total[1:]

    s1 = sweep(b, w1, ("vv", "vw", "ww"))
    s2 = sweep(w1, w2, ("vw", "ww"))
    s3 = last_sum(w2)
    flat = []
    for i in range(2):
        flat += list(s1[i]) + list(s2[i]) + list(s3[i]) + [zero, zero]
    stack = jnp.concatenate([jnp.sum(x, axis=0, keepdims=True) for x in flat], axis=0)
    total = jnp.sum(stack, axis=1, keepdims=True)
    line = jnp.sum(jnp.where(lanes((16, 128)) == rows((16, 128)), total, 0.0), axis=0, keepdims=True)
    sums[...] = jnp.broadcast_to(line, (DEV, 128))


def krylov(sides, flow, momentum, above, below, coef):
    return pl.pallas_call(
        krylov_kernel,
        in_specs=[pl.BlockSpec(memory_space=pltpu.SMEM)] + [VMEM] * 5,
        out_specs=[VMEM] * 4,
        out_shape=[jax.ShapeDtypeStruct((2, 5, LROWS, 128), F32)] * 3 + [jax.ShapeDtypeStruct((DEV, 128), F32)],
        compiler_params=params(24),
        name="krylov",
    )(sides, flow, momentum, above, below, coef)


def steps(nu):
    def inner(u, v):
        return sum(u[i] * v[j] * nu[i + j] for i in range(len(u)) for j in range(len(v)))

    def times(u):
        lo = [4.0 * x for x in u] + [None]
        hi = [None] + [0.5 * x for x in u]
        return [a if b is None else b if a is None else a + b for a, b in zip(lo, hi)]

    def add(u, v, scale):
        u = list(u) + [None] * (len(v) - len(u))
        return [x + scale * y if x is not None and y is not None else scale * y if x is None else x
                for x, y in zip(u, list(v) + [None] * (len(u) - len(v)))]

    r = p = [jnp.ones_like(nu[0])]
    rr = nu[0]
    x = None
    for it in range(3):
        image = times(p)
        curve = inner(p, image)
        alpha = jnp.where(curve > 0.0, rr / curve, 0.25)
        alpha = jnp.minimum(jnp.maximum(alpha, 1.0 / 7.0), 1.0 / 1.2)
        x = [alpha * q for q in p] if x is None else add(x, p, alpha)
        if it == 2:
            return x
        r = add(r, image, -alpha)
        new = jnp.maximum(inner(r, r), 0.0)
        beta = jnp.minimum(jnp.where(rr > 0.0, new / rr, 0.0), 6.0)
        p = add(r, p, beta)
        rr = new


def finish_kernel(sums, b, w1, w2, x_hbm, coef, x, sems):
    total = jnp.sum(sums[...], axis=0, keepdims=True)
    lane = lanes((1, 128))
    for c in range(2):
        nu = [
            jnp.sum(jnp.where(lane == 8 * c + k, total, 0.0), axis=1, keepdims=True) for k in range(6)
        ]
        e = steps(nu)
        for k in range(3):
            coef[3 * c + k : 3 * c + k + 1, :] = jnp.broadcast_to(e[k], (1, 128))
    step = 64
    copies = []
    for c in range(2):
        e = [jnp.broadcast_to(coef[3 * c + k : 3 * c + k + 1, :], (step, 128)) for k in range(3)]

        def body(t, _):
            s = pl.ds(pl.multiple_of(t * step, step), step)
            at = pl.ds(pl.multiple_of(LTOP + t * step, 8), step)
            for j in range(4):
                x[c, s, 128 * j : 128 * j + 128] = e[0] * b[c, j, at, :] + e[1] * w1[c, j, at, :] + e[2] * w2[c, j, at, :]
            return 0

        for half in range(2):
            lax.fori_loop(half * L // step // 2, (half + 1) * L // step // 2, body, 0)
            s = pl.ds(half * L // 2, L // 2)
            copies.append(pltpu.make_async_copy(x.at[c, s, :], x_hbm.at[c, s, :], sems.at[2 * c + half]))
            copies[-1].start()
    for copy in copies:
        copy.wait()


def finish(sums, b, w1, w2):
    return pl.pallas_call(
        finish_kernel,
        in_specs=[VMEM] * 4,
        out_specs=HBM,
        out_shape=jax.ShapeDtypeStruct((2, L, C), F32),
        scratch_shapes=[pltpu.VMEM((8, 128), F32), pltpu.VMEM((2, L, C), F32), pltpu.SemaphoreType.DMA((4,))],
        compiler_params=params(16),
        name="finish",
    )(sums, b, w1, w2)


def shift(x, axis, by):
    n = {"gx": NX, "gy": NY}[axis]
    return lax.ppermute(x, axis, [(i, i + by) for i in range(n) if 0 <= i + by < n])


def exchange(x):
    return lax.all_to_all(x, AXES, split_axis=0, concat_axis=0, tiled=True)


def per_device(h, mom, bed, fric, act, owners, offsets, height, lm, d):
    up, dn = edge_rows(h, mom, bed, fric, act, d)
    above, below = shift(dn, "gx", 1), shift(up, "gx", -1)
    to_right, to_left = edge_columns(h, mom, bed, fric, act, d, lm, above, below)
    from_left, from_right = shift(to_right, "gy", 1), shift(to_left, "gy", -1)
    own, off = owners.reshape(1, R), offsets.reshape(1, R)
    fields, payload = slope(h, mom, bed, fric, act, above, below, from_left, from_right, own, off)
    recv = exchange(payload.reshape(DEV, UNITS, 1, 128)).reshape(DEV * UNITS, 128)
    coef, momentum, first, last = prepare(d, lm, above, below, from_left, from_right)
    flow, first, last = place(recv, first, last)
    new_height = raise_lake(recv, height)
    b_above, b_below = shift(last, "gx", 1), shift(first, "gx", -1)
    i, j = lax.axis_index("gx"), lax.axis_index("gy")
    sides = jnp.stack([i > 0, i < NX - 1, j > 0, j < NY - 1]).astype(jnp.int32)
    flow, new_height = lax.optimization_barrier((flow, new_height))
    b, w1, w2, sums = krylov(sides, flow, momentum, b_above, b_below, coef)
    sums = exchange(sums.reshape(DEV, 1, 128)).reshape(DEV, 128)
    return fields, new_height, finish(sums, b, w1, w2)


def solution(mesh):
    return jax.shard_map(
        per_device,
        mesh=mesh,
        in_specs=(
            P("gx", "gy"),
            P(None, "gx", "gy"),
            P(None, "gx", "gy"),
            P("gx", "gy"),
            P("gx", "gy"),
            P("gx", "gy", None, None),
            P("gx", "gy", None),
            P("gx", "gy"),
            P(None, "gx", "gy"),
            P("gx", "gy"),
        ),
        out_specs=(P(None, "gx", "gy"), P("gx", "gy"), P(None, "gx", "gy")),
        check_vma=False,
    )
```

time: 142 us -> 124 us (0.87)
  Pallas kernels: 35.5 us -> 24.6 us
  waiting for transfers between devices: 47.5 us -> 43.3 us
  local copies, waits for them, and re-layouts: 14.1 us -> 10.8 us
    pallas_call x1, Pallas kernels: 13 us -> 6.71 us  [krylov(): pl.pallas_call(krylov_kernel, in_specs=[pl.BlockSpec(memory_space=pltpu.S...]
    pallas_call x6 -> x7, Pallas kernels: 22.5 us -> 17.9 us  [the longest x1 6.84 us: slope(): pl.pallas_call(slope_kernel, in_specs=[VMEM] * 11, out_specs=[VMEM] * 2,...]
    unnamed x42 -> x38, local copies, waits for them, and re-layouts: 14.1 us -> 10.8 us
    all_to_all x1, waiting for transfers between devices: 37 us -> 34.4 us  [exchange(): return lax.all_to_all(x, AXES, split_axis=0, concat_axis=0, tiled=True)]
    ppermute x6, waiting for transfers between devices: 10.5 us -> 8.93 us  [shift(): lax.ppermute(x, axis, [(i, i + by) for i in range(n) if 0 <= i + by < n])]
  transfers between devices with their start and end apart: 7 -> 7, of which waited for: 5 -> 5; matrix products, arithmetic and copies ran while one was open for 0% -> 0% of each run, Pallas kernels for 1% -> 3%
where the time goes in v2:
time: 124 us; the launch traced here: 123 us
  waiting for transfers between devices  43.3 us (35%)
  starting transfers between devices  29 us (23%)
  Pallas kernels  24.6 us (20%)
  blocking collectives  14.6 us (12%)
  local copies, waits for them, and re-layouts  10.8 us (9%)
    all_to_all x1, waiting for transfers between devices, exchange(): return lax.all_to_all(x, AXES, split_axis=0, concat_axis=0, tiled=True)  34.4 us
    ppermute x6, starting transfers between devices, shift(): lax.ppermute(x, axis, [(i, i + by) for i in range(n) if 0 <= i + by < n])  16.1 us
    all_to_all x1, blocking collectives, exchange(): return lax.all_to_all(x, AXES, split_axis=0, concat_axis=0, tiled=True)  14.6 us
    all_to_all x1, starting transfers between devices, exchange(): return lax.all_to_all(x, AXES, split_axis=0, concat_axis=0, tiled=True)  12.9 us
    unnamed x38, local copies, waits for them, and re-layouts  10.8 us
    ppermute x6, waiting for transfers between devices, shift(): lax.ppermute(x, axis, [(i, i + by) for i in range(n) if 0 <= i + by < n])  8.93 us
    pallas_call x1, Pallas kernels, slope(): pl.pallas_call(slope_kernel, in_specs=[VMEM] * 11, out_specs=[VMEM] * 2,...  6.84 us
    pallas_call x1, Pallas kernels, krylov(): pl.pallas_call(krylov_kernel, in_specs=[pl.BlockSpec(memory_space=pltpu.S...  6.71 us
  transfers between devices with their start and end apart: 7, of which 5 were waited for; matrix products, arithmetic and copies ran while one was open for 0% of the time, Pallas kernels for 3%

profile of v2, /device:TPU:1, one launch (start us, length us, event | category | flops | bytes accessed | tf_op | source)
XLA Modules:
  0.0 123.2 jit_solution(15241403146569628262)
XLA Ops:
  0.6 0.0 copy-start.2
  0.6 0.0 copy-start.1
  0.7 0.0 copy-start
  0.7 0.0 copy-start.6
  0.7 1.8 %edge_rows.1 = (f32[16,512]{1,0:T(8,128)}, f32[16,512]{1,0:T(8,128)}) custom-call(f32[256,512]{1,0:T(8,128)} %h_in.1, f32[2,256,512]{2,1,0:T(8,128)} %mom.1, f32[2,256,512]{2,1,0:T(8,128)} %bed.1, f32[256,512]{1,0:T(8,128)} %fric.1, s32[256,512]{1,0:T(8,128)} %act.1, f32[512,512]{1,0:T(8,128)} %d.5), custom_call_target="tpu_custom_call" | custom-call | tf_op jit(solution)/shard_map/edge_rows/pallas_call | solution.py:71
  2.5 4.6 %collective-permute-start = (f32[16,512]{1,0:T(8,128)}, f32[16,512]{1,0:T(8,128)S(1)}, u32[]{:S(2)}, u32[]{:S(2)}) collective-permute-start(f32[16,512]{1,0:T(8,128)} %get-tuple-element.22), channel_id=1, source_target_pairs={{0,16},{16,32},{32,48},{48,64},{64,80},{80,96},{96,112},{1,17},{17... | collective-permute-start | bytes 98312 | tf_op jit(solution)/shard_map/ppermute | solution.py:689
  7.1 0.0 copy-start.17
  7.1 1.9 %collective-permute-start.1 = (f32[16,512]{1,0:T(8,128)}, f32[16,512]{1,0:T(8,128)S(1)}, u32[]{:S(2)}, u32[]{:S(2)}) collective-permute-start(f32[16,512]{1,0:T(8,128)} %get-tuple-element.23), channel_id=1, source_target_pairs={{16,0},{32,16},{48,32},{64,48},{80,64},{96,80},{112,96},{17,1},{33... | collective-permute-start | bytes 98312 | tf_op jit(solution)/shard_map/ppermute | solution.py:689
  9.0 0.0 collective-permute-done.above
  9.0 3.5 %collective-permute-done.1.below = f32[16,512]{1,0:T(8,128)S(1)} collective-permute-done((f32[16,512]{1,0:T(8,128)}, f32[16,512]{1,0:T(8,128)S(1)}, u32[]{:S(2)}, u32[]{:S(2)}) %collective-permute-start.1) | collective-permute-done | bytes 32800 | tf_op jit(solution)/shard_map/ppermute | solution.py:689
  12.5 0.0 copy-done.2
  12.5 0.0 copy-done.1
  12.5 0.0 copy-done
  12.5 0.0 copy-done.6
  12.5 0.0 copy-start.4
  12.6 1.6 %copy-done.4 = f32[2,512,512]{2,1,0:T(8,128)S(1)} copy-done((f32[2,512,512]{2,1,0:T(8,128)S(1)}, f32[2,512,512]{2,1,0:T(8,128)}, u32[]{:S(2)}) %copy-start.4) | copy-done | bytes 2097176
  14.1 1.0 copy-done.7
  15.2 1.0 copy-done.9
  16.2 1.6 %edge_columns.1 = (f32[32,640]{1,0:T(8,128)S(1)}, f32[32,640]{1,0:T(8,128)S(1)}) custom-call(f32[256,512]{1,0:T(8,128)S(1)} %copy-done.6, f32[2,256,512]{2,1,0:T(8,128)S(1)} %copy-done, f32[2,256,512]{2,1,0:T(8,128)S(1)} %copy-done.1, f32[256,512]{1,0:T(8,128)S(1)} %copy-done.7, s32[256,512]{1,0:T(8,128)S(1)} %copy-done.9, f32[512,512]{1,0:T(8,128)S(1)} %copy-done.2, ...), custom_call_target="tpu_custom_call" | custom-call | tf_op jit(solution)/shard_map/edge_columns/pallas_call | solution.py:162
  17.8 3.1 %collective-permute-start.2 = (f32[32,640]{1,0:T(8,128)S(1)}, f32[32,640]{1,0:T(8,128)S(1)}, u32[]{:S(2)}, u32[]{:S(2)}) collective-permute-start(f32[32,640]{1,0:T(8,128)S(1)} %get-tuple-element.24), channel_id=1, source_target_pairs={{0,1},{1,2},{2,3},{3,4},{4,5},{5,6},{6,7},{7,8},{8,9},{9,10},{10,1... | collective-permute-start | bytes 245768 | tf_op jit(solution)/shard_map/ppermute | solution.py:689
  21.0 1.3 %collective-permute-start.3 = (f32[32,640]{1,0:T(8,128)S(1)}, f32[32,640]{1,0:T(8,128)S(1)}, u32[]{:S(2)}, u32[]{:S(2)}) collective-permute-start(f32[32,640]{1,0:T(8,128)S(1)} %get-tuple-element.25), channel_id=1, source_target_pairs={{1,0},{2,1},{3,2},{4,3},{5,4},{6,5},{7,6},{8,7},{9,8},{10,9},{11,1... | collective-permute-start | bytes 245768 | tf_op jit(solution)/shard_map/ppermute | solution.py:689
  22.3 0.2 collective-permute-done.2.from_left
  22.4 3.7 %collective-permute-done.3.from_right = f32[32,640]{1,0:T(8,128)S(1)} collective-permute-done((f32[32,640]{1,0:T(8,128)S(1)}, f32[32,640]{1,0:T(8,128)S(1)}, u32[]{:S(2)}, u32[]{:S(2)}) %collective-permute-start.3) | collective-permute-done | bytes 81952 | tf_op jit(solution)/shard_map/ppermute | solution.py:689
  26.1 0.0 copy-done.17
  26.1 0.0 copy-done.8
  26.1 0.0 copy-done.10
  26.2 0.0 copy-done.18
  26.2 6.8 %slope.1 = (f32[3,256,512]{2,1,0:T(8,128)}, f32[6272,128]{1,0:T(8,128)S(1)}) custom-call(f32[256,512]{1,0:T(8,128)S(1)} %copy-done.6, f32[2,256,512]{2,1,0:T(8,128)S(1)} %copy-done, f32[2,256,512]{2,1,0:T(8,128)S(1)} %copy-done.1, f32[256,512]{1,0:T(8,128)S(1)} %copy-done.8, s32[256,512]{1,0:T(8,128)S(1)} %copy-done.10, ...), custom_call_target="tpu_custom_call" | custom-call | tf_op jit(solution)/shard_map/slope/pallas_call | solution.py:364
  33.0 1.6 %copy-done.11 = f32[6272,128]{1,0:T(8,128)} copy-done((f32[6272,128]{1,0:T(8,128)}, f32[6272,128]{1,0:T(8,128)S(1)}, u32[]{:S(2)}) %copy-start.11) | copy-done | bytes 3211288
  34.7 12.9 %all-to-all-start = ((f32[128,49,1,128]{3,2,1,0:T(1,128)}), f32[128,49,1,128]{3,2,1,0:T(1,128)S(1)}, u32[]{:S(2)}, u32[]{:S(2)}) async-start(f32[128,49,1,128]{3,2,1,0:T(1,128)} %bitcast.14), calls=%async_computation | async-start | bytes 6422528 | tf_op jit(solution)/shard_map/all_to_all | solution.py:693
  47.6 0.1 add_convert_fusion.sides
  47.7 1.2 copy-done.3
  48.9 1.6 %copy-done.5 = f32[2,512,512]{2,1,0:T(8,128)S(1)} copy-done((f32[2,512,512]{2,1,0:T(8,128)S(1)}, f32[2,512,512]{2,1,0:T(8,128)}, u32[]{:S(2)}) %copy-start.5) | copy-done | bytes 2097176
  50.5 1.3 %prepare.1 = (f32[5,544,128]{2,1,0:T(8,128)S(1)}, f32[2,5,512,128]{3,2,1,0:T(8,128)S(1)}, f32[2,5,8,128]{3,2,1,0:T(8,128)S(1)}, f32[2,5,8,128]{3,2,1,0:T(8,128)S(1)}) custom-call(f32[512,512]{1,0:T(8,128)S(1)} %copy-done.3, f32[2,512,512]{2,1,0:T(8,128)S(1)} %copy-done.5, f32[16,512]{1,0:T(8,128)S(1)} %collective-permute-done.above, ...), custom_call_target="tpu_custom_call" | custom-call | flops 4194304 | bytes 8388608 | tf_op jit(solution)/shard_map/prepare/pallas_call | solution.py:429
  51.8 1.5 %copy-done.12 = f32[2,5,512,128]{3,2,1,0:T(8,128)} copy-done((f32[2,5,512,128]{3,2,1,0:T(8,128)}, f32[2,5,512,128]{3,2,1,0:T(8,128)S(1)}, u32[]{:S(2)}) %copy-start.12) | copy-done | bytes 2621464
  53.3 1.1 copy-done.14
  54.4 34.4 %all-to-all-done = f32[128,49,1,128]{3,2,1,0:T(1,128)S(1)} async-done(((f32[128,49,1,128]{3,2,1,0:T(1,128)}), f32[128,49,1,128]{3,2,1,0:T(1,128)S(1)}, u32[]{:S(2)}, u32[]{:S(2)}) %all-to-all-start) | async-done | bytes 3211296 | tf_op jit(solution)/shard_map/all_to_all | solution.py:693
  88.8 2.8 %place.1 = (f32[2,5,512,128]{3,2,1,0:T(8,128)S(1)}, f32[2,5,8,128]{3,2,1,0:T(8,128)S(1)}, f32[2,5,8,128]{3,2,1,0:T(8,128)S(1)}) custom-call(f32[6272,128]{1,0:T(8,128)S(1)} %bitcast.12, f32[2,5,8,128]{3,2,1,0:T(8,128)S(1)} %get-tuple-element.28.first_momentum, f32[2,5,8,128]{3,2,1,0:T(8,128)S(1)} %get-tuple-element.29.last_momentum), custom_call_target="tpu_custom_call" | custom-call | tf_op jit(solution)/shard_map/place/pallas_call | solution.py:476
  91.6 3.0 %collective-permute-start.4 = (f32[2,5,8,128]{3,2,1,0:T(8,128)S(1)}, f32[2,5,8,128]{3,2,1,0:T(8,128)S(1)}, u32[]{:S(2)}, u32[]{:S(2)}) collective-permute-start(f32[2,5,8,128]{3,2,1,0:T(8,128)S(1)} %get-tuple-element.34), channel_id=1, source_target_pairs={{0,16},{16,32},{32,48},{48,64},{64,80},{80,96},{96,112},{1,17},{17... | collective-permute-start | bytes 122888 | tf_op jit(solution)/shard_map/ppermute | solution.py:689
  94.6 0.0 copy-start.15
  94.7 2.2 %collective-permute-start.5 = (f32[2,5,8,128]{3,2,1,0:T(8,128)S(1)}, f32[2,5,8,128]{3,2,1,0:T(8,128)S(1)}, u32[]{:S(2)}, u32[]{:S(2)}) collective-permute-start(f32[2,5,8,128]{3,2,1,0:T(8,128)S(1)} %get-tuple-element.35), channel_id=1, source_target_pairs={{16,0},{32,16},{48,32},{64,48},{80,64},{96,80},{112,96},{17,1},{33... | collective-permute-start | bytes 122888 | tf_op jit(solution)/shard_map/ppermute | solution.py:689
  96.9 1.8 %raise_lake.1 = f32[512,512]{1,0:T(8,128)} custom-call(f32[6272,128]{1,0:T(8,128)S(1)} %bitcast.13, f32[512,512]{1,0:T(8,128)S(1)} %copy-done.16), custom_call_target="tpu_custom_call" | custom-call | flops 629145600 | bytes 6291456 | tf_op jit(solution)/shard_map/raise_lake/pallas_call | solution.py:492
  98.7 0.0 collective-permute-done.4.above
  98.7 1.5 %collective-permute-done.5.below = f32[2,5,8,128]{3,2,1,0:T(8,128)S(1)} collective-permute-done((f32[2,5,8,128]{3,2,1,0:T(8,128)S(1)}, f32[2,5,8,128]{3,2,1,0:T(8,128)S(1)}, u32[]{:S(2)}, u32[]{:S(2)}) %collective-permute-start.5) | collective-permute-done | bytes 40992 | tf_op jit(solution)/shard_map/ppermute | solution.py:689
  100.2 0.0 copy-done.15
  100.2 6.7 %krylov.1 = (f32[2,5,544,128]{3,2,1,0:T(8,128)S(1)}, f32[2,5,544,128]{3,2,1,0:T(8,128)S(1)}, f32[2,5,544,128]{3,2,1,0:T(8,128)S(1)}, f32[128,128]{1,0:T(8,128)S(1)}) custom-call(s32[4]{0:T(128)S(1)} %add_convert_fusion.sides, f32[2,5,512,128]{3,2,1,0:T(8,128)S(1)} %get-tuple-element.32.flow, f32[2,5,512,128]{3,2,1,0:T(8,128)S(1)} %copy-done.13, ...), custom_call_target="tpu_custom_call" | custom-call | tf_op jit(solution)/shard_map/krylov/pallas_call | solution.py:602
  107.0 14.6 %all_to_all.10 = f32[128,1,128]{2,1,0:T(1,128)S(1)} all-to-all(f32[128,1,128]{2,1,0:T(1,128)S(1)} %bitcast.16), channel_id=1, replica_groups=mesh['gx'=8,'gy'=16] {'gx','gy'}, dimensions={0} | all-to-all | bytes 131072 | tf_op jit(solution)/shard_map/all_to_all | solution.py:693
  121.5 1.6 %finish.1 = f32[2,512,512]{2,1,0:T(8,128)} custom-call(f32[128,128]{1,0:T(8,128)S(1)} %bitcast.15, f32[2,5,544,128]{3,2,1,0:T(8,128)S(1)} %get-tuple-element.38.b, f32[2,5,544,128]{3,2,1,0:T(8,128)S(1)} %get-tuple-element.39.w1, f32[2,5,544,128]{3,2,1,0:T(8,128)S(1)} %get-tuple-element.40.w2), custom_call_target="tpu_custom_call" | custom-call | tf_op jit(solution)/shard_map/finish/pallas_call | solution.py:676
  (14 shorter events, 0.0 us)
Async XLA Ops:
  0.6 11.9 %copy-start.2 = (f32[512,512]{1,0:T(8,128)S(1)}, f32[512,512]{1,0:T(8,128)}, u32[]{:S(2)}) copy-start(f32[512,512]{1,0:T(8,128)} %d.5) | copy-start | bytes 3145732
  0.6 11.9 %copy-start.1 = (f32[2,256,512]{2,1,0:T(8,128)S(1)}, f32[2,256,512]{2,1,0:T(8,128)}, u32[]{:S(2)}) copy-start(f32[2,256,512]{2,1,0:T(8,128)} %bed.1) | copy-start | bytes 3145732
  0.7 11.9 %copy-start = (f32[2,256,512]{2,1,0:T(8,128)S(1)}, f32[2,256,512]{2,1,0:T(8,128)}, u32[]{:S(2)}) copy-start(f32[2,256,512]{2,1,0:T(8,128)} %mom.1) | copy-start | bytes 3145732
  0.7 11.9 %copy-start.6 = (f32[256,512]{1,0:T(8,128)S(1)}, f32[256,512]{1,0:T(8,128)}, u32[]{:S(2)}) copy-start(f32[256,512]{1,0:T(8,128)} %h_in.1) | copy-start | bytes 1572868
  2.5 6.5 %collective-permute-start = (f32[16,512]{1,0:T(8,128)}, f32[16,512]{1,0:T(8,128)S(1)}, u32[]{:S(2)}, u32[]{:S(2)}) collective-permute-start(f32[16,512]{1,0:T(8,128)} %get-tuple-element.22), channel_id=1, source_target_pairs={{0,16},{16,32},{32,48},{48,64},{64,80},{80,96},{96,112},{1,17},{17... | collective-permute-start | bytes 98312 | tf_op jit(solution)/shard_map/ppermute | solution.py:689
  7.1 19.1 %copy-start.17 = (s32[1,1,256,1]{2,3,1,0:T(1,128)S(1)}, s32[1,1,256,1]{2,3,1,0:T(1,128)}, u32[]{:S(2)}) copy-start(s32[1,1,256,1]{2,3,1,0:T(1,128)} %param.15) | copy-start | bytes 3076
  7.1 5.4 %collective-permute-start.1 = (f32[16,512]{1,0:T(8,128)}, f32[16,512]{1,0:T(8,128)S(1)}, u32[]{:S(2)}, u32[]{:S(2)}) collective-permute-start(f32[16,512]{1,0:T(8,128)} %get-tuple-element.23), channel_id=1, source_target_pairs={{16,0},{32,16},{48,32},{64,48},{80,64},{96,80},{112,96},{17,1},{33... | collective-permute-start | bytes 98312 | tf_op jit(solution)/shard_map/ppermute | solution.py:689
  12.5 1.6 %copy-start.4 = (f32[2,512,512]{2,1,0:T(8,128)S(1)}, f32[2,512,512]{2,1,0:T(8,128)}, u32[]{:S(2)}) copy-start(f32[2,512,512]{2,1,0:T(8,128)} %lm.1) | copy-start | bytes 6291460
  14.1 1.0 copy-start.7
  15.2 1.0 copy-start.9
  16.2 9.9 %copy-start.8 = (f32[256,512]{1,0:T(8,128)S(1)}, f32[256,512]{1,0:T(8,128)}, u32[]{:S(2)}) copy-start(f32[256,512]{1,0:T(8,128)} %fric.1) | copy-start | bytes 1572868
  16.2 9.9 %copy-start.10 = (s32[256,512]{1,0:T(8,128)S(1)}, s32[256,512]{1,0:T(8,128)}, u32[]{:S(2)}) copy-start(s32[256,512]{1,0:T(8,128)} %act.1) | copy-start | bytes 1572868
  16.2 9.9 %copy-start.18 = (s32[1,1,256]{2,1,0:T(1,128)S(1)}, s32[1,1,256]{2,1,0:T(1,128)}, u32[]{:S(2)}) copy-start(s32[1,1,256]{2,1,0:T(1,128)} %param.16) | copy-start | bytes 3076
  17.8 4.6 %collective-permute-start.2 = (f32[32,640]{1,0:T(8,128)S(1)}, f32[32,640]{1,0:T(8,128)S(1)}, u32[]{:S(2)}, u32[]{:S(2)}) collective-permute-start(f32[32,640]{1,0:T(8,128)S(1)} %get-tuple-element.24), channel_id=1, source_target_pairs={{0,1},{1,2},{2,3},{3,4},{4,5},{5,6},{6,7},{7,8},{8,9},{9,10},{10,1... | collective-permute-start | bytes 245768 | tf_op jit(solution)/shard_map/ppermute | solution.py:689
  21.0 5.2 %collective-permute-start.3 = (f32[32,640]{1,0:T(8,128)S(1)}, f32[32,640]{1,0:T(8,128)S(1)}, u32[]{:S(2)}, u32[]{:S(2)}) collective-permute-start(f32[32,640]{1,0:T(8,128)S(1)} %get-tuple-element.25), channel_id=1, source_target_pairs={{1,0},{2,1},{3,2},{4,3},{5,4},{6,5},{7,6},{8,7},{9,8},{10,9},{11,1... | collective-permute-start | bytes 245768 | tf_op jit(solution)/shard_map/ppermute | solution.py:689
  33.0 1.7 %copy-start.11 = (f32[6272,128]{1,0:T(8,128)}, f32[6272,128]{1,0:T(8,128)S(1)}, u32[]{:S(2)}) copy-start(f32[6272,128]{1,0:T(8,128)S(1)} %get-tuple-element.27) | copy-start | bytes 9633796
  34.7 54.1 %all-to-all-start = ((f32[128,49,1,128]{3,2,1,0:T(1,128)}), f32[128,49,1,128]{3,2,1,0:T(1,128)S(1)}, u32[]{:S(2)}, u32[]{:S(2)}) async-start(f32[128,49,1,128]{3,2,1,0:T(1,128)} %bitcast.14), calls=%async_computation | async-start | bytes 6422528 | tf_op jit(solution)/shard_map/all_to_all | solution.py:693
  47.7 1.2 copy-start.3
  48.9 1.6 %copy-start.5 = (f32[2,512,512]{2,1,0:T(8,128)S(1)}, f32[2,512,512]{2,1,0:T(8,128)}, u32[]{:S(2)}) copy-start(f32[2,512,512]{2,1,0:T(8,128)} %lm.1) | copy-start | bytes 6291460
  51.8 1.5 %copy-start.12 = (f32[2,5,512,128]{3,2,1,0:T(8,128)}, f32[2,5,512,128]{3,2,1,0:T(8,128)S(1)}, u32[]{:S(2)}) copy-start(f32[2,5,512,128]{3,2,1,0:T(8,128)S(1)} %get-tuple-element.33.momentum) | copy-start | bytes 7864324
  53.3 1.1 copy-start.14
  88.8 8.1 %copy-start.16 = (f32[512,512]{1,0:T(8,128)S(1)}, f32[512,512]{1,0:T(8,128)}, u32[]{:S(2)}) copy-start(f32[512,512]{1,0:T(8,128)} %height.1) | copy-start | bytes 3145732
  91.6 7.1 %collective-permute-start.4 = (f32[2,5,8,128]{3,2,1,0:T(8,128)S(1)}, f32[2,5,8,128]{3,2,1,0:T(8,128)S(1)}, u32[]{:S(2)}, u32[]{:S(2)}) collective-permute-start(f32[2,5,8,128]{3,2,1,0:T(8,128)S(1)} %get-tuple-element.34), channel_id=1, source_target_pairs={{0,16},{16,32},{32,48},{48,64},{64,80},{80,96},{96,112},{1,17},{17... | collective-permute-start | bytes 122888 | tf_op jit(solution)/shard_map/ppermute | solution.py:689
  94.6 5.6 %copy-start.13 = (f32[2,5,512,128]{3,2,1,0:T(8,128)S(1)}, f32[2,5,512,128]{3,2,1,0:T(8,128)}, u32[]{:S(2)}) copy-start(f32[2,5,512,128]{3,2,1,0:T(8,128)} %copy-done.12) | copy-start | bytes 7864324
  94.6 5.6 %copy-start.15 = (f32[5,544,128]{2,1,0:T(8,128)S(1)}, f32[5,544,128]{2,1,0:T(8,128)}, u32[]{:S(2)}) copy-start(f32[5,544,128]{2,1,0:T(8,128)} %copy-done.14) | copy-start | bytes 4177924
  94.7 5.6 %collective-permute-start.5 = (f32[2,5,8,128]{3,2,1,0:T(8,128)S(1)}, f32[2,5,8,128]{3,2,1,0:T(8,128)S(1)}, u32[]{:S(2)}, u32[]{:S(2)}) collective-permute-start(f32[2,5,8,128]{3,2,1,0:T(8,128)S(1)} %get-tuple-element.35), channel_id=1, source_target_pairs={{16,0},{32,16},{48,32},{64,48},{80,64},{96,80},{112,96},{17,1},{33... | collective-permute-start | bytes 122888 | tf_op jit(solution)/shard_map/ppermute | solution.py:689

commit v3 on v2

--- a/solution.py
+++ b/solution.py
@@ -87,87 +87,138 @@
     )(h, mom, bed, fric, act, d)
 
 
-def edge_columns_kernel(h, m, b, f, a, d, l, above, below, right, left, mat):
-    sides = (slice(0, 128), slice(C - 128, C))
-
-    def pair(read):
-        return tuple(functools.partial(read, lane) for lane in sides)
-
+GROUP = R + 128
+LAKE = 4 * GROUP
+WIDTH = LAKE + L + 128
+
+
+def put(acc, lane, first, last, base, wide):
+    turned = pltpu.roll(last, (base + wide) % 128, 1)
+    acc = jnp.where((lane >= base) & (lane < base + wide), turned, acc)
+    turned = pltpu.roll(first, 64 + base, 1)
+    return jnp.where((lane >= 64 + base) & (lane < 64 + base + wide), turned, acc)
+
+
+def edge_columns_kernel(h, m, b, f, a, d, l, right, left, hs, ms, bs, fs, as_, ds, ls, mat, sems):
+    copies = []
+    pairs = ((h, hs), (m, ms), (b, bs), (f, fs), (a, as_), (d, ds), (l, ls))
+    for q, (src, dst) in enumerate(pairs):
+        for side, lane in enumerate((0, C - 128)):
+            at = (slice(None),) * (len(src.shape) - 1) + (pl.ds(lane, 128),)
+            copies.append(pltpu.make_async_copy(src.at[at], dst.at[side], sems.at[2 * q + side]))
+    for c in copies:
+        c.start()
     slope = (
-        pair(lambda lane, s: h[s, lane]),
-        pair(lambda lane, s: m[0, s, lane]),
-        pair(lambda lane, s: m[1, s, lane]),
-        pair(lambda lane, s: b[0, s, lane]),
-        pair(lambda lane, s: b[1, s, lane]),
-        pair(lambda lane, s: f[s, lane]),
-        pair(lambda lane, s: a[s, lane].astype(F32)),
+        lambda e, s: hs[e, s, :],
+        lambda e, s: ms[e, 0, s, :],
+        lambda e, s: ms[e, 1, s, :],
+        lambda e, s: bs[e, 0, s, :],
+        lambda e, s: bs[e, 1, s, :],
+        lambda e, s: fs[e, s, :],
+        lambda e, s: as_[e, s, :].astype(F32),
     )
     lake = (
-        pair(lambda lane, s: d[s, lane]),
-        pair(lambda lane, s: l[0, s, lane]),
-        pair(lambda lane, s: l[1, s, lane]),
+        (lambda e, s: ds[e, s, :], 32, 2),
+        (lambda e, s: ls[e, 0, s, :], 34, 3),
+        (lambda e, s: ls[e, 1, s, :], 37, 3),
     )
     step = 64
-
-    def put(acc, lane, first, last, i, wide):
-        base, base_left = (2 * i, 64 + 2 * i) if wide == 2 else (16 + 3 * i, 80 + 3 * i)
-        turned = pltpu.roll(last, (base + wide) % 128, 1)
-        acc = jnp.where((lane >= base) & (lane < base + wide), turned, acc)
-        turned = pltpu.roll(first, base_left, 1)
-        return jnp.where((lane >= base_left) & (lane < base_left + wide), turned, acc)
-
-    def both(t, _):
-        s = pl.ds(pl.multiple_of(t * step, step), step)
-        lane = lanes((step, 128))
-        acc = jnp.zeros((step, 128), F32)
-        for i, (first, last) in enumerate(slope):
-            acc = put(acc, lane, first(s), last(s), i, 2)
-        for i, (first, last) in enumerate(lake):
-            acc = put(acc, lane, first(s), last(s), i, 3)
-        mat[s, :] = acc
-        return 0
-
-    def lake_only(t, _):
-        s = pl.ds(pl.multiple_of(t * step, step), step)
-        lane = lanes((step, 128))
-        acc = jnp.zeros((step, 128), F32)
-        for i, (first, last) in enumerate(lake):
-            acc = put(acc, lane, first(s), last(s), i, 3)
-        mat[s, :] = acc
-        return 0
-
-    lax.fori_loop(0, R // step, both, 0)
-    lax.fori_loop(R // step, L // step, lake_only, 0)
-    lane, row = lanes((8, 128)), rows((8, 128))
-
-    def corner(b_row, a_row, where):
-        low = jnp.broadcast_to(below[b_row : b_row + 1, where], (8, 128))
-        high = jnp.broadcast_to(above[a_row : a_row + 1, where], (8, 128))
-        return jnp.where(row == 0, low, jnp.where(row == 7, high, 0.0))
-
-    acc = mat[R : R + 8, :]
-    for i in range(3):
-        acc = put(acc, lane, corner(2 * i, 2 * i + 1, slice(0, 128)), corner(2 * i, 2 * i + 1, slice(C - 128, C)), i, 2)
-    mat[R : R + 8, :] = acc
-    acc = put(jnp.zeros((8, 128), F32), lane, corner(10, 11, slice(0, 128)), corner(10, 11, slice(C - 128, C)), 0, 3)
-    mat[L : L + 8, :] = acc
-    mat[L + 8 : L + 128, :] = jnp.zeros((120, 128), F32)
+    mat[L:, :] = jnp.zeros((128, 128), F32)
+    for c in copies:
+        c.wait()
+
+    def body(both):
+        def run(t, _):
+            s = pl.ds(pl.multiple_of(t * step, step), step)
+            lane = lanes((step, 128))
+            acc = jnp.zeros((step, 128), F32)
+            if both:
+                for i, read in enumerate(slope):
+                    acc = put(acc, lane, read(0, s), read(1, s), 4 * i, 4)
+            for read, base, wide in lake:
+                acc = put(acc, lane, read(0, s), read(1, s), base, wide)
+            mat[s, :] = acc
+            return 0
+
+        return run
+
+    lax.fori_loop(0, R // step, body(True), 0)
+    lax.fori_loop(R // step, L // step, body(False), 0)
     for t in range(5):
         turned = mat[128 * t : 128 * t + 128, :].T
-        right[:, 128 * t : 128 * t + 128] = turned[0:32, :]
-        left[:, 128 * t : 128 * t + 128] = turned[64:96, :]
-
-
-def edge_columns(h, mom, bed, fric, act, d, lm, above, below):
+        for out, row in ((right, 0), (left, 64)):
+            if t < 3:
+                for g in range(4):
+                    at = GROUP * g + 128 * t
+                    out[:, at : at + 128] = turned[row + 8 * g : row + 8 * g + 8, :]
+            out[:, LAKE + 128 * t : LAKE + 128 * t + 128] = turned[row + 32 : row + 40, :]
+
+
+def edge_columns(h, mom, bed, fric, act, d, lm):
     return pl.pallas_call(
         edge_columns_kernel,
-        in_specs=[VMEM] * 9,
+        in_specs=[HBM] * 7,
         out_specs=[VMEM] * 2,
-        out_shape=[jax.ShapeDtypeStruct((32, WIDE), F32)] * 2,
-        scratch_shapes=[pltpu.VMEM((WIDE, 128), F32)],
-        compiler_params=params(16),
+        out_shape=[jax.ShapeDtypeStruct((8, WIDTH), F32)] * 2,
+        scratch_shapes=[
+            pltpu.VMEM((2, R, 128), F32),
+            pltpu.VMEM((2, 2, R, 128), F32),
+            pltpu.VMEM((2, 2, R, 128), F32),
+            pltpu.VMEM((2, R, 128), F32),
+            pltpu.VMEM((2, R, 128), jnp.int32),
+            pltpu.VMEM((2, L, 128), F32),
+            pltpu.VMEM((2, 2, L, 128), F32),
+            pltpu.VMEM((WIDE, 128), F32),
+            pltpu.SemaphoreType.DMA((14,)),
+        ],
+        compiler_params=params(),
+        cost_estimate=pl.CostEstimate(flops=8 * MIB, bytes_accessed=6 * MIB, transcendentals=0),
         name="edge_columns",
-    )(h, mom, bed, fric, act, d, lm, above, below)
+    )(h, mom, bed, fric, act, d, lm)
+
+
+def corners_kernel(right_in, left_in, above, below, right, left):
+    lane, row = lanes((8, 128)), rows((8, 128))
+
+    def line(x, r, where):
+        return jnp.broadcast_to(x[r : r + 1, where], (8, 128))
+
+    def end(x, first_row, second_row, a, b):
+        def block(where):
+            y = jnp.where(row == first_row, line(x, a, where), 0.0)
+            return y if b is None else jnp.where(row == second_row, line(x, b, where), y)
+
+        return block(slice(0, 128)), block(slice(C - 128, C))
+
+    low, high = jnp.zeros((8, 128), F32), jnp.zeros((8, 128), F32)
+    for i in range(8):
+        if i == 7:
+            a, b, base, wide = 10, 11, 32, 2
+        elif i < 3:
+            a, b, base, wide = 2 * i, 2 * i + 1, 4 * i, 4
+        else:
+            a, b, base, wide = 3 + i, None, 4 * i, 4
+        low = put(low, lane, *end(below, 0, 1, a, b), base, wide)
+        if b is None:
+            high = put(high, lane, *end(above, 7, None, a, None), base, wide)
+        else:
+            high = put(high, lane, *end(above, 6, 7, a, b), base, wide)
+    turned = jnp.concatenate([low, jnp.zeros((112, 128), F32), high], axis=0).T
+    for out, src, at in ((right, right_in, 0), (left, left_in, 64)):
+        out[...] = src[...]
+        for g in range(4):
+            s = slice(GROUP * g + R, GROUP * g + R + 128)
+            out[:, s] = turned[at + 8 * g : at + 8 * g + 8, :]
+        out[:, LAKE + L :] = turned[at + 32 : at + 40, :]
+
+
+def corners(right, left, above, below):
+    return pl.pallas_call(
+        corners_kernel,
+        out_shape=[jax.ShapeDtypeStruct((8, WIDTH), F32)] * 2,
+        compiler_params=params(4),
+        name="corners",
+    )(right, left, above, below)
 
 
 def split2(x):
@@ -180,19 +231,33 @@
 
 
 def beside(xs):
-    lane = lanes(xs[0].shape)
+    lane, n = lanes(xs[0].shape), len(xs)
     r = [pltpu.roll(x, 1, 1) for x in xs]
-    left = [jnp.where(lane == 0, r[j - 1], r[j]) for j in range(5)]
+    left = [jnp.where(lane == 0, r[j - 1], r[j]) for j in range(n)]
     r = [pltpu.roll(x, 127, 1) for x in xs]
-    right = [jnp.where(lane == 127, r[(j + 1) % 5], r[j]) for j in range(5)]
+    right = [jnp.where(lane == 127, r[(j + 1) % n], r[j]) for j in range(n)]
     return left, right
 
 
-def slope_kernel(
-    h_in, mom, bed, fric, act, above, below, from_left, from_right, own, off,
-    out, payload,
-    ends, side, pa, qa, acc, turn,
-):
+def local_fluxes(h, m, n):
+    q = 0.25 / 0.075
+    inv = 1.0 / jnp.maximum(h, 0.25)
+    p = (0.5 * h) * h
+    mi = m * inv
+    cross = mi * n
+    fm = mi * m + p
+    gn = (n * inv) * n + p
+    h4, m4, n4 = q * h, q * m, q * n
+    along = ((h4 - m, h4 + m), (m4 - fm, m4 + fm), (n4 - cross, n4 + cross))
+    across = ((h4 - n, h4 + n), (m4 - cross, m4 + cross), (n4 - gn, n4 + gn))
+    return along, across
+
+
+def forcing(h, m, n, b0, b1, fr):
+    return None, 2.0 * (h * b0 - fr * m), 2.0 * (h * b1 - fr * n)
+
+
+def slope_kernel(h_in, mom, bed, fric, act, above, below, out, ends, pa, qa, acc):
     tile = (
         lambda s, lane: h_in[s, lane],
         lambda s, lane: mom[0, s, lane],
@@ -212,62 +277,20 @@
             else:
                 ends[0, i, j, 7:8, :] = above[3 + i : 4 + i, s]
                 ends[1, i, j, 0:1, :] = below[3 + i : 4 + i, s]
-    for t in range(3):
-        s = slice(128 * t, 128 * t + 128)
-        both = jnp.concatenate(
-            [from_left[:, s], jnp.zeros((32, 128), F32), from_right[:, s], jnp.zeros((32, 128), F32)], axis=0
-        )
-        turn[s, :] = both.T
-
-    def halo(w, lane, i):
-        left = pltpu.roll(w, 126 - 2 * i, 1)
-        right = pltpu.roll(w, 64 - 2 * i, 1)
-        return jnp.where(lane >= 126, left, jnp.where(lane < 2, right, 0.0))
-
-    step = 64
-
-    def columns(t, _):
-        r = pl.multiple_of(t * step, step)
-        w = turn[pl.ds(r, step), :]
-        lane = lanes((step, 128))
-        for i in range(7):
-            side[i, pl.ds(r, step), :] = halo(w, lane, i)
-        return 0
-
-    lax.fori_loop(0, R // step, columns, 0)
-    w = turn[R : R + 8, :]
-    row = rows((8, 128))
-    for i in range(3):
-        block = halo(w, lanes((8, 128)), i)
-        ends[0, i, 4, :, :] = jnp.where(row == 7, block, 0.0)
-        ends[1, i, 4, :, :] = jnp.where(row == 0, block, 0.0)
-
-    k, q = 0.075, 0.25 / 0.075
+    k = 0.075
 
     def fluxes(u, s, get, h, m, n):
         pairs = [[], [], []]
-        for j in range(5):
-            inv = 1.0 / jnp.maximum(h[j], 0.25)
-            p = (0.5 * h[j]) * h[j]
-            mi = m[j] * inv
-            cross = mi * n[j]
-            fm = mi * m[j] + p
-            gn = (n[j] * inv) * n[j] + p
-            h4, m4, n4 = q * h[j], q * m[j], q * n[j]
-            pa[u, 0, j, s, :] = h4 - m[j]
-            qa[u, 0, j, s, :] = h4 + m[j]
-            pa[u, 1, j, s, :] = m4 - fm
-            qa[u, 1, j, s, :] = m4 + fm
-            pa[u, 2, j, s, :] = n4 - cross
-            qa[u, 2, j, s, :] = n4 + cross
-            fr = get(5, j)
-            pairs[0].append((h4 - n[j], h4 + n[j], None))
-            pairs[1].append((m4 - cross, m4 + cross, 2.0 * (h[j] * get(3, j) - fr * m[j])))
-            pairs[2].append((n4 - gn, n4 + gn, 2.0 * (h[j] * get(4, j) - fr * n[j])))
+        for j in range(4):
+            along, across = local_fluxes(h[j], m[j], n[j])
+            force = forcing(h[j], m[j], n[j], get(3, j), get(4, j), get(5, j))
+            for i in range(3):
+                pa[u, i, j, s, :], qa[u, i, j, s, :] = along[i]
+                pairs[i].append(across[i] + (force[i],))
         for i in range(3):
             _, right = beside([x[0] for x in pairs[i]])
             left, _ = beside([x[1] for x in pairs[i]])
-            for j in range(5):
+            for j in range(4):
                 x = left[j] + right[j]
                 acc[u, i, j, s, :] = x if i == 0 else x + pairs[i][j][2]
 
@@ -278,7 +301,7 @@
 
     def reader(s):
         def get(i, j):
-            return side[i, s, :] if j == 4 else tile[i](s, slice(128 * j, 128 * j + 128))
+            return tile[i](s, slice(128 * j, 128 * j + 128))
 
         return get
 
@@ -287,9 +310,9 @@
 
     def section(u, to, n, get):
         if u == 0:
-            new = [[get(i, j) for j in range(5)] for i in range(3)]
+            new = [[get(i, j) for j in range(4)] for i in range(3)]
         else:
-            new = [[combine(0, i, j, to, n, get(6, j)) for j in range(5)] for i in range(3)]
+            new = [[combine(0, i, j, to, n, get(6, j)) for j in range(4)] for i in range(3)]
         fluxes(u, pl.ds(to, n), get, *new)
 
     def body(u):
@@ -310,13 +333,60 @@
                 out[i, to, s] = combine(1, i, j, pl.multiple_of(TOP + r, 8), CHUNK, on)
         return 0
 
-    pa[0, :, :, TOP + R + 8 :, :] = jnp.zeros((3, 5, 8, 128), F32)
-    qa[0, :, :, 0:8, :] = jnp.zeros((3, 5, 8, 128), F32)
+    pa[0, :, :, TOP + R + 8 :, :] = jnp.zeros((3, 4, 8, 128), F32)
+    qa[0, :, :, 0:8, :] = jnp.zeros((3, 4, 8, 128), F32)
     for u in range(2):
         section(u, TOP - 8, 8, end_reader(0))
         section(u, TOP + R, 8, end_reader(1))
         lax.fori_loop(0, R // CHUNK, body(u), 0)
     lax.fori_loop(0, R // CHUNK, last, 0)
+
+
+def slope(h, mom, bed, fric, act, above, below):
+    return pl.pallas_call(
+        slope_kernel,
+        out_shape=jax.ShapeDtypeStruct((3, R, C), F32),
+        scratch_shapes=[pltpu.VMEM((2, 7, 4, 8, 128), F32)] + [pltpu.VMEM((2, 3, 4, SROWS, 128), F32)] * 3,
+        compiler_params=params(24),
+        cost_estimate=pl.CostEstimate(flops=32 * MIB, bytes_accessed=6 * MIB, transcendentals=0),
+        name="slope",
+    )(h, mom, bed, fric, act, above, below)
+
+
+def pack_kernel(fields, to_right, to_left, from_left, from_right, own, off, out, payload, strip):
+    shape = (8, GROUP)
+
+    def section(x):
+        h, m, n = x[:3]
+        along, across = local_fluxes(h, m, n)
+        force = forcing(h, m, n, *x[3:6])
+        new = []
+        for i in range(3):
+            y = pltpu.roll(along[i][0], GROUP - 1, 1) + pltpu.roll(along[i][1], 1, 1)
+            y = y + pltpu.roll(across[i][0], 7, 0) + pltpu.roll(across[i][1], 1, 0)
+            y = y if i == 0 else y + force[i]
+            new.append((0.075 * x[6]) * y)
+        return new
+
+    ends = []
+    for e, (before, after) in enumerate(((from_left, to_left), (to_right, from_right))):
+        for i in range(7):
+            r, s = 4 * (i % 2), slice(GROUP * (i // 2), GROUP * (i // 2) + GROUP)
+            strip[e, i, 0:4, :] = before[r : r + 4, s]
+            strip[e, i, 4:8, :] = after[r : r + 4, s]
+        x = [strip[e, i, :, :] for i in range(7)]
+        x = section(x) + x[3:]
+        ends.append([pltpu.roll(y, 4, 0) for y in section(x)])
+    row, lane = rows(shape), lanes((128, 128))
+    for i in range(3):
+        first = jnp.where(row < 2, ends[0][i], 0.0)
+        last = jnp.where(row >= 6, ends[1][i], 0.0)
+        for t in range(R // 128):
+            s = slice(128 * t, 128 * t + 128)
+            turned = jnp.concatenate([first[:, s], jnp.zeros((112, 128), F32), last[:, s]], axis=0).T
+            out[i, s, 0:128] = jnp.where(lane < 2, turned, fields[i, s, 0:128])
+            out[i, s, C - 128 : C] = jnp.where(lane >= 126, turned, fields[i, s, C - 128 : C])
+        out[i, :, 128 : C - 128] = fields[i, :, 128 : C - 128]
 
     owner = jnp.broadcast_to(own[...], (DEV, R))
     mine = rows((DEV, R)) == owner
@@ -360,37 +430,28 @@
     payload[pl.ds(TAG, DEV, stride=UNITS), :] = tags + to_right + to_left
 
 
-def slope(h, mom, bed, fric, act, above, below, from_left, from_right, own, off):
-    return pl.pallas_call(
-        slope_kernel,
-        in_specs=[VMEM] * 11,
-        out_specs=[VMEM] * 2,
+def pack(fields, to_right, to_left, from_left, from_right, own, off):
+    return pl.pallas_call(
+        pack_kernel,
         out_shape=[jax.ShapeDtypeStruct((3, R, C), F32), jax.ShapeDtypeStruct((DEV * UNITS, 128), F32)],
-        scratch_shapes=[
-            pltpu.VMEM((2, 7, 5, 8, 128), F32),
-            pltpu.VMEM((7, R, 128), F32),
-            pltpu.VMEM((2, 3, 5, SROWS, 128), F32),
-            pltpu.VMEM((2, 3, 5, SROWS, 128), F32),
-            pltpu.VMEM((2, 3, 5, SROWS, 128), F32),
-            pltpu.VMEM((384, 128), F32),
-        ],
-        compiler_params=params(34),
-        name="slope",
-    )(h, mom, bed, fric, act, above, below, from_left, from_right, own, off)
+        scratch_shapes=[pltpu.VMEM((2, 7, 8, GROUP), F32)],
+        compiler_params=params(20),
+        name="pack",
+    )(fields, to_right, to_left, from_left, from_right, own, off)
 
 
 def prepare_kernel(d, lm, above, below, from_left, from_right, coef, momentum, first, last, turn):
+    gap = jnp.zeros((56, 128), F32)
     for t in range(5):
-        s = slice(128 * t, 128 * t + 128)
-        both = jnp.concatenate(
-            [from_left[:, s], jnp.zeros((32, 128), F32), from_right[:, s], jnp.zeros((32, 128), F32)], axis=0
-        )
-        turn[s, :] = both.T
+        s = slice(LAKE + 128 * t, LAKE + 128 * t + 128)
+        both = jnp.concatenate([from_left[:, s], gap, from_right[:, s], gap], axis=0)
+        turn[128 * t : 128 * t + 128, :] = both.T
 
     def halo(w, lane, i):
-        left = pltpu.roll(w, 109 - 3 * i, 1)
-        right = pltpu.roll(w, 48 - 3 * i, 1)
-        return jnp.where(lane >= 125, left, jnp.where(lane < 3, right, 0.0))
+        wide, at = (2, 0) if i == 0 else (3, 3 * i - 1)
+        left = pltpu.roll(w, 128 - wide - at, 1)
+        right = pltpu.roll(w, 64 - at, 1)
+        return jnp.where(lane >= 128 - wide, left, jnp.where(lane < wide, right, 0.0))
 
     step = 64
 
@@ -417,10 +478,8 @@
             s = slice(128 * j, 128 * j + 128)
             coef[j, LTOP - 2 : LTOP, :] = 2.0 * above[10:12, s] - 2.0
             coef[j, LTOP + L : LTOP + L + 2, :] = 2.0 * below[10:12, s] - 2.0
-    block = 2.0 * halo(turn[L : L + 8, :], lanes((8, 128)), 0) - 2.0
-    row = rows((8, 128))
-    coef[4, LTOP - 8 : LTOP, :] = jnp.where(row == 7, block, 0.0)
-    coef[4, LTOP + L : LTOP + L + 8, :] = jnp.where(row == 0, block, 0.0)
+    coef[4, LTOP - 8 : LTOP, :] = 2.0 * halo(turn[L + 120 :, :], lanes((8, 128)), 0) - 2.0
+    coef[4, LTOP + L : LTOP + L + 8, :] = 2.0 * halo(turn[L : L + 8, :], lanes((8, 128)), 0) - 2.0
     first[...] = momentum[:, :, 0:8, :]
     last[...] = momentum[:, :, L - 8 : L, :]
 
@@ -696,10 +755,12 @@
 def per_device(h, mom, bed, fric, act, owners, offsets, height, lm, d):
     up, dn = edge_rows(h, mom, bed, fric, act, d)
     above, below = shift(dn, "gx", 1), shift(up, "gx", -1)
-    to_right, to_left = edge_columns(h, mom, bed, fric, act, d, lm, above, below)
+    to_right, to_left = edge_columns(h, mom, bed, fric, act, d, lm)
+    to_right, to_left = corners(to_right, to_left, above, below)
     from_left, from_right = shift(to_right, "gy", 1), shift(to_left, "gy", -1)
+    fields = slope(h, mom, bed, fric, act, above, below)
     own, off = owners.reshape(1, R), offsets.reshape(1, R)
-    fields, payload = slope(h, mom, bed, fric, act, above, below, from_left, from_right, own, off)
+    fields, payload = pack(fields, to_right, to_left, from_left, from_right, own, off)
     recv = exchange(payload.reshape(DEV, UNITS, 1, 128)).reshape(DEV * UNITS, 128)
     coef, momentum, first, last = prepare(d, lm, above, below, from_left, from_right)
     flow, first, last = place(recv, first, last)

time: 124 us -> 117 us (0.944)
  waiting for transfers between devices: 43.3 us -> 36 us
  local copies, waits for them, and re-layouts: 10.8 us -> 8.85 us
  Pallas kernels: 24.6 us -> 26.4 us
    ppermute x6, waiting for transfers between devices: 8.93 us -> 1.55 us  [shift(): lax.ppermute(x, axis, [(i, i + by) for i in range(n) if 0 <= i + by < n])]
    pallas_call x2 -> x4, Pallas kernels: 8.44 us -> 10.3 us  [the longest x1 4.35 us: edge_columns(): pl.pallas_call(edge_columns_kernel, in_specs=[HBM] * 7, out_specs=[VMEM]...]
    unnamed x38 -> x34, local copies, waits for them, and re-layouts: 10.8 us -> 8.85 us
  transfers between devices with their start and end apart: 7 -> 7, of which waited for: 5 -> 2; matrix products, arithmetic and copies ran while one was open for 0% -> 0% of each run, Pallas kernels for 3% -> 10%
where the time goes in v3:
time: 117 us
  waiting for transfers between devices  36 us (31%)
  starting transfers between devices  29.9 us (26%)
  Pallas kernels  26.4 us (23%)
  blocking collectives  14.6 us (12%)
  local copies, waits for them, and re-layouts  8.85 us (8%)
    all_to_all x1, waiting for transfers between devices, exchange(): return lax.all_to_all(x, AXES, split_axis=0, concat_axis=0, tiled=True)  34.4 us
    ppermute x6, starting transfers between devices, shift(): lax.ppermute(x, axis, [(i, i + by) for i in range(n) if 0 <= i + by < n])  16.3 us
    all_to_all x1, blocking collectives, exchange(): return lax.all_to_all(x, AXES, split_axis=0, concat_axis=0, tiled=True)  14.6 us
    all_to_all x1, starting transfers between devices, exchange(): return lax.all_to_all(x, AXES, split_axis=0, concat_axis=0, tiled=True)  13.6 us
    unnamed x34, local copies, waits for them, and re-layouts  8.85 us
    pallas_call x1, Pallas kernels, krylov(): pl.pallas_call(krylov_kernel, in_specs=[pl.BlockSpec(memory_space=pltpu.S...  6.71 us
    pallas_call x1, Pallas kernels, edge_columns(): pl.pallas_call(edge_columns_kernel, in_specs=[HBM] * 7, out_specs=[VMEM]...  4.35 us
    pallas_call x1, Pallas kernels, slope(): pl.pallas_call(slope_kernel, out_shape=jax.ShapeDtypeStruct((3, R, C), F3...  3.8 us
  transfers between devices with their start and end apart: 7, of which 2 were waited for; matrix products, arithmetic and copies ran while one was open for 0% of the time, Pallas kernels for 10%

profile of v3, /device:TPU:1, one launch (start us, length us, event | category | flops | bytes accessed | tf_op | source)
XLA Modules:
  0.0 116.7 jit_solution(11898239015606050481)
XLA Ops:
  0.6 1.7 %edge_rows.1 = (f32[16,512]{1,0:T(8,128)}, f32[16,512]{1,0:T(8,128)}) custom-call(f32[256,512]{1,0:T(8,128)} %h.3, f32[2,256,512]{2,1,0:T(8,128)} %m.3, f32[2,256,512]{2,1,0:T(8,128)} %b.3, f32[256,512]{1,0:T(8,128)} %f.3, s32[256,512]{1,0:T(8,128)} %a.3, f32[512,512]{1,0:T(8,128)} %d.5), custom_call_target="tpu_custom_call" | custom-call | tf_op jit(solution)/shard_map/edge_rows/pallas_call | solution.py:71
  2.3 4.6 %collective-permute-start = (f32[16,512]{1,0:T(8,128)}, f32[16,512]{1,0:T(8,128)S(1)}, u32[]{:S(2)}, u32[]{:S(2)}) collective-permute-start(f32[16,512]{1,0:T(8,128)} %get-tuple-element.24), channel_id=1, source_target_pairs={{0,16},{16,32},{32,48},{48,64},{64,80},{80,96},{96,112},{1,17},{17... | collective-permute-start | bytes 98312 | tf_op jit(solution)/shard_map/ppermute | solution.py:748
  6.9 0.0 copy-start.1
  6.9 0.0 copy-start.2
  6.9 0.0 copy-start.4
  6.9 0.0 copy-start.5
  7.0 0.0 copy-start.6
  7.0 2.2 %collective-permute-start.1 = (f32[16,512]{1,0:T(8,128)}, f32[16,512]{1,0:T(8,128)S(1)}, u32[]{:S(2)}, u32[]{:S(2)}) collective-permute-start(f32[16,512]{1,0:T(8,128)} %get-tuple-element.25), channel_id=1, source_target_pairs={{16,0},{32,16},{48,32},{64,48},{80,64},{96,80},{112,96},{17,1},{33... | collective-permute-start | bytes 98312 | tf_op jit(solution)/shard_map/ppermute | solution.py:748
  9.2 4.3 %edge_columns.1 = (f32[8,2176]{1,0:T(8,128)}, f32[8,2176]{1,0:T(8,128)}) custom-call(f32[256,512]{1,0:T(8,128)} %h.3, f32[2,256,512]{2,1,0:T(8,128)} %m.3, f32[2,256,512]{2,1,0:T(8,128)} %b.3, f32[256,512]{1,0:T(8,128)} %f.3, s32[256,512]{1,0:T(8,128)} %a.3, f32[512,512]{1,0:T(8,128)} %d.5, f32[2,512,512]{2,1,0:T(8,128)} %lm.1), custom_call_target="tpu_custom_call" | custom-call | flops 8388608 | bytes 6291456 | tf_op jit(solution)/shard_map/edge_columns/pallas_call | solution.py:158
  13.5 0.0 collective-permute-done.above
  13.5 0.0 collective-permute-done.1.below
  13.5 0.0 copy-start.13
  13.6 0.9 copy-done.13
  14.4 0.9 copy-done.14
  15.3 0.2 corners.1
  15.5 3.1 %collective-permute-start.2 = (f32[8,2176]{1,0:T(8,128)S(1)}, f32[8,2176]{1,0:T(8,128)S(1)}, u32[]{:S(2)}, u32[]{:S(2)}) collective-permute-start(f32[8,2176]{1,0:T(8,128)S(1)} %get-tuple-element.28.to_right), channel_id=1, source_target_pairs={{0,1},{1,2},{2,3},{3,4},{4,5},{5,6},{6,7},{7,8},{8,9},{9,10},{10,1... | collective-permute-start | bytes 208904 | tf_op jit(solution)/shard_map/ppermute | solution.py:748
  18.6 0.0 copy-start.15
  18.6 0.0 copy-start.16
  18.6 1.3 %collective-permute-start.3 = (f32[8,2176]{1,0:T(8,128)S(1)}, f32[8,2176]{1,0:T(8,128)S(1)}, u32[]{:S(2)}, u32[]{:S(2)}) collective-permute-start(f32[8,2176]{1,0:T(8,128)S(1)} %get-tuple-element.29.to_left), channel_id=1, source_target_pairs={{1,0},{2,1},{3,2},{4,3},{5,4},{6,5},{7,6},{8,7},{9,8},{10,9},{11,1... | collective-permute-start | bytes 208904 | tf_op jit(solution)/shard_map/ppermute | solution.py:748
  19.9 0.0 copy-done.1
  19.9 0.0 copy-done.2
  20.0 0.0 copy-done.4
  20.0 0.0 copy-done.5
  20.0 0.0 copy-done.6
  20.0 3.8 %slope.1.fields = f32[3,256,512]{2,1,0:T(8,128)S(1)} custom-call(f32[256,512]{1,0:T(8,128)S(1)} %copy-done.4, f32[2,256,512]{2,1,0:T(8,128)S(1)} %copy-done.1, f32[2,256,512]{2,1,0:T(8,128)S(1)} %copy-done.2, f32[256,512]{1,0:T(8,128)S(1)} %copy-done.5, s32[256,512]{1,0:T(8,128)S(1)} %copy-done.6, f32[16,512]{1,0:T(8,128)S(1)} %collective-permute-done.above, ...), custom_call_target="tpu_custom_call" | custom-call | flops 33554432 | bytes 6291456 | tf_op jit(solution)/shard_map/slope/pallas_call | solution.py:346
  23.8 0.0 collective-permute-done.2.from_left
  23.8 0.0 collective-permute-done.3.from_right
  23.8 2.0 %pack.1 = (f32[3,256,512]{2,1,0:T(8,128)}, f32[6272,128]{1,0:T(8,128)S(1)}) custom-call(f32[3,256,512]{2,1,0:T(8,128)S(1)} %slope.1.fields, f32[8,2176]{1,0:T(8,128)S(1)} %get-tuple-element.28.to_right, f32[8,2176]{1,0:T(8,128)S(1)} %get-tuple-element.29.to_left, f32[8,2176]{1,0:T(8,128)S(1)} %collective-permute-done.2.from_left, ...), custom_call_target="tpu_custom_call" | custom-call | tf_op jit(solution)/shard_map/pack/pallas_call | solution.py:434
  25.9 1.6 %copy-done.7 = f32[6272,128]{1,0:T(8,128)} copy-done((f32[6272,128]{1,0:T(8,128)}, f32[6272,128]{1,0:T(8,128)S(1)}, u32[]{:S(2)}) %copy-start.7) | copy-done | bytes 3211288
  27.5 13.6 %all-to-all-start = ((f32[128,49,1,128]{3,2,1,0:T(1,128)}), f32[128,49,1,128]{3,2,1,0:T(1,128)S(1)}, u32[]{:S(2)}, u32[]{:S(2)}) async-start(f32[128,49,1,128]{3,2,1,0:T(1,128)} %bitcast.14), calls=%async_computation | async-start | bytes 6422528 | tf_op jit(solution)/shard_map/all_to_all | solution.py:752
  41.1 0.1 add_convert_fusion.sides
  41.2 1.2 %copy-done = f32[512,512]{1,0:T(8,128)S(1)} copy-done((f32[512,512]{1,0:T(8,128)S(1)}, f32[512,512]{1,0:T(8,128)}, u32[]{:S(2)}) %copy-start) | copy-done | bytes 1048600
  42.4 1.6 %copy-done.3 = f32[2,512,512]{2,1,0:T(8,128)S(1)} copy-done((f32[2,512,512]{2,1,0:T(8,128)S(1)}, f32[2,512,512]{2,1,0:T(8,128)}, u32[]{:S(2)}) %copy-start.3) | copy-done | bytes 2097176
  44.0 1.3 %prepare.1 = (f32[5,544,128]{2,1,0:T(8,128)S(1)}, f32[2,5,512,128]{3,2,1,0:T(8,128)S(1)}, f32[2,5,8,128]{3,2,1,0:T(8,128)S(1)}, f32[2,5,8,128]{3,2,1,0:T(8,128)S(1)}) custom-call(f32[512,512]{1,0:T(8,128)S(1)} %copy-done, f32[2,512,512]{2,1,0:T(8,128)S(1)} %copy-done.3, f32[16,512]{1,0:T(8,128)S(1)} %collective-permute-done.above, ...), custom_call_target="tpu_custom_call" | custom-call | flops 4194304 | bytes 8388608 | tf_op jit(solution)/shard_map/prepare/pallas_call | solution.py:488
  45.3 1.5 %copy-done.8 = f32[2,5,512,128]{3,2,1,0:T(8,128)} copy-done((f32[2,5,512,128]{3,2,1,0:T(8,128)}, f32[2,5,512,128]{3,2,1,0:T(8,128)S(1)}, u32[]{:S(2)}) %copy-start.8) | copy-done | bytes 2621464
  46.8 1.1 copy-done.10
  47.9 34.4 %all-to-all-done = f32[128,49,1,128]{3,2,1,0:T(1,128)S(1)} async-done(((f32[128,49,1,128]{3,2,1,0:T(1,128)}), f32[128,49,1,128]{3,2,1,0:T(1,128)S(1)}, u32[]{:S(2)}, u32[]{:S(2)}) %all-to-all-start) | async-done | bytes 3211296 | tf_op jit(solution)/shard_map/all_to_all | solution.py:752
  82.3 2.8 %place.1 = (f32[2,5,512,128]{3,2,1,0:T(8,128)S(1)}, f32[2,5,8,128]{3,2,1,0:T(8,128)S(1)}, f32[2,5,8,128]{3,2,1,0:T(8,128)S(1)}) custom-call(f32[6272,128]{1,0:T(8,128)S(1)} %bitcast.12, f32[2,5,8,128]{3,2,1,0:T(8,128)S(1)} %get-tuple-element.32.first_momentum, f32[2,5,8,128]{3,2,1,0:T(8,128)S(1)} %get-tuple-element.33.last_momentum), custom_call_target="tpu_custom_call" | custom-call | tf_op jit(solution)/shard_map/place/pallas_call | solution.py:535
  85.1 3.0 %collective-permute-start.4 = (f32[2,5,8,128]{3,2,1,0:T(8,128)S(1)}, f32[2,5,8,128]{3,2,1,0:T(8,128)S(1)}, u32[]{:S(2)}, u32[]{:S(2)}) collective-permute-start(f32[2,5,8,128]{3,2,1,0:T(8,128)S(1)} %get-tuple-element.38), channel_id=1, source_target_pairs={{0,16},{16,32},{32,48},{48,64},{64,80},{80,96},{96,112},{1,17},{17... | collective-permute-start | bytes 122888 | tf_op jit(solution)/shard_map/ppermute | solution.py:748
  88.2 0.0 copy-start.11
  88.2 2.2 %collective-permute-start.5 = (f32[2,5,8,128]{3,2,1,0:T(8,128)S(1)}, f32[2,5,8,128]{3,2,1,0:T(8,128)S(1)}, u32[]{:S(2)}, u32[]{:S(2)}) collective-permute-start(f32[2,5,8,128]{3,2,1,0:T(8,128)S(1)} %get-tuple-element.39), channel_id=1, source_target_pairs={{16,0},{32,16},{48,32},{64,48},{80,64},{96,80},{112,96},{17,1},{33... | collective-permute-start | bytes 122888 | tf_op jit(solution)/shard_map/ppermute | solution.py:748
  90.4 1.8 %raise_lake.1 = f32[512,512]{1,0:T(8,128)} custom-call(f32[6272,128]{1,0:T(8,128)S(1)} %bitcast.13, f32[512,512]{1,0:T(8,128)S(1)} %copy-done.12), custom_call_target="tpu_custom_call" | custom-call | flops 629145600 | bytes 6291456 | tf_op jit(solution)/shard_map/raise_lake/pallas_call | solution.py:551
  92.2 0.0 collective-permute-done.4.above
  92.2 1.5 %collective-permute-done.5.below = f32[2,5,8,128]{3,2,1,0:T(8,128)S(1)} collective-permute-done((f32[2,5,8,128]{3,2,1,0:T(8,128)S(1)}, f32[2,5,8,128]{3,2,1,0:T(8,128)S(1)}, u32[]{:S(2)}, u32[]{:S(2)}) %collective-permute-start.5) | collective-permute-done | bytes 40992 | tf_op jit(solution)/shard_map/ppermute | solution.py:748
  93.7 0.0 copy-done.11
  93.8 6.7 %krylov.1 = (f32[2,5,544,128]{3,2,1,0:T(8,128)S(1)}, f32[2,5,544,128]{3,2,1,0:T(8,128)S(1)}, f32[2,5,544,128]{3,2,1,0:T(8,128)S(1)}, f32[128,128]{1,0:T(8,128)S(1)}) custom-call(s32[4]{0:T(128)S(1)} %add_convert_fusion.sides, f32[2,5,512,128]{3,2,1,0:T(8,128)S(1)} %get-tuple-element.36.flow, f32[2,5,512,128]{3,2,1,0:T(8,128)S(1)} %copy-done.9, ...), custom_call_target="tpu_custom_call" | custom-call | tf_op jit(solution)/shard_map/krylov/pallas_call | solution.py:661
  100.5 14.6 %all_to_all.10 = f32[128,1,128]{2,1,0:T(1,128)S(1)} all-to-all(f32[128,1,128]{2,1,0:T(1,128)S(1)} %bitcast.16), channel_id=1, replica_groups=mesh['gx'=8,'gy'=16] {'gx','gy'}, dimensions={0} | all-to-all | bytes 131072 | tf_op jit(solution)/shard_map/all_to_all | solution.py:752
  115.0 1.6 %finish.1 = f32[2,512,512]{2,1,0:T(8,128)} custom-call(f32[128,128]{1,0:T(8,128)S(1)} %bitcast.15, f32[2,5,544,128]{3,2,1,0:T(8,128)S(1)} %get-tuple-element.42.b, f32[2,5,544,128]{3,2,1,0:T(8,128)S(1)} %get-tuple-element.43.w1, f32[2,5,544,128]{3,2,1,0:T(8,128)S(1)} %get-tuple-element.44.w2), custom_call_target="tpu_custom_call" | custom-call | tf_op jit(solution)/shard_map/finish/pallas_call | solution.py:735
  (12 shorter events, 0.0 us)
Async XLA Ops:
  2.3 11.2 %collective-permute-start = (f32[16,512]{1,0:T(8,128)}, f32[16,512]{1,0:T(8,128)S(1)}, u32[]{:S(2)}, u32[]{:S(2)}) collective-permute-start(f32[16,512]{1,0:T(8,128)} %get-tuple-element.24), channel_id=1, source_target_pairs={{0,16},{16,32},{32,48},{48,64},{64,80},{80,96},{96,112},{1,17},{17... | collective-permute-start | bytes 98312 | tf_op jit(solution)/shard_map/ppermute | solution.py:748
  6.9 13.0 %copy-start.1 = (f32[2,256,512]{2,1,0:T(8,128)S(1)}, f32[2,256,512]{2,1,0:T(8,128)}, u32[]{:S(2)}) copy-start(f32[2,256,512]{2,1,0:T(8,128)} %m.3) | copy-start | bytes 3145732
  6.9 13.0 %copy-start.2 = (f32[2,256,512]{2,1,0:T(8,128)S(1)}, f32[2,256,512]{2,1,0:T(8,128)}, u32[]{:S(2)}) copy-start(f32[2,256,512]{2,1,0:T(8,128)} %b.3) | copy-start | bytes 3145732
  6.9 13.0 %copy-start.4 = (f32[256,512]{1,0:T(8,128)S(1)}, f32[256,512]{1,0:T(8,128)}, u32[]{:S(2)}) copy-start(f32[256,512]{1,0:T(8,128)} %h.3) | copy-start | bytes 1572868
  6.9 13.0 %copy-start.5 = (f32[256,512]{1,0:T(8,128)S(1)}, f32[256,512]{1,0:T(8,128)}, u32[]{:S(2)}) copy-start(f32[256,512]{1,0:T(8,128)} %f.3) | copy-start | bytes 1572868
  7.0 13.0 %copy-start.6 = (s32[256,512]{1,0:T(8,128)S(1)}, s32[256,512]{1,0:T(8,128)}, u32[]{:S(2)}) copy-start(s32[256,512]{1,0:T(8,128)} %a.3) | copy-start | bytes 1572868
  7.0 6.6 %collective-permute-start.1 = (f32[16,512]{1,0:T(8,128)}, f32[16,512]{1,0:T(8,128)S(1)}, u32[]{:S(2)}, u32[]{:S(2)}) collective-permute-start(f32[16,512]{1,0:T(8,128)} %get-tuple-element.25), channel_id=1, source_target_pairs={{16,0},{32,16},{48,32},{64,48},{80,64},{96,80},{112,96},{17,1},{33... | collective-permute-start | bytes 98312 | tf_op jit(solution)/shard_map/ppermute | solution.py:748
  13.5 0.9 copy-start.13
  14.4 0.9 copy-start.14
  15.5 8.3 %collective-permute-start.2 = (f32[8,2176]{1,0:T(8,128)S(1)}, f32[8,2176]{1,0:T(8,128)S(1)}, u32[]{:S(2)}, u32[]{:S(2)}) collective-permute-start(f32[8,2176]{1,0:T(8,128)S(1)} %get-tuple-element.28.to_right), channel_id=1, source_target_pairs={{0,1},{1,2},{2,3},{3,4},{4,5},{5,6},{6,7},{7,8},{8,9},{9,10},{10,1... | collective-permute-start | bytes 208904 | tf_op jit(solution)/shard_map/ppermute | solution.py:748
  18.6 5.2 %copy-start.15 = (s32[1,1,256,1]{2,3,1,0:T(1,128)S(1)}, s32[1,1,256,1]{2,3,1,0:T(1,128)}, u32[]{:S(2)}) copy-start(s32[1,1,256,1]{2,3,1,0:T(1,128)} %param.15) | copy-start | bytes 3076
  18.6 5.2 %copy-start.16 = (s32[1,1,256]{2,1,0:T(1,128)S(1)}, s32[1,1,256]{2,1,0:T(1,128)}, u32[]{:S(2)}) copy-start(s32[1,1,256]{2,1,0:T(1,128)} %param.16) | copy-start | bytes 3076
  18.6 5.2 %collective-permute-start.3 = (f32[8,2176]{1,0:T(8,128)S(1)}, f32[8,2176]{1,0:T(8,128)S(1)}, u32[]{:S(2)}, u32[]{:S(2)}) collective-permute-start(f32[8,2176]{1,0:T(8,128)S(1)} %get-tuple-element.29.to_left), channel_id=1, source_target_pairs={{1,0},{2,1},{3,2},{4,3},{5,4},{6,5},{7,6},{8,7},{9,8},{10,9},{11,1... | collective-permute-start | bytes 208904 | tf_op jit(solution)/shard_map/ppermute | solution.py:748
  25.9 1.6 %copy-start.7 = (f32[6272,128]{1,0:T(8,128)}, f32[6272,128]{1,0:T(8,128)S(1)}, u32[]{:S(2)}) copy-start(f32[6272,128]{1,0:T(8,128)S(1)} %get-tuple-element.31) | copy-start | bytes 9633796
  27.5 54.8 %all-to-all-start = ((f32[128,49,1,128]{3,2,1,0:T(1,128)}), f32[128,49,1,128]{3,2,1,0:T(1,128)S(1)}, u32[]{:S(2)}, u32[]{:S(2)}) async-start(f32[128,49,1,128]{3,2,1,0:T(1,128)} %bitcast.14), calls=%async_computation | async-start | bytes 6422528 | tf_op jit(solution)/shard_map/all_to_all | solution.py:752
  41.2 1.2 %copy-start = (f32[512,512]{1,0:T(8,128)S(1)}, f32[512,512]{1,0:T(8,128)}, u32[]{:S(2)}) copy-start(f32[512,512]{1,0:T(8,128)} %d.5) | copy-start | bytes 3145732
  42.4 1.6 %copy-start.3 = (f32[2,512,512]{2,1,0:T(8,128)S(1)}, f32[2,512,512]{2,1,0:T(8,128)}, u32[]{:S(2)}) copy-start(f32[2,512,512]{2,1,0:T(8,128)} %lm.1) | copy-start | bytes 6291460
  45.3 1.5 %copy-start.8 = (f32[2,5,512,128]{3,2,1,0:T(8,128)}, f32[2,5,512,128]{3,2,1,0:T(8,128)S(1)}, u32[]{:S(2)}) copy-start(f32[2,5,512,128]{3,2,1,0:T(8,128)S(1)} %get-tuple-element.37.momentum) | copy-start | bytes 7864324
  46.8 1.1 copy-start.10
  82.3 8.1 %copy-start.12 = (f32[512,512]{1,0:T(8,128)S(1)}, f32[512,512]{1,0:T(8,128)}, u32[]{:S(2)}) copy-start(f32[512,512]{1,0:T(8,128)} %height.1) | copy-start | bytes 3145732
  85.1 7.1 %collective-permute-start.4 = (f32[2,5,8,128]{3,2,1,0:T(8,128)S(1)}, f32[2,5,8,128]{3,2,1,0:T(8,128)S(1)}, u32[]{:S(2)}, u32[]{:S(2)}) collective-permute-start(f32[2,5,8,128]{3,2,1,0:T(8,128)S(1)} %get-tuple-element.38), channel_id=1, source_target_pairs={{0,16},{16,32},{32,48},{48,64},{64,80},{80,96},{96,112},{1,17},{17... | collective-permute-start | bytes 122888 | tf_op jit(solution)/shard_map/ppermute | solution.py:748
  88.1 5.6 %copy-start.9 = (f32[2,5,512,128]{3,2,1,0:T(8,128)S(1)}, f32[2,5,512,128]{3,2,1,0:T(8,128)}, u32[]{:S(2)}) copy-start(f32[2,5,512,128]{3,2,1,0:T(8,128)} %copy-done.8) | copy-start | bytes 7864324
  88.2 5.6 %copy-start.11 = (f32[5,544,128]{2,1,0:T(8,128)S(1)}, f32[5,544,128]{2,1,0:T(8,128)}, u32[]{:S(2)}) copy-start(f32[5,544,128]{2,1,0:T(8,128)} %copy-done.10) | copy-start | bytes 4177924
  88.2 5.6 %collective-permute-start.5 = (f32[2,5,8,128]{3,2,1,0:T(8,128)S(1)}, f32[2,5,8,128]{3,2,1,0:T(8,128)S(1)}, u32[]{:S(2)}, u32[]{:S(2)}) collective-permute-start(f32[2,5,8,128]{3,2,1,0:T(8,128)S(1)} %get-tuple-element.39), channel_id=1, source_target_pairs={{16,0},{32,16},{48,32},{64,48},{80,64},{96,80},{112,96},{17,1},{33... | collective-permute-start | bytes 122888 | tf_op jit(solution)/shard_map/ppermute | solution.py:748

commit v4 on v3

--- a/solution.py
+++ b/solution.py
@@ -28,11 +28,16 @@
 
 
 HBM = pl.BlockSpec(memory_space=pltpu.HBM)
+SMEM = pl.BlockSpec(memory_space=pltpu.SMEM)
 VMEM = pl.BlockSpec(memory_space=pltpu.VMEM)
 
 
-def params(limit=None):
-    return pltpu.CompilerParams(vmem_limit_bytes=limit * MIB if limit else 60 * 1024 * 1024)
+def params(limit=None, room=0):
+    return pltpu.CompilerParams(vmem_limit_bytes=limit * MIB if limit else 60 * 1024 * 1024 - room)
+
+
+def present(sides):
+    return tuple(sides[i].astype(F32) for i in range(4))
 
 
 def lanes(shape):
@@ -82,7 +87,7 @@
             pltpu.VMEM((2, 8, C), F32),
             pltpu.SemaphoreType.DMA((12,)),
         ],
-        compiler_params=params(),
+        compiler_params=params(room=7_000_000),
         name="edge_rows",
     )(h, mom, bed, fric, act, d)
 
@@ -99,7 +104,7 @@
     return jnp.where((lane >= 64 + base) & (lane < 64 + base + wide), turned, acc)
 
 
-def edge_columns_kernel(h, m, b, f, a, d, l, right, left, hs, ms, bs, fs, as_, ds, ls, mat, sems):
+def edge_columns_kernel(h, m, b, f, a, d, l, both, hs, ms, bs, fs, as_, ds, ls, mat, sems):
     copies = []
     pairs = ((h, hs), (m, ms), (b, bs), (f, fs), (a, as_), (d, ds), (l, ls))
     for q, (src, dst) in enumerate(pairs):
@@ -127,12 +132,12 @@
     for c in copies:
         c.wait()
 
-    def body(both):
+    def body(slope_too):
         def run(t, _):
             s = pl.ds(pl.multiple_of(t * step, step), step)
             lane = lanes((step, 128))
             acc = jnp.zeros((step, 128), F32)
-            if both:
+            if slope_too:
                 for i, read in enumerate(slope):
                     acc = put(acc, lane, read(0, s), read(1, s), 4 * i, 4)
             for read, base, wide in lake:
@@ -146,20 +151,20 @@
     lax.fori_loop(R // step, L // step, body(False), 0)
     for t in range(5):
         turned = mat[128 * t : 128 * t + 128, :].T
-        for out, row in ((right, 0), (left, 64)):
+        for e, row in ((0, 0), (1, 64)):
             if t < 3:
                 for g in range(4):
                     at = GROUP * g + 128 * t
-                    out[:, at : at + 128] = turned[row + 8 * g : row + 8 * g + 8, :]
-            out[:, LAKE + 128 * t : LAKE + 128 * t + 128] = turned[row + 32 : row + 40, :]
+                    both[e, :, at : at + 128] = turned[row + 8 * g : row + 8 * g + 8, :]
+            both[e, :, LAKE + 128 * t : LAKE + 128 * t + 128] = turned[row + 32 : row + 40, :]
 
 
 def edge_columns(h, mom, bed, fric, act, d, lm):
     return pl.pallas_call(
         edge_columns_kernel,
         in_specs=[HBM] * 7,
-        out_specs=[VMEM] * 2,
-        out_shape=[jax.ShapeDtypeStruct((8, WIDTH), F32)] * 2,
+        out_specs=VMEM,
+        out_shape=jax.ShapeDtypeStruct((2, 8, WIDTH), F32),
         scratch_shapes=[
             pltpu.VMEM((2, R, 128), F32),
             pltpu.VMEM((2, 2, R, 128), F32),
@@ -171,13 +176,13 @@
             pltpu.VMEM((WIDE, 128), F32),
             pltpu.SemaphoreType.DMA((14,)),
         ],
-        compiler_params=params(),
+        compiler_params=params(room=7_300_000),
         cost_estimate=pl.CostEstimate(flops=8 * MIB, bytes_accessed=6 * MIB, transcendentals=0),
         name="edge_columns",
     )(h, mom, bed, fric, act, d, lm)
 
 
-def corners_kernel(right_in, left_in, above, below, right, left):
+def corners_kernel(sides, both, above, below, right, left):
     lane, row = lanes((8, 128)), rows((8, 128))
 
     def line(x, r, where):
@@ -203,22 +208,24 @@
             high = put(high, lane, *end(above, 7, None, a, None), base, wide)
         else:
             high = put(high, lane, *end(above, 6, 7, a, b), base, wide)
-    turned = jnp.concatenate([low, jnp.zeros((112, 128), F32), high], axis=0).T
-    for out, src, at in ((right, right_in, 0), (left, left_in, 64)):
-        out[...] = src[...]
+    up, down, _, _ = present(sides)
+    turned = jnp.concatenate([down * low, jnp.zeros((112, 128), F32), up * high], axis=0).T
+    for e, out, at in ((0, right, 0), (1, left, 64)):
+        out[...] = both[e]
         for g in range(4):
             s = slice(GROUP * g + R, GROUP * g + R + 128)
             out[:, s] = turned[at + 8 * g : at + 8 * g + 8, :]
         out[:, LAKE + L :] = turned[at + 32 : at + 40, :]
 
 
-def corners(right, left, above, below):
+def corners(sides, both, above, below):
     return pl.pallas_call(
         corners_kernel,
+        in_specs=[SMEM] + [VMEM] * 3,
         out_shape=[jax.ShapeDtypeStruct((8, WIDTH), F32)] * 2,
         compiler_params=params(4),
         name="corners",
-    )(right, left, above, below)
+    )(sides, both, above, below)
 
 
 def split2(x):
@@ -257,7 +264,7 @@
     return None, 2.0 * (h * b0 - fr * m), 2.0 * (h * b1 - fr * n)
 
 
-def slope_kernel(h_in, mom, bed, fric, act, above, below, out, ends, pa, qa, acc):
+def slope_kernel(sides, h_in, mom, bed, fric, act, above, below, out, ends, pa, qa, acc):
     tile = (
         lambda s, lane: h_in[s, lane],
         lambda s, lane: mom[0, s, lane],
@@ -267,16 +274,17 @@
         lambda s, lane: fric[s, lane],
         lambda s, lane: act[s, lane].astype(F32),
     )
+    up, down, _, _ = present(sides)
     ends[...] = jnp.zeros(ends.shape, F32)
     for i in range(7):
         for j in range(4):
             s = slice(128 * j, 128 * j + 128)
             if i < 3:
-                ends[0, i, j, 6:8, :] = above[2 * i : 2 * i + 2, s]
-                ends[1, i, j, 0:2, :] = below[2 * i : 2 * i + 2, s]
+                ends[0, i, j, 6:8, :] = up * above[2 * i : 2 * i + 2, s]
+                ends[1, i, j, 0:2, :] = down * below[2 * i : 2 * i + 2, s]
             else:
-                ends[0, i, j, 7:8, :] = above[3 + i : 4 + i, s]
-                ends[1, i, j, 0:1, :] = below[3 + i : 4 + i, s]
+                ends[0, i, j, 7:8, :] = up * above[3 + i : 4 + i, s]
+                ends[1, i, j, 0:1, :] = down * below[3 + i : 4 + i, s]
     k = 0.075
 
     def fluxes(u, s, get, h, m, n):
@@ -342,18 +350,19 @@
     lax.fori_loop(0, R // CHUNK, last, 0)
 
 
-def slope(h, mom, bed, fric, act, above, below):
+def slope(sides, h, mom, bed, fric, act, above, below):
     return pl.pallas_call(
         slope_kernel,
+        in_specs=[SMEM] + [VMEM] * 7,
         out_shape=jax.ShapeDtypeStruct((3, R, C), F32),
         scratch_shapes=[pltpu.VMEM((2, 7, 4, 8, 128), F32)] + [pltpu.VMEM((2, 3, 4, SROWS, 128), F32)] * 3,
         compiler_params=params(24),
         cost_estimate=pl.CostEstimate(flops=32 * MIB, bytes_accessed=6 * MIB, transcendentals=0),
         name="slope",
-    )(h, mom, bed, fric, act, above, below)
-
-
-def pack_kernel(fields, to_right, to_left, from_left, from_right, own, off, out, payload, strip):
+    )(sides, h, mom, bed, fric, act, above, below)
+
+
+def pack_kernel(sides, fields, to_right, to_left, from_left, from_right, own, off, fields_out, sent, strip, out, payload, sems):
     shape = (8, GROUP)
 
     def section(x):
@@ -369,15 +378,17 @@
         return new
 
     ends = []
-    for e, (before, after) in enumerate(((from_left, to_left), (to_right, from_right))):
+    _, _, on_left, on_right = present(sides)
+    for e, (before, after, a, b) in enumerate(((from_left, to_left, on_left, 1.0), (to_right, from_right, 1.0, on_right))):
         for i in range(7):
             r, s = 4 * (i % 2), slice(GROUP * (i // 2), GROUP * (i // 2) + GROUP)
-            strip[e, i, 0:4, :] = before[r : r + 4, s]
-            strip[e, i, 4:8, :] = after[r : r + 4, s]
+            strip[e, i, 0:4, :] = a * before[r : r + 4, s]
+            strip[e, i, 4:8, :] = b * after[r : r + 4, s]
         x = [strip[e, i, :, :] for i in range(7)]
         x = section(x) + x[3:]
         ends.append([pltpu.roll(y, 4, 0) for y in section(x)])
     row, lane = rows(shape), lanes((128, 128))
+    copies = []
     for i in range(3):
         first = jnp.where(row < 2, ends[0][i], 0.0)
         last = jnp.where(row >= 6, ends[1][i], 0.0)
@@ -387,6 +398,10 @@
             out[i, s, 0:128] = jnp.where(lane < 2, turned, fields[i, s, 0:128])
             out[i, s, C - 128 : C] = jnp.where(lane >= 126, turned, fields[i, s, C - 128 : C])
         out[i, :, 128 : C - 128] = fields[i, :, 128 : C - 128]
+        for t in range(2):
+            s = pl.ds(R // 2 * t, R // 2)
+            copies.append(pltpu.make_async_copy(out.at[i, s, :], fields_out.at[i, s, :], sems.at[2 * i + t]))
+            copies[-1].start()
 
     owner = jnp.broadcast_to(own[...], (DEV, R))
     mine = rows((DEV, R)) == owner
@@ -394,13 +409,6 @@
     rank = jnp.dot(mine.astype(BF16), before, preferred_element_type=F32)
     picks = [mine & (rank == float(k_)) for k_ in range(CAP)]
     pickb = [p.astype(BF16) for p in picks]
-    for i in range(3):
-        parts = split2(out[i])
-        for k_ in range(CAP):
-            y = pick(pickb[k_], parts)
-            for j in range(4):
-                payload[pl.ds(12 * k_ + 4 * i + j, DEV, stride=UNITS), :] = y[:, 128 * j : 128 * j + 128]
-
     lane, dest = lanes((DEV, 128)), rows((DEV, 128))
     tags = jnp.zeros((DEV, 128), F32)
     tag_value = jnp.broadcast_to((off[...] + 1).astype(F32), (DEV, R))
@@ -429,18 +437,44 @@
     to_left = jnp.where(column < NY - 1, pltpu.roll(to_left, DEV - 1, 0), 0.0)
     payload[pl.ds(TAG, DEV, stride=UNITS), :] = tags + to_right + to_left
 
-
-def pack(fields, to_right, to_left, from_left, from_right, own, off):
+    parts = [split2(out[i]) for i in range(3)]
+    groups, piece = 4, 32
+    part = DEV // groups
+    for e in range(groups):
+        some = jnp.concatenate([x[part * e : part * e + part, :] for x in pickb], axis=0)
+        for i in range(3):
+            y = pick(some, parts[i])
+            for k_ in range(CAP):
+                for j in range(4):
+                    at = part * UNITS * e + 12 * k_ + 4 * i + j
+                    payload[pl.ds(at, part, stride=UNITS), :] = y[part * k_ : part * k_ + part, 128 * j : 128 * j + 128]
+        for t in range(part * e, part * e + part, piece):
+            s = pl.ds(UNITS * t, UNITS * piece)
+            copies.append(pltpu.make_async_copy(payload.at[s, :], sent.at[s, :], sems.at[6 + t // piece]))
+            copies[-1].start()
+    for copy in copies:
+        copy.wait()
+
+
+def pack(sides, fields, to_right, to_left, from_left, from_right, own, off):
     return pl.pallas_call(
         pack_kernel,
+        in_specs=[SMEM] + [VMEM] * 7,
+        out_specs=[HBM, HBM],
         out_shape=[jax.ShapeDtypeStruct((3, R, C), F32), jax.ShapeDtypeStruct((DEV * UNITS, 128), F32)],
-        scratch_shapes=[pltpu.VMEM((2, 7, 8, GROUP), F32)],
-        compiler_params=params(20),
+        scratch_shapes=[
+            pltpu.VMEM((2, 7, 8, GROUP), F32),
+            pltpu.VMEM((3, R, C), F32),
+            pltpu.VMEM((DEV * UNITS, 128), F32),
+            pltpu.SemaphoreType.DMA((22,)),
+        ],
+        compiler_params=params(room=12_000_000),
         name="pack",
-    )(fields, to_right, to_left, from_left, from_right, own, off)
-
-
-def prepare_kernel(d, lm, above, below, from_left, from_right, coef, momentum, first, last, turn):
+    )(sides, fields, to_right, to_left, from_left, from_right, own, off)
+
+
+def prepare_kernel(sides, d, lm, above, below, from_left, from_right, coef, momentum, first, last, turn):
+    _, _, on_left, on_right = present(sides)
     gap = jnp.zeros((56, 128), F32)
     for t in range(5):
         s = slice(LAKE + 128 * t, LAKE + 128 * t + 128)
@@ -451,7 +485,7 @@
         wide, at = (2, 0) if i == 0 else (3, 3 * i - 1)
         left = pltpu.roll(w, 128 - wide - at, 1)
         right = pltpu.roll(w, 64 - at, 1)
-        return jnp.where(lane >= 128 - wide, left, jnp.where(lane < wide, right, 0.0))
+        return jnp.where(lane >= 128 - wide, on_left * left, jnp.where(lane < wide, on_right * right, 0.0))
 
     step = 64
 
@@ -484,15 +518,16 @@
     last[...] = momentum[:, :, L - 8 : L, :]
 
 
-def prepare(d, lm, above, below, from_left, from_right):
+def prepare(sides, d, lm, above, below, from_left, from_right):
     return pl.pallas_call(
         prepare_kernel,
+        in_specs=[SMEM] + [VMEM] * 6,
         out_shape=[jax.ShapeDtypeStruct(x, F32) for x in ((5, LROWS, 128), (2, 5, L, 128), (2, 5, 8, 128), (2, 5, 8, 128))],
         scratch_shapes=[pltpu.VMEM((WIDE, 128), F32)],
         compiler_params=params(16),
         cost_estimate=pl.CostEstimate(flops=4 * MIB, bytes_accessed=8 * MIB, transcendentals=0),
         name="prepare",
-    )(d, lm, above, below, from_left, from_right)
+    )(sides, d, lm, above, below, from_left, from_right)
 
 
 def one_hot(hot, tags, first):
@@ -564,9 +599,9 @@
     for x in (b, w1, w2):
         x[:, :, 0 : LTOP - 8, :] = jnp.zeros((2, 5, LTOP - 8, 128), F32)
         x[:, :, LTOP + L + 8 :, :] = jnp.zeros((2, 5, LTOP - 8, 128), F32)
-    b[:, :, LTOP - 8 : LTOP, :] = above[...]
-    b[:, :, LTOP + L : LTOP + L + 8, :] = below[...]
-    up, down, left, right = (sides[i].astype(F32) for i in range(4))
+    up, down, left, right = present(sides)
+    b[:, :, LTOP - 8 : LTOP, :] = up * above[...]
+    b[:, :, LTOP + L : LTOP + L + 8, :] = down * below[...]
     edge = jnp.where(lanes((1, 128)) < 64, right, left)
 
     def total_side(t, _):
@@ -745,7 +780,7 @@
 
 def shift(x, axis, by):
     n = {"gx": NX, "gy": NY}[axis]
-    return lax.ppermute(x, axis, [(i, i + by) for i in range(n) if 0 <= i + by < n])
+    return lax.ppermute(x, axis, [(i, (i + by) % n) for i in range(n)])
 
 
 def exchange(x):
@@ -753,21 +788,21 @@
 
 
 def per_device(h, mom, bed, fric, act, owners, offsets, height, lm, d):
+    i, j = lax.axis_index("gx"), lax.axis_index("gy")
+    sides = jnp.stack([i > 0, i < NX - 1, j > 0, j < NY - 1]).astype(jnp.int32)
     up, dn = edge_rows(h, mom, bed, fric, act, d)
     above, below = shift(dn, "gx", 1), shift(up, "gx", -1)
-    to_right, to_left = edge_columns(h, mom, bed, fric, act, d, lm)
-    to_right, to_left = corners(to_right, to_left, above, below)
+    columns = edge_columns(h, mom, bed, fric, act, d, lm)
+    to_right, to_left = corners(sides, columns, above, below)
     from_left, from_right = shift(to_right, "gy", 1), shift(to_left, "gy", -1)
-    fields = slope(h, mom, bed, fric, act, above, below)
+    fields = slope(sides, h, mom, bed, fric, act, above, below)
     own, off = owners.reshape(1, R), offsets.reshape(1, R)
-    fields, payload = pack(fields, to_right, to_left, from_left, from_right, own, off)
+    fields, payload = pack(sides, fields, to_right, to_left, from_left, from_right, own, off)
     recv = exchange(payload.reshape(DEV, UNITS, 1, 128)).reshape(DEV * UNITS, 128)
-    coef, momentum, first, last = prepare(d, lm, above, below, from_left, from_right)
+    coef, momentum, first, last = prepare(sides, d, lm, above, below, from_left, from_right)
     flow, first, last = place(recv, first, last)
     new_height = raise_lake(recv, height)
     b_above, b_below = shift(last, "gx", 1), shift(first, "gx", -1)
-    i, j = lax.axis_index("gx"), lax.axis_index("gy")
-    sides = jnp.stack([i > 0, i < NX - 1, j > 0, j < NY - 1]).astype(jnp.int32)
     flow, new_height = lax.optimization_barrier((flow, new_height))
     b, w1, w2, sums = krylov(sides, flow, momentum, b_above, b_below, coef)
     sums = exchange(sums.reshape(DEV, 1, 128)).reshape(DEV, 128)

time: 117 us -> 107 us (0.915)
  starting transfers between devices: 29.9 us -> 17.3 us
  Pallas kernels: 26.4 us -> 28.5 us
  blocking collectives: 14.6 us -> 16.4 us
    ppermute x6, starting transfers between devices: 16.3 us -> 9.9 us  [shift(): return lax.ppermute(x, axis, [(i, (i + by) % n) for i in range(n)])]
    all_to_all x1, starting transfers between devices: 13.6 us -> 7.43 us  [exchange(): return lax.all_to_all(x, AXES, split_axis=0, concat_axis=0, tiled=True)]
    pallas_call x5, Pallas kernels: 11.7 us -> 14.3 us  [the longest x1 4.54 us: slope(): pl.pallas_call(slope_kernel, in_specs=[SMEM] + [VMEM] * 7, out_shape=jax....]
    all_to_all x1, blocking collectives: 14.6 us -> 16.4 us  [exchange(): return lax.all_to_all(x, AXES, split_axis=0, concat_axis=0, tiled=True)]
    unnamed x34 -> x32, local copies, waits for them, and re-layouts: 8.85 us -> 8.1 us
  transfers between devices with their start and end apart: 7 -> 7, of which waited for: 2 -> 2; matrix products, arithmetic and copies ran while one was open for 0% -> 0% of each run, Pallas kernels for 10% -> 11%
where the time goes in v4:
time: 107 us
  waiting for transfers between devices  35.8 us (33%)
  Pallas kernels  28.5 us (27%)
  starting transfers between devices  17.3 us (16%)
  blocking collectives  16.4 us (15%)
  local copies, waits for them, and re-layouts  8.1 us (8%)
    all_to_all x1, waiting for transfers between devices, exchange(): return lax.all_to_all(x, AXES, split_axis=0, concat_axis=0, tiled=True)  33.9 us
    all_to_all x1, blocking collectives, exchange(): return lax.all_to_all(x, AXES, split_axis=0, concat_axis=0, tiled=True)  16.4 us
    ppermute x6, starting transfers between devices, shift(): return lax.ppermute(x, axis, [(i, (i + by) % n) for i in range(n)])  9.9 us
    unnamed x32, local copies, waits for them, and re-layouts  8.1 us
    all_to_all x1, starting transfers between devices, exchange(): return lax.all_to_all(x, AXES, split_axis=0, concat_axis=0, tiled=True)  7.43 us
    pallas_call x1, Pallas kernels, krylov(): pl.pallas_call(krylov_kernel, in_specs=[pl.BlockSpec(memory_space=pltpu.S...  6.72 us
    pallas_call x1, Pallas kernels, slope(): pl.pallas_call(slope_kernel, in_specs=[SMEM] + [VMEM] * 7, out_shape=jax....  4.54 us
    pallas_call x1, Pallas kernels, edge_columns(): pl.pallas_call(edge_columns_kernel, in_specs=[HBM] * 7, out_specs=VMEM, o...  3.75 us
  transfers between devices with their start and end apart: 7, of which 2 were waited for; matrix products, arithmetic and copies ran while one was open for 0% of the time, Pallas kernels for 11%

profile of v4, /device:TPU:1, one launch (start us, length us, event | category | flops | bytes accessed | tf_op | source)
XLA Modules:
  0.0 107.0 jit_solution(6323473264854004325)
XLA Ops:
  0.6 0.0 copy-start.4
  0.6 1.0 copy-done.4
  1.7 0.0 copy-start.5
  1.7 1.1 %edge_rows.1 = (f32[16,512]{1,0:T(8,128)S(1)}, f32[16,512]{1,0:T(8,128)S(1)}) custom-call(f32[256,512]{1,0:T(8,128)S(1)} %copy-done.4, f32[2,256,512]{2,1,0:T(8,128)} %m.3, f32[2,256,512]{2,1,0:T(8,128)} %b.3, f32[256,512]{1,0:T(8,128)} %f.3, s32[256,512]{1,0:T(8,128)} %a.3, f32[512,512]{1,0:T(8,128)} %d.5), custom_call_target="tpu_custom_call" | custom-call | tf_op jit(solution)/shard_map/edge_rows/pallas_call | solution.py:76
  2.8 2.7 %collective-permute-start = (f32[16,512]{1,0:T(8,128)S(1)}, f32[16,512]{1,0:T(8,128)S(1)}, u32[]{:S(2)}, u32[]{:S(2)}) collective-permute-start(f32[16,512]{1,0:T(8,128)S(1)} %get-tuple-element.22), channel_id=1, source_target_pairs={{0,16},{16,32},{32,48},{48,64},{64,80},{80,96},{96,112},{112,0},{1... | collective-permute-start | bytes 98312 | tf_op jit(solution)/shard_map/ppermute | solution.py:783
  5.5 0.0 collective-permute-start.1
  5.5 0.1 add_convert_fusion.sides
  5.6 0.0 copy-done.5
  5.6 0.0 copy-start.6
  5.6 0.0 copy-start.7
  5.6 3.8 %edge_columns.1.both = f32[2,8,2176]{2,1,0:T(8,128)S(1)} custom-call(f32[256,512]{1,0:T(8,128)S(1)} %copy-done.5, f32[2,256,512]{2,1,0:T(8,128)} %m.3, f32[2,256,512]{2,1,0:T(8,128)} %b.3, f32[256,512]{1,0:T(8,128)} %f.3, s32[256,512]{1,0:T(8,128)} %a.3, f32[512,512]{1,0:T(8,128)} %d.5, f32[2,512,512]{2,1,0:T(8,128)} %lm.1), custom_call_target="tpu_custom_call" | custom-call | flops 8388608 | bytes 6291456 | tf_op jit(solution)/shard_map/edge_columns/pallas_call | solution.py:163
  9.3 0.0 collective-permute-done.above
  9.4 0.0 collective-permute-done.1.below
  9.4 0.7 corners.1
  10.1 1.3 %collective-permute-start.2 = (f32[8,2176]{1,0:T(8,128)S(1)}, f32[8,2176]{1,0:T(8,128)S(1)}, u32[]{:S(2)}, u32[]{:S(2)}) collective-permute-start(f32[8,2176]{1,0:T(8,128)S(1)} %get-tuple-element.24.to_right), channel_id=1, source_target_pairs={{0,1},{1,2},{2,3},{3,4},{4,5},{5,6},{6,7},{7,8},{8,9},{9,10},{10,1... | collective-permute-start | bytes 208904 | tf_op jit(solution)/shard_map/ppermute | solution.py:783
  11.4 4.8 %collective-permute-start.3 = (f32[8,2176]{1,0:T(8,128)S(1)}, f32[8,2176]{1,0:T(8,128)S(1)}, u32[]{:S(2)}, u32[]{:S(2)}) collective-permute-start(f32[8,2176]{1,0:T(8,128)S(1)} %get-tuple-element.25.to_left), channel_id=1, source_target_pairs={{0,15},{1,0},{2,1},{3,2},{4,3},{5,4},{6,5},{7,6},{8,7},{9,8},{10,9... | collective-permute-start | bytes 208904 | tf_op jit(solution)/shard_map/ppermute | solution.py:783
  16.2 0.0 copy-done.1
  16.2 0.0 copy-done.2
  16.2 0.0 copy-done.6
  16.2 0.0 copy-done.7
  16.2 4.5 %slope.1.fields = f32[3,256,512]{2,1,0:T(8,128)S(1)} custom-call(s32[4]{0:T(128)S(1)} %add_convert_fusion.sides, f32[256,512]{1,0:T(8,128)S(1)} %copy-done.5, f32[2,256,512]{2,1,0:T(8,128)S(1)} %copy-done.1, f32[2,256,512]{2,1,0:T(8,128)S(1)} %copy-done.2, f32[256,512]{1,0:T(8,128)S(1)} %copy-done.6, s32[256,512]{1,0:T(8,128)S(1)} %copy-done.7, ...), custom_call_target="tpu_custom_call" | custom-call | flops 33554432 | bytes 6291456 | tf_op jit(solution)/shard_map/slope/pallas_call | solution.py:354
  20.8 0.0 collective-permute-done.2.from_left
  20.8 0.0 collective-permute-done.3.from_right
  20.8 0.0 copy-done.14
  20.8 0.0 copy-done.15
  20.8 3.4 %pack.1 = (f32[3,256,512]{2,1,0:T(8,128)}, f32[6272,128]{1,0:T(8,128)S(1)}) custom-call(s32[4]{0:T(128)S(1)} %add_convert_fusion.sides, f32[3,256,512]{2,1,0:T(8,128)S(1)} %slope.1.fields, f32[8,2176]{1,0:T(8,128)S(1)} %get-tuple-element.24.to_right, f32[8,2176]{1,0:T(8,128)S(1)} %get-tuple-element.25.to_left, ...), custom_call_target="tpu_custom_call" | custom-call | tf_op jit(solution)/shard_map/pack/pallas_call | solution.py:460
  24.2 0.0 copy-start.8
  24.3 1.6 %copy-done.8 = f32[6272,128]{1,0:T(8,128)} copy-done((f32[6272,128]{1,0:T(8,128)}, f32[6272,128]{1,0:T(8,128)S(1)}, u32[]{:S(2)}) %copy-start.8) | copy-done | bytes 3211288
  25.9 7.4 %all-to-all-start = ((f32[128,49,1,128]{3,2,1,0:T(1,128)}), f32[128,49,1,128]{3,2,1,0:T(1,128)S(1)}, u32[]{:S(2)}, u32[]{:S(2)}) async-start(f32[128,49,1,128]{3,2,1,0:T(1,128)} %bitcast.14), calls=%async_computation | async-start | bytes 6422528 | tf_op jit(solution)/shard_map/all_to_all | solution.py:787
  33.3 0.0 copy-start
  33.4 1.2 %copy-done = f32[512,512]{1,0:T(8,128)S(1)} copy-done((f32[512,512]{1,0:T(8,128)S(1)}, f32[512,512]{1,0:T(8,128)}, u32[]{:S(2)}) %copy-start) | copy-done | bytes 1048600
  34.6 1.6 %copy-done.3 = f32[2,512,512]{2,1,0:T(8,128)S(1)} copy-done((f32[2,512,512]{2,1,0:T(8,128)S(1)}, f32[2,512,512]{2,1,0:T(8,128)}, u32[]{:S(2)}) %copy-start.3) | copy-done | bytes 2097176
  36.2 1.9 %prepare.1 = (f32[5,544,128]{2,1,0:T(8,128)S(1)}, f32[2,5,512,128]{3,2,1,0:T(8,128)S(1)}, f32[2,5,8,128]{3,2,1,0:T(8,128)S(1)}, f32[2,5,8,128]{3,2,1,0:T(8,128)S(1)}) custom-call(s32[4]{0:T(128)S(1)} %add_convert_fusion.sides, f32[512,512]{1,0:T(8,128)S(1)} %copy-done, f32[2,512,512]{2,1,0:T(8,128)S(1)} %copy-done.3, ...), custom_call_target="tpu_custom_call" | custom-call | flops 4194304 | bytes 8388608 | tf_op jit(solution)/shard_map/prepare/pallas_call | solution.py:522
  38.1 1.5 %copy-done.9 = f32[2,5,512,128]{3,2,1,0:T(8,128)} copy-done((f32[2,5,512,128]{3,2,1,0:T(8,128)}, f32[2,5,512,128]{3,2,1,0:T(8,128)S(1)}, u32[]{:S(2)}) %copy-start.9) | copy-done | bytes 2621464
  39.5 1.1 %copy-done.11 = f32[5,544,128]{2,1,0:T(8,128)} copy-done((f32[5,544,128]{2,1,0:T(8,128)}, f32[5,544,128]{2,1,0:T(8,128)S(1)}, u32[]{:S(2)}) %copy-start.11) | copy-done | bytes 1392664
  40.6 33.9 %all-to-all-done = f32[128,49,1,128]{3,2,1,0:T(1,128)S(1)} async-done(((f32[128,49,1,128]{3,2,1,0:T(1,128)}), f32[128,49,1,128]{3,2,1,0:T(1,128)S(1)}, u32[]{:S(2)}, u32[]{:S(2)}) %all-to-all-start) | async-done | bytes 3211296 | tf_op jit(solution)/shard_map/all_to_all | solution.py:787
  74.6 2.8 %place.1 = (f32[2,5,512,128]{3,2,1,0:T(8,128)S(1)}, f32[2,5,8,128]{3,2,1,0:T(8,128)S(1)}, f32[2,5,8,128]{3,2,1,0:T(8,128)S(1)}) custom-call(f32[6272,128]{1,0:T(8,128)S(1)} %bitcast.12, f32[2,5,8,128]{3,2,1,0:T(8,128)S(1)} %get-tuple-element.28.first_momentum, f32[2,5,8,128]{3,2,1,0:T(8,128)S(1)} %get-tuple-element.29.last_momentum), custom_call_target="tpu_custom_call" | custom-call | tf_op jit(solution)/shard_map/place/pallas_call | solution.py:570
  77.4 1.1 %collective-permute-start.4 = (f32[2,5,8,128]{3,2,1,0:T(8,128)S(1)}, f32[2,5,8,128]{3,2,1,0:T(8,128)S(1)}, u32[]{:S(2)}, u32[]{:S(2)}) collective-permute-start(f32[2,5,8,128]{3,2,1,0:T(8,128)S(1)} %get-tuple-element.34), channel_id=1, source_target_pairs={{0,16},{16,32},{32,48},{48,64},{64,80},{80,96},{96,112},{112,0},{1... | collective-permute-start | bytes 122888 | tf_op jit(solution)/shard_map/ppermute | solution.py:783
  78.5 0.0 collective-permute-start.5
  78.5 0.0 copy-done.13
  78.5 1.8 %raise_lake.1 = f32[512,512]{1,0:T(8,128)} custom-call(f32[6272,128]{1,0:T(8,128)S(1)} %bitcast.13, f32[512,512]{1,0:T(8,128)S(1)} %copy-done.13), custom_call_target="tpu_custom_call" | custom-call | flops 629145600 | bytes 6291456 | tf_op jit(solution)/shard_map/raise_lake/pallas_call | solution.py:586
  80.4 0.0 collective-permute-done.4.above
  80.4 1.9 %collective-permute-done.5.below = f32[2,5,8,128]{3,2,1,0:T(8,128)S(1)} collective-permute-done((f32[2,5,8,128]{3,2,1,0:T(8,128)S(1)}, f32[2,5,8,128]{3,2,1,0:T(8,128)S(1)}, u32[]{:S(2)}, u32[]{:S(2)}) %collective-permute-start.5) | collective-permute-done | bytes 40992 | tf_op jit(solution)/shard_map/ppermute | solution.py:783
  82.2 0.0 copy-done.10
  82.2 0.0 copy-done.12
  82.2 6.7 %krylov.1 = (f32[2,5,544,128]{3,2,1,0:T(8,128)S(1)}, f32[2,5,544,128]{3,2,1,0:T(8,128)S(1)}, f32[2,5,544,128]{3,2,1,0:T(8,128)S(1)}, f32[128,128]{1,0:T(8,128)S(1)}) custom-call(s32[4]{0:T(128)S(1)} %add_convert_fusion.sides, f32[2,5,512,128]{3,2,1,0:T(8,128)S(1)} %get-tuple-element.32.flow, f32[2,5,512,128]{3,2,1,0:T(8,128)S(1)} %copy-done.10, ...), custom_call_target="tpu_custom_call" | custom-call | tf_op jit(solution)/shard_map/krylov/pallas_call | solution.py:696
  88.9 16.4 %all_to_all.10 = f32[128,1,128]{2,1,0:T(1,128)S(1)} all-to-all(f32[128,1,128]{2,1,0:T(1,128)S(1)} %bitcast.16), channel_id=1, replica_groups=mesh['gx'=8,'gy'=16] {'gx','gy'}, dimensions={0} | all-to-all | bytes 131072 | tf_op jit(solution)/shard_map/all_to_all | solution.py:787
  105.3 1.6 %finish.1 = f32[2,512,512]{2,1,0:T(8,128)} custom-call(f32[128,128]{1,0:T(8,128)S(1)} %bitcast.15, f32[2,5,544,128]{3,2,1,0:T(8,128)S(1)} %get-tuple-element.38.b, f32[2,5,544,128]{3,2,1,0:T(8,128)S(1)} %get-tuple-element.39.w1, f32[2,5,544,128]{3,2,1,0:T(8,128)S(1)} %get-tuple-element.40.w2), custom_call_target="tpu_custom_call" | custom-call | tf_op jit(solution)/shard_map/finish/pallas_call | solution.py:770
  (10 shorter events, 0.0 us)
Async XLA Ops:
  0.6 1.0 copy-start.4
  1.7 3.9 %copy-start.5 = (f32[256,512]{1,0:T(8,128)S(1)}, f32[256,512]{1,0:T(8,128)}, u32[]{:S(2)}) copy-start(f32[256,512]{1,0:T(8,128)} %h.3) | copy-start | bytes 1572868
  2.8 6.6 %collective-permute-start = (f32[16,512]{1,0:T(8,128)S(1)}, f32[16,512]{1,0:T(8,128)S(1)}, u32[]{:S(2)}, u32[]{:S(2)}) collective-permute-start(f32[16,512]{1,0:T(8,128)S(1)} %get-tuple-element.22), channel_id=1, source_target_pairs={{0,16},{16,32},{32,48},{48,64},{64,80},{80,96},{96,112},{112,0},{1... | collective-permute-start | bytes 98312 | tf_op jit(solution)/shard_map/ppermute | solution.py:783
  5.5 3.9 %collective-permute-start.1 = (f32[16,512]{1,0:T(8,128)S(1)}, f32[16,512]{1,0:T(8,128)S(1)}, u32[]{:S(2)}, u32[]{:S(2)}) collective-permute-start(f32[16,512]{1,0:T(8,128)S(1)} %get-tuple-element.23), channel_id=1, source_target_pairs={{0,112},{16,0},{32,16},{48,32},{64,48},{80,64},{96,80},{112,96},{1... | collective-permute-start | bytes 98312 | tf_op jit(solution)/shard_map/ppermute | solution.py:783
  5.6 10.7 %copy-start.1 = (f32[2,256,512]{2,1,0:T(8,128)S(1)}, f32[2,256,512]{2,1,0:T(8,128)}, u32[]{:S(2)}) copy-start(f32[2,256,512]{2,1,0:T(8,128)} %m.3) | copy-start | bytes 3145732
  5.6 10.7 %copy-start.2 = (f32[2,256,512]{2,1,0:T(8,128)S(1)}, f32[2,256,512]{2,1,0:T(8,128)}, u32[]{:S(2)}) copy-start(f32[2,256,512]{2,1,0:T(8,128)} %b.3) | copy-start | bytes 3145732
  5.6 10.7 %copy-start.6 = (f32[256,512]{1,0:T(8,128)S(1)}, f32[256,512]{1,0:T(8,128)}, u32[]{:S(2)}) copy-start(f32[256,512]{1,0:T(8,128)} %f.3) | copy-start | bytes 1572868
  5.6 10.6 %copy-start.7 = (s32[256,512]{1,0:T(8,128)S(1)}, s32[256,512]{1,0:T(8,128)}, u32[]{:S(2)}) copy-start(s32[256,512]{1,0:T(8,128)} %a.3) | copy-start | bytes 1572868
  10.1 10.7 %collective-permute-start.2 = (f32[8,2176]{1,0:T(8,128)S(1)}, f32[8,2176]{1,0:T(8,128)S(1)}, u32[]{:S(2)}, u32[]{:S(2)}) collective-permute-start(f32[8,2176]{1,0:T(8,128)S(1)} %get-tuple-element.24.to_right), channel_id=1, source_target_pairs={{0,1},{1,2},{2,3},{3,4},{4,5},{5,6},{6,7},{7,8},{8,9},{9,10},{10,1... | collective-permute-start | bytes 208904 | tf_op jit(solution)/shard_map/ppermute | solution.py:783
  11.4 9.4 %copy-start.14 = (s32[1,1,256,1]{2,3,1,0:T(1,128)S(1)}, s32[1,1,256,1]{2,3,1,0:T(1,128)}, u32[]{:S(2)}) copy-start(s32[1,1,256,1]{2,3,1,0:T(1,128)} %param.15) | copy-start | bytes 3076
  11.4 9.4 %copy-start.15 = (s32[1,1,256]{2,1,0:T(1,128)S(1)}, s32[1,1,256]{2,1,0:T(1,128)}, u32[]{:S(2)}) copy-start(s32[1,1,256]{2,1,0:T(1,128)} %param.16) | copy-start | bytes 3076
  11.4 9.4 %collective-permute-start.3 = (f32[8,2176]{1,0:T(8,128)S(1)}, f32[8,2176]{1,0:T(8,128)S(1)}, u32[]{:S(2)}, u32[]{:S(2)}) collective-permute-start(f32[8,2176]{1,0:T(8,128)S(1)} %get-tuple-element.25.to_left), channel_id=1, source_target_pairs={{0,15},{1,0},{2,1},{3,2},{4,3},{5,4},{6,5},{7,6},{8,7},{9,8},{10,9... | collective-permute-start | bytes 208904 | tf_op jit(solution)/shard_map/ppermute | solution.py:783
  24.2 1.6 %copy-start.8 = (f32[6272,128]{1,0:T(8,128)}, f32[6272,128]{1,0:T(8,128)S(1)}, u32[]{:S(2)}) copy-start(f32[6272,128]{1,0:T(8,128)S(1)} %get-tuple-element.27) | copy-start | bytes 9633796
  25.9 48.7 %all-to-all-start = ((f32[128,49,1,128]{3,2,1,0:T(1,128)}), f32[128,49,1,128]{3,2,1,0:T(1,128)S(1)}, u32[]{:S(2)}, u32[]{:S(2)}) async-start(f32[128,49,1,128]{3,2,1,0:T(1,128)} %bitcast.14), calls=%async_computation | async-start | bytes 6422528 | tf_op jit(solution)/shard_map/all_to_all | solution.py:787
  33.3 1.2 %copy-start = (f32[512,512]{1,0:T(8,128)S(1)}, f32[512,512]{1,0:T(8,128)}, u32[]{:S(2)}) copy-start(f32[512,512]{1,0:T(8,128)} %d.5) | copy-start | bytes 3145732
  34.6 1.6 %copy-start.3 = (f32[2,512,512]{2,1,0:T(8,128)S(1)}, f32[2,512,512]{2,1,0:T(8,128)}, u32[]{:S(2)}) copy-start(f32[2,512,512]{2,1,0:T(8,128)} %lm.1) | copy-start | bytes 6291460
  38.1 1.5 %copy-start.9 = (f32[2,5,512,128]{3,2,1,0:T(8,128)}, f32[2,5,512,128]{3,2,1,0:T(8,128)S(1)}, u32[]{:S(2)}) copy-start(f32[2,5,512,128]{3,2,1,0:T(8,128)S(1)} %get-tuple-element.33.momentum) | copy-start | bytes 7864324
  39.5 1.1 %copy-start.11 = (f32[5,544,128]{2,1,0:T(8,128)}, f32[5,544,128]{2,1,0:T(8,128)S(1)}, u32[]{:S(2)}) copy-start(f32[5,544,128]{2,1,0:T(8,128)S(1)} %get-tuple-element.36.coef) | copy-start | bytes 4177924
  74.6 3.9 %copy-start.13 = (f32[512,512]{1,0:T(8,128)S(1)}, f32[512,512]{1,0:T(8,128)}, u32[]{:S(2)}) copy-start(f32[512,512]{1,0:T(8,128)} %height.1) | copy-start | bytes 3145732
  77.4 3.0 %collective-permute-start.4 = (f32[2,5,8,128]{3,2,1,0:T(8,128)S(1)}, f32[2,5,8,128]{3,2,1,0:T(8,128)S(1)}, u32[]{:S(2)}, u32[]{:S(2)}) collective-permute-start(f32[2,5,8,128]{3,2,1,0:T(8,128)S(1)} %get-tuple-element.34), channel_id=1, source_target_pairs={{0,16},{16,32},{32,48},{48,64},{64,80},{80,96},{96,112},{112,0},{1... | collective-permute-start | bytes 122888 | tf_op jit(solution)/shard_map/ppermute | solution.py:783
  78.5 3.7 %copy-start.10 = (f32[2,5,512,128]{3,2,1,0:T(8,128)S(1)}, f32[2,5,512,128]{3,2,1,0:T(8,128)}, u32[]{:S(2)}) copy-start(f32[2,5,512,128]{3,2,1,0:T(8,128)} %copy-done.9) | copy-start | bytes 7864324
  78.5 3.7 %copy-start.12 = (f32[5,544,128]{2,1,0:T(8,128)S(1)}, f32[5,544,128]{2,1,0:T(8,128)}, u32[]{:S(2)}) copy-start(f32[5,544,128]{2,1,0:T(8,128)} %copy-done.11) | copy-start | bytes 4177924
  78.5 3.7 %collective-permute-start.5 = (f32[2,5,8,128]{3,2,1,0:T(8,128)S(1)}, f32[2,5,8,128]{3,2,1,0:T(8,128)S(1)}, u32[]{:S(2)}, u32[]{:S(2)}) collective-permute-start(f32[2,5,8,128]{3,2,1,0:T(8,128)S(1)} %get-tuple-element.35), channel_id=1, source_target_pairs={{0,112},{16,0},{32,16},{48,32},{64,48},{80,64},{96,80},{112,96},{1... | collective-permute-start | bytes 122888 | tf_op jit(solution)/shard_map/ppermute | solution.py:783

commit v5 on v4

--- a/solution.py
+++ b/solution.py
@@ -19,16 +19,15 @@
 WIDE = C + 128
 TOP = 16
 SROWS = R + 2 * TOP
-CHUNK = 32
+CHUNK = 64
 LTOP = 16
 LROWS = L + 2 * LTOP
-LCHUNK = 64
+LCHUNK = 256
 LSUB = 16
 MIB = 1 << 20
 
 
 HBM = pl.BlockSpec(memory_space=pltpu.HBM)
-SMEM = pl.BlockSpec(memory_space=pltpu.SMEM)
 VMEM = pl.BlockSpec(memory_space=pltpu.VMEM)
 
 
@@ -37,7 +36,7 @@
 
 
 def present(sides):
-    return tuple(sides[i].astype(F32) for i in range(4))
+    return tuple(sides[i : i + 1, :] for i in range(4))
 
 
 def lanes(shape):
@@ -93,8 +92,9 @@
 
 
 GROUP = R + 128
-LAKE = 4 * GROUP
-WIDTH = LAKE + L + 128
+WIDTH = 4 * GROUP
+LAKE_WIDTH = L + 128
+LAKE_CHANNELS = ((0, 2), (2, 3), (5, 3))
 
 
 def put(acc, lane, first, last, base, wide):
@@ -104,9 +104,9 @@
     return jnp.where((lane >= 64 + base) & (lane < 64 + base + wide), turned, acc)
 
 
-def edge_columns_kernel(h, m, b, f, a, d, l, both, hs, ms, bs, fs, as_, ds, ls, mat, sems):
+def edge_columns_kernel(h, m, b, f, a, both, hs, ms, bs, fs, as_, mat, sems):
     copies = []
-    pairs = ((h, hs), (m, ms), (b, bs), (f, fs), (a, as_), (d, ds), (l, ls))
+    pairs = ((h, hs), (m, ms), (b, bs), (f, fs), (a, as_))
     for q, (src, dst) in enumerate(pairs):
         for side, lane in enumerate((0, C - 128)):
             at = (slice(None),) * (len(src.shape) - 1) + (pl.ds(lane, 128),)
@@ -122,47 +122,33 @@
         lambda e, s: fs[e, s, :],
         lambda e, s: as_[e, s, :].astype(F32),
     )
-    lake = (
-        (lambda e, s: ds[e, s, :], 32, 2),
-        (lambda e, s: ls[e, 0, s, :], 34, 3),
-        (lambda e, s: ls[e, 1, s, :], 37, 3),
-    )
     step = 64
-    mat[L:, :] = jnp.zeros((128, 128), F32)
+    mat[R:, :] = jnp.zeros((128, 128), F32)
     for c in copies:
         c.wait()
 
-    def body(slope_too):
-        def run(t, _):
-            s = pl.ds(pl.multiple_of(t * step, step), step)
-            lane = lanes((step, 128))
-            acc = jnp.zeros((step, 128), F32)
-            if slope_too:
-                for i, read in enumerate(slope):
-                    acc = put(acc, lane, read(0, s), read(1, s), 4 * i, 4)
-            for read, base, wide in lake:
-                acc = put(acc, lane, read(0, s), read(1, s), base, wide)
-            mat[s, :] = acc
-            return 0
-
-        return run
-
-    lax.fori_loop(0, R // step, body(True), 0)
-    lax.fori_loop(R // step, L // step, body(False), 0)
-    for t in range(5):
+    def body(t, _):
+        s = pl.ds(pl.multiple_of(t * step, step), step)
+        lane = lanes((step, 128))
+        acc = jnp.zeros((step, 128), F32)
+        for i, read in enumerate(slope):
+            acc = put(acc, lane, read(0, s), read(1, s), 4 * i, 4)
+        mat[s, :] = acc
+        return 0
+
+    lax.fori_loop(0, R // step, body, 0)
+    for t in range(3):
         turned = mat[128 * t : 128 * t + 128, :].T
         for e, row in ((0, 0), (1, 64)):
-            if t < 3:
-                for g in range(4):
-                    at = GROUP * g + 128 * t
-                    both[e, :, at : at + 128] = turned[row + 8 * g : row + 8 * g + 8, :]
-            both[e, :, LAKE + 128 * t : LAKE + 128 * t + 128] = turned[row + 32 : row + 40, :]
-
-
-def edge_columns(h, mom, bed, fric, act, d, lm):
+            for g in range(4):
+                at = GROUP * g + 128 * t
+                both[e, :, at : at + 128] = turned[row + 8 * g : row + 8 * g + 8, :]
+
+
+def edge_columns(h, mom, bed, fric, act):
     return pl.pallas_call(
         edge_columns_kernel,
-        in_specs=[HBM] * 7,
+        in_specs=[HBM] * 5,
         out_specs=VMEM,
         out_shape=jax.ShapeDtypeStruct((2, 8, WIDTH), F32),
         scratch_shapes=[
@@ -171,43 +157,38 @@
             pltpu.VMEM((2, 2, R, 128), F32),
             pltpu.VMEM((2, R, 128), F32),
             pltpu.VMEM((2, R, 128), jnp.int32),
-            pltpu.VMEM((2, L, 128), F32),
-            pltpu.VMEM((2, 2, L, 128), F32),
-            pltpu.VMEM((WIDE, 128), F32),
-            pltpu.SemaphoreType.DMA((14,)),
+            pltpu.VMEM((GROUP, 128), F32),
+            pltpu.SemaphoreType.DMA((10,)),
         ],
         compiler_params=params(room=7_300_000),
         cost_estimate=pl.CostEstimate(flops=8 * MIB, bytes_accessed=6 * MIB, transcendentals=0),
         name="edge_columns",
-    )(h, mom, bed, fric, act, d, lm)
+    )(h, mom, bed, fric, act)
+
+
+def corner_block(x, first_row, second_row, a, b):
+    row = rows((8, 128))
+
+    def block(where):
+        y = jnp.where(row == first_row, jnp.broadcast_to(x[a : a + 1, where], (8, 128)), 0.0)
+        return y if b is None else jnp.where(row == second_row, jnp.broadcast_to(x[b : b + 1, where], (8, 128)), y)
+
+    return block(slice(0, 128)), block(slice(C - 128, C))
 
 
 def corners_kernel(sides, both, above, below, right, left):
-    lane, row = lanes((8, 128)), rows((8, 128))
-
-    def line(x, r, where):
-        return jnp.broadcast_to(x[r : r + 1, where], (8, 128))
-
-    def end(x, first_row, second_row, a, b):
-        def block(where):
-            y = jnp.where(row == first_row, line(x, a, where), 0.0)
-            return y if b is None else jnp.where(row == second_row, line(x, b, where), y)
-
-        return block(slice(0, 128)), block(slice(C - 128, C))
-
+    lane = lanes((8, 128))
     low, high = jnp.zeros((8, 128), F32), jnp.zeros((8, 128), F32)
-    for i in range(8):
-        if i == 7:
-            a, b, base, wide = 10, 11, 32, 2
-        elif i < 3:
+    for i in range(7):
+        if i < 3:
             a, b, base, wide = 2 * i, 2 * i + 1, 4 * i, 4
         else:
             a, b, base, wide = 3 + i, None, 4 * i, 4
-        low = put(low, lane, *end(below, 0, 1, a, b), base, wide)
+        low = put(low, lane, *corner_block(below, 0, 1, a, b), base, wide)
         if b is None:
-            high = put(high, lane, *end(above, 7, None, a, None), base, wide)
+            high = put(high, lane, *corner_block(above, 7, None, a, None), base, wide)
         else:
-            high = put(high, lane, *end(above, 6, 7, a, b), base, wide)
+            high = put(high, lane, *corner_block(above, 6, 7, a, b), base, wide)
     up, down, _, _ = present(sides)
     turned = jnp.concatenate([down * low, jnp.zeros((112, 128), F32), up * high], axis=0).T
     for e, out, at in ((0, right, 0), (1, left, 64)):
@@ -215,17 +196,53 @@
         for g in range(4):
             s = slice(GROUP * g + R, GROUP * g + R + 128)
             out[:, s] = turned[at + 8 * g : at + 8 * g + 8, :]
-        out[:, LAKE + L :] = turned[at + 32 : at + 40, :]
 
 
 def corners(sides, both, above, below):
     return pl.pallas_call(
         corners_kernel,
-        in_specs=[SMEM] + [VMEM] * 3,
+        in_specs=[VMEM] * 4,
         out_shape=[jax.ShapeDtypeStruct((8, WIDTH), F32)] * 2,
         compiler_params=params(4),
         name="corners",
     )(sides, both, above, below)
+
+
+def lake_columns_kernel(sides, d, l, above, below, right, left, mat):
+    reads = (lambda s, at: d[s, at], lambda s, at: l[0, s, at], lambda s, at: l[1, s, at])
+    ends = (slice(0, 128), slice(C - 128, C))
+    step = 128
+
+    def body(t, _):
+        s = pl.ds(pl.multiple_of(t * step, step), step)
+        lane = lanes((step, 128))
+        acc = jnp.zeros((step, 128), F32)
+        for read, (base, wide) in zip(reads, LAKE_CHANNELS):
+            acc = put(acc, lane, read(s, ends[0]), read(s, ends[1]), base, wide)
+        mat[s, :] = acc
+        return 0
+
+    lax.fori_loop(0, L // step, body, 0)
+    up, down, _, _ = present(sides)
+    lane, zero = lanes((8, 128)), jnp.zeros((8, 128), F32)
+    mat[L:, :] = jnp.zeros((128, 128), F32)
+    mat[L : L + 8, :] = down * put(zero, lane, *corner_block(below, 0, 1, 10, 11), *LAKE_CHANNELS[0])
+    mat[L + 120 :, :] = up * put(zero, lane, *corner_block(above, 6, 7, 10, 11), *LAKE_CHANNELS[0])
+    for t in range(5):
+        turned = mat[128 * t : 128 * t + 128, :].T
+        right[:, 128 * t : 128 * t + 128] = turned[0:8, :]
+        left[:, 128 * t : 128 * t + 128] = turned[64:72, :]
+
+
+def lake_columns(sides, d, lm, above, below):
+    return pl.pallas_call(
+        lake_columns_kernel,
+        out_shape=[jax.ShapeDtypeStruct((8, LAKE_WIDTH), F32)] * 2,
+        scratch_shapes=[pltpu.VMEM((LAKE_WIDTH, 128), F32)],
+        compiler_params=params(16),
+        cost_estimate=pl.CostEstimate(flops=4 * MIB, bytes_accessed=4 * MIB, transcendentals=0),
+        name="lake_columns",
+    )(sides, d, lm, above, below)
 
 
 def split2(x):
@@ -353,7 +370,7 @@
 def slope(sides, h, mom, bed, fric, act, above, below):
     return pl.pallas_call(
         slope_kernel,
-        in_specs=[SMEM] + [VMEM] * 7,
+        in_specs=[VMEM] * 8,
         out_shape=jax.ShapeDtypeStruct((3, R, C), F32),
         scratch_shapes=[pltpu.VMEM((2, 7, 4, 8, 128), F32)] + [pltpu.VMEM((2, 3, 4, SROWS, 128), F32)] * 3,
         compiler_params=params(24),
@@ -379,7 +396,8 @@
 
     ends = []
     _, _, on_left, on_right = present(sides)
-    for e, (before, after, a, b) in enumerate(((from_left, to_left, on_left, 1.0), (to_right, from_right, 1.0, on_right))):
+    for e, (before, after, a, b) in enumerate(((from_left, to_left, on_left, None), (to_right, from_right, None, on_right))):
+        a, b = (1.0 if x is None else jnp.concatenate([x] * (GROUP // 128), axis=1) for x in (a, b))
         for i in range(7):
             r, s = 4 * (i % 2), slice(GROUP * (i // 2), GROUP * (i // 2) + GROUP)
             strip[e, i, 0:4, :] = a * before[r : r + 4, s]
@@ -459,7 +477,7 @@
 def pack(sides, fields, to_right, to_left, from_left, from_right, own, off):
     return pl.pallas_call(
         pack_kernel,
-        in_specs=[SMEM] + [VMEM] * 7,
+        in_specs=[VMEM] * 8,
         out_specs=[HBM, HBM],
         out_shape=[jax.ShapeDtypeStruct((3, R, C), F32), jax.ShapeDtypeStruct((DEV * UNITS, 128), F32)],
         scratch_shapes=[
@@ -468,66 +486,58 @@
             pltpu.VMEM((DEV * UNITS, 128), F32),
             pltpu.SemaphoreType.DMA((22,)),
         ],
-        compiler_params=params(room=12_000_000),
+        compiler_params=params(room=10_000_000),
         name="pack",
     )(sides, fields, to_right, to_left, from_left, from_right, own, off)
 
 
-def prepare_kernel(sides, d, lm, above, below, from_left, from_right, coef, momentum, first, last, turn):
-    _, _, on_left, on_right = present(sides)
-    gap = jnp.zeros((56, 128), F32)
-    for t in range(5):
-        s = slice(LAKE + 128 * t, LAKE + 128 * t + 128)
-        both = jnp.concatenate([from_left[:, s], gap, from_right[:, s], gap], axis=0)
-        turn[128 * t : 128 * t + 128, :] = both.T
-
-    def halo(w, lane, i):
-        wide, at = (2, 0) if i == 0 else (3, 3 * i - 1)
-        left = pltpu.roll(w, 128 - wide - at, 1)
-        right = pltpu.roll(w, 64 - at, 1)
-        return jnp.where(lane >= 128 - wide, on_left * left, jnp.where(lane < wide, on_right * right, 0.0))
-
+def prepare_kernel(d, lm, above, below, coef, momentum, first, last):
     step = 64
 
     def body(t, _):
         r = pl.multiple_of(t * step, step)
         s = pl.ds(r, step)
-        w = turn[s, :]
-        lane = lanes((step, 128))
         to = pl.ds(pl.multiple_of(LTOP + r, 8), step)
         for j in range(4):
-            coef[j, to, :] = 2.0 * d[s, 128 * j : 128 * j + 128] - 2.0
-        coef[4, to, :] = 2.0 * halo(w, lane, 0) - 2.0
-        for i in range(2):
-            for j in range(4):
-                momentum[i, j, s, :] = lm[i, s, 128 * j : 128 * j + 128]
-            momentum[i, 4, s, :] = halo(w, lane, i + 1)
+            at = slice(128 * j, 128 * j + 128)
+            coef[j, to, :] = 2.0 * d[s, at] - 2.0
+            for i in range(2):
+                momentum[i, j, s, :] = lm[i, s, at]
         return 0
 
     lax.fori_loop(0, L // step, body, 0)
-    for j in range(5):
+    for j in range(4):
         coef[j, 0:LTOP, :] = jnp.zeros((LTOP, 128), F32)
         coef[j, LTOP + L :, :] = jnp.zeros((LTOP, 128), F32)
-        if j < 4:
-            s = slice(128 * j, 128 * j + 128)
-            coef[j, LTOP - 2 : LTOP, :] = 2.0 * above[10:12, s] - 2.0
-            coef[j, LTOP + L : LTOP + L + 2, :] = 2.0 * below[10:12, s] - 2.0
-    coef[4, LTOP - 8 : LTOP, :] = 2.0 * halo(turn[L + 120 :, :], lanes((8, 128)), 0) - 2.0
-    coef[4, LTOP + L : LTOP + L + 8, :] = 2.0 * halo(turn[L : L + 8, :], lanes((8, 128)), 0) - 2.0
+        s = slice(128 * j, 128 * j + 128)
+        coef[j, LTOP - 2 : LTOP, :] = 2.0 * above[10:12, s] - 2.0
+        coef[j, LTOP + L : LTOP + L + 2, :] = 2.0 * below[10:12, s] - 2.0
     first[...] = momentum[:, :, 0:8, :]
     last[...] = momentum[:, :, L - 8 : L, :]
 
 
-def prepare(sides, d, lm, above, below, from_left, from_right):
+def prepare(d, lm, above, below):
     return pl.pallas_call(
         prepare_kernel,
-        in_specs=[SMEM] + [VMEM] * 6,
-        out_shape=[jax.ShapeDtypeStruct(x, F32) for x in ((5, LROWS, 128), (2, 5, L, 128), (2, 5, 8, 128), (2, 5, 8, 128))],
-        scratch_shapes=[pltpu.VMEM((WIDE, 128), F32)],
+        out_shape=[jax.ShapeDtypeStruct(x, F32) for x in ((4, LROWS, 128), (2, 4, L, 128), (2, 4, 8, 128), (2, 4, 8, 128))],
         compiler_params=params(16),
         cost_estimate=pl.CostEstimate(flops=4 * MIB, bytes_accessed=8 * MIB, transcendentals=0),
         name="prepare",
-    )(sides, d, lm, above, below, from_left, from_right)
+    )(d, lm, above, below)
+
+
+def lake_turn(from_left, from_right, t):
+    gap, s = jnp.zeros((56, 128), F32), slice(128 * t, 128 * t + 128)
+    return jnp.concatenate([from_left[:, s], gap, from_right[:, s], gap], axis=0).T
+
+
+def lake_halo(sides, w, i):
+    _, _, on_left, on_right = present(sides)
+    at, wide = LAKE_CHANNELS[i]
+    lane = lanes(w.shape)
+    left = pltpu.roll(w, 128 - wide - at, 1)
+    right = pltpu.roll(w, 64 - at, 1)
+    return jnp.where(lane >= 128 - wide, on_left * left, jnp.where(lane < wide, on_right * right, 0.0))
 
 
 def one_hot(hot, tags, first):
@@ -546,7 +556,7 @@
                 term[t, DEV * k : DEV * k + DEV, 128 * j : 128 * j + 128] = parts[t]
 
 
-def place_kernel(recv, first_momentum, last_momentum, flow, first, last, hot, term):
+def place_kernel(sides, recv, first_momentum, last_momentum, from_left, from_right, flow, first, last, hot, term):
     marks = recv[pl.ds(TAG, DEV, stride=UNITS), :]
     one_hot(hot, marks.T, (0, 56, 60))
     own = hot[:, 0 : CAP * DEV]
@@ -562,18 +572,23 @@
             left.append(jnp.where(lane >= 125, pltpu.roll(marks, 117 - 6 * k - 3 * c, 1), 0.0))
             right.append(jnp.where(lane < 3, pltpu.roll(marks, 96 - 6 * k - 3 * c, 1), 0.0))
         flow[c, 4, :, :] = pick(side, split2(jnp.concatenate(left + right, axis=0)))
-    first[...] = first_momentum[...] + flow[:, :, 0:8, :]
-    last[...] = last_momentum[...] + flow[:, :, L - 8 : L, :]
-
-
-def place(recv, first_momentum, last_momentum):
+    first[:, 0:4, :, :] = first_momentum[...] + flow[:, 0:4, 0:8, :]
+    last[:, 0:4, :, :] = last_momentum[...] + flow[:, 0:4, L - 8 : L, :]
+    top = lake_turn(from_left, from_right, 0)[0:8, :]
+    bottom = lake_turn(from_left, from_right, L // 128 - 1)[120:128, :]
+    for c in range(2):
+        first[c, 4, :, :] = lake_halo(sides, top, c + 1) + flow[c, 4, 0:8, :]
+        last[c, 4, :, :] = lake_halo(sides, bottom, c + 1) + flow[c, 4, L - 8 : L, :]
+
+
+def place(sides, recv, first_momentum, last_momentum, from_left, from_right):
     return pl.pallas_call(
         place_kernel,
         out_shape=[jax.ShapeDtypeStruct((2, 5, n, 128), F32) for n in (L, 8, 8)],
         scratch_shapes=[pltpu.VMEM((L, 3 * CAP * DEV), BF16), pltpu.VMEM((2, CAP * DEV, C), BF16)],
         compiler_params=params(20),
         name="place",
-    )(recv, first_momentum, last_momentum)
+    )(sides, recv, first_momentum, last_momentum, from_left, from_right)
 
 
 def raise_kernel(recv, height, new_height, hot, term):
@@ -595,7 +610,7 @@
     )(recv, height)
 
 
-def krylov_kernel(sides, flow, momentum, above, below, coef, b, w1, w2, sums):
+def krylov_kernel(sides, flow, momentum, above, below, coef, from_left, from_right, b, w1, w2, sums, turn, side_coef):
     for x in (b, w1, w2):
         x[:, :, 0 : LTOP - 8, :] = jnp.zeros((2, 5, LTOP - 8, 128), F32)
         x[:, :, LTOP + L + 8 :, :] = jnp.zeros((2, 5, LTOP - 8, 128), F32)
@@ -606,13 +621,19 @@
 
     def total_side(t, _):
         r = pl.multiple_of(t * 64, 64)
+        s, to = pl.ds(r, 64), pl.ds(pl.multiple_of(LTOP + r, 8), 64)
+        w = turn[s, :]
+        side_coef[to, :] = 2.0 * lake_halo(sides, w, 0) - 2.0
         for i in range(2):
-            for j in range(5):
-                b[i, j, pl.ds(pl.multiple_of(LTOP + r, 8), 64), :] = (
-                    flow[i, j, pl.ds(r, 64), :] + momentum[i, j, pl.ds(r, 64), :]
-                )
+            for j in range(4):
+                b[i, j, to, :] = flow[i, j, s, :] + momentum[i, j, s, :]
+            b[i, 4, to, :] = flow[i, 4, s, :] + lake_halo(sides, w, i + 1)
         return 0
 
+    for t in range(5):
+        turn[128 * t : 128 * t + 128, :] = lake_turn(from_left, from_right, t)
+    side_coef[LTOP - 8 : LTOP, :] = 2.0 * lake_halo(sides, turn[L + 120 :, :], 0) - 2.0
+    side_coef[LTOP + L : LTOP + L + 8, :] = 2.0 * lake_halo(sides, turn[L : L + 8, :], 0) - 2.0
     lax.fori_loop(0, L // 64, total_side, 0)
 
     def image(x, i, r, n):
@@ -621,7 +642,8 @@
         w = []
         for j in range(5):
             around = (x[i, j, pl.ds(r - 1, n), :] + x[i, j, pl.ds(r + 1, n), :]) + (west[j] + east[j])
-            w.append(coef[j, pl.ds(r, n), :] * v[j] - around)
+            diagonal = coef[j, pl.ds(r, n), :] if j < 4 else side_coef[pl.ds(r, n), :]
+            w.append(diagonal * v[j] - around)
         w[4] = w[4] * edge
         return v, w
 
@@ -692,15 +714,16 @@
     sums[...] = jnp.broadcast_to(line, (DEV, 128))
 
 
-def krylov(sides, flow, momentum, above, below, coef):
+def krylov(sides, flow, momentum, above, below, coef, from_left, from_right):
     return pl.pallas_call(
         krylov_kernel,
-        in_specs=[pl.BlockSpec(memory_space=pltpu.SMEM)] + [VMEM] * 5,
+        in_specs=[VMEM] * 8,
         out_specs=[VMEM] * 4,
         out_shape=[jax.ShapeDtypeStruct((2, 5, LROWS, 128), F32)] * 3 + [jax.ShapeDtypeStruct((DEV, 128), F32)],
+        scratch_shapes=[pltpu.VMEM((LAKE_WIDTH, 128), F32), pltpu.VMEM((LROWS, 128), F32)],
         compiler_params=params(24),
         name="krylov",
-    )(sides, flow, momentum, above, below, coef)
+    )(sides, flow, momentum, above, below, coef, from_left, from_right)
 
 
 def steps(nu):
@@ -789,22 +812,27 @@
 
 def per_device(h, mom, bed, fric, act, owners, offsets, height, lm, d):
     i, j = lax.axis_index("gx"), lax.axis_index("gy")
-    sides = jnp.stack([i > 0, i < NX - 1, j > 0, j < NY - 1]).astype(jnp.int32)
+    row = rows((8, 128))
+    inside = ((row == 0) & (i > 0)) | ((row == 1) & (i < NX - 1)) | ((row == 2) & (j > 0)) | ((row == 3) & (j < NY - 1))
+    sides = inside.astype(F32)
     up, dn = edge_rows(h, mom, bed, fric, act, d)
     above, below = shift(dn, "gx", 1), shift(up, "gx", -1)
-    columns = edge_columns(h, mom, bed, fric, act, d, lm)
+    columns = edge_columns(h, mom, bed, fric, act)
     to_right, to_left = corners(sides, columns, above, below)
     from_left, from_right = shift(to_right, "gy", 1), shift(to_left, "gy", -1)
     fields = slope(sides, h, mom, bed, fric, act, above, below)
     own, off = owners.reshape(1, R), offsets.reshape(1, R)
     fields, payload = pack(sides, fields, to_right, to_left, from_left, from_right, own, off)
+    payload, d, lm = lax.optimization_barrier((payload, d, lm))
     recv = exchange(payload.reshape(DEV, UNITS, 1, 128)).reshape(DEV * UNITS, 128)
-    coef, momentum, first, last = prepare(sides, d, lm, above, below, from_left, from_right)
-    flow, first, last = place(recv, first, last)
+    to_right, to_left = lake_columns(sides, d, lm, above, below)
+    from_left, from_right = shift(to_right, "gy", 1), shift(to_left, "gy", -1)
+    coef, momentum, first, last = prepare(d, lm, above, below)
+    flow, first, last = place(sides, recv, first, last, from_left, from_right)
     new_height = raise_lake(recv, height)
     b_above, b_below = shift(last, "gx", 1), shift(first, "gx", -1)
     flow, new_height = lax.optimization_barrier((flow, new_height))
-    b, w1, w2, sums = krylov(sides, flow, momentum, b_above, b_below, coef)
+    b, w1, w2, sums = krylov(sides, flow, momentum, b_above, b_below, coef, from_left, from_right)
     sums = exchange(sums.reshape(DEV, 1, 128)).reshape(DEV, 128)
     return fields, new_height, finish(sums, b, w1, w2)
 

time: 107 us -> 103 us (0.963)
  starting transfers between devices: 17.3 us -> 22.8 us
  Pallas kernels: 28.5 us -> 23.8 us
  waiting for transfers between devices: 35.8 us -> 32.4 us
  local copies, waits for them, and re-layouts: 8.1 us -> 6.3 us
    all_to_all x1, waiting for transfers between devices: 33.9 us -> 2.11 us  [exchange(): return lax.all_to_all(x, AXES, split_axis=0, concat_axis=0, tiled=True)]
    ppermute x6 -> x8, waiting for transfers between devices: 1.88 us -> 30.3 us  [shift(): return lax.ppermute(x, axis, [(i, (i + by) % n) for i in range(n)])]
    ppermute x6 -> x8, starting transfers between devices: 9.9 us -> 15.5 us  [shift(): return lax.ppermute(x, axis, [(i, (i + by) % n) for i in range(n)])]
    pallas_call x6 -> x7, Pallas kernels: 21 us -> 16.2 us  [the longest x1 5.99 us: krylov(): pl.pallas_call(krylov_kernel, in_specs=[VMEM] * 8, out_specs=[VMEM] * 4,...]
    unnamed x32, local copies, waits for them, and re-layouts: 8.1 us -> 6.23 us
  transfers between devices with their start and end apart: 7 -> 9, of which waited for: 2 -> 4; matrix products, arithmetic and copies ran while one was open for 0% -> 0% of each run, Pallas kernels for 11% -> 9%
where the time goes in v5:
time: 103 us
  waiting for transfers between devices  32.4 us (31%)
  Pallas kernels  23.8 us (23%)
  starting transfers between devices  22.8 us (22%)
  blocking collectives  16.4 us (16%)
  local copies, waits for them, and re-layouts  6.3 us (6%)
    ppermute x8, waiting for transfers between devices, shift(): return lax.ppermute(x, axis, [(i, (i + by) % n) for i in range(n)])  30.3 us
    all_to_all x1, blocking collectives, exchange(): return lax.all_to_all(x, AXES, split_axis=0, concat_axis=0, tiled=True)  16.4 us
    ppermute x8, starting transfers between devices, shift(): return lax.ppermute(x, axis, [(i, (i + by) % n) for i in range(n)])  15.5 us
    all_to_all x1, starting transfers between devices, exchange(): return lax.all_to_all(x, AXES, split_axis=0, concat_axis=0, tiled=True)  7.36 us
    unnamed x32, local copies, waits for them, and re-layouts  6.23 us
    pallas_call x1, Pallas kernels, krylov(): pl.pallas_call(krylov_kernel, in_specs=[VMEM] * 8, out_specs=[VMEM] * 4,...  5.99 us
    pallas_call x1, Pallas kernels, slope(): pl.pallas_call(slope_kernel, in_specs=[VMEM] * 8, out_shape=jax.ShapeDtyp...  3.55 us
    pallas_call x1, Pallas kernels, pack(): pl.pallas_call(pack_kernel, in_specs=[VMEM] * 8, out_specs=[HBM, HBM], ou...  3.08 us
  transfers between devices with their start and end apart: 9, of which 4 were waited for; matrix products, arithmetic and copies ran while one was open for 0% of the time, Pallas kernels for 9%

profile of v5, /device:TPU:1, one launch (start us, length us, event | category | flops | bytes accessed | tf_op | source)
XLA Modules:
  0.0 102.5 jit_solution(4789103057213648184)
XLA Ops:
  0.6 0.0 copy-start.5
  0.6 1.0 %copy-done.5 = f32[256,512]{1,0:T(8,128)S(1)} copy-done((f32[256,512]{1,0:T(8,128)S(1)}, f32[256,512]{1,0:T(8,128)}, u32[]{:S(2)}) %copy-start.5) | copy-done | bytes 524312
  1.7 1.1 %edge_rows.1 = (f32[16,512]{1,0:T(8,128)S(1)}, f32[16,512]{1,0:T(8,128)S(1)}) custom-call(f32[256,512]{1,0:T(8,128)S(1)} %copy-done.5, f32[2,256,512]{2,1,0:T(8,128)} %m.3, f32[2,256,512]{2,1,0:T(8,128)} %b.3, f32[256,512]{1,0:T(8,128)} %f.3, s32[256,512]{1,0:T(8,128)} %a.3, f32[512,512]{1,0:T(8,128)} %d.3), custom_call_target="tpu_custom_call" | custom-call | tf_op jit(solution)/shard_map/edge_rows/pallas_call | solution.py:75
  2.8 0.0 copy-start.1
  2.8 0.0 copy-start.2
  2.8 0.0 copy-start.7
  2.8 2.7 %collective-permute-start = (f32[16,512]{1,0:T(8,128)S(1)}, f32[16,512]{1,0:T(8,128)S(1)}, u32[]{:S(2)}, u32[]{:S(2)}) collective-permute-start(f32[16,512]{1,0:T(8,128)S(1)} %get-tuple-element.27), channel_id=1, source_target_pairs={{0,16},{16,32},{32,48},{48,64},{64,80},{80,96},{96,112},{112,0},{1... | collective-permute-start | bytes 98312 | tf_op jit(solution)/shard_map/ppermute | solution.py:806
  5.5 0.0 collective-permute-start.1
  5.5 0.0 copy-done.6
  5.5 2.4 %edge_columns.1.both = f32[2,8,1536]{2,1,0:T(8,128)S(1)} custom-call(f32[256,512]{1,0:T(8,128)S(1)} %copy-done.6, f32[2,256,512]{2,1,0:T(8,128)} %m.3, f32[2,256,512]{2,1,0:T(8,128)} %b.3, f32[256,512]{1,0:T(8,128)} %f.3, s32[256,512]{1,0:T(8,128)} %a.3), custom_call_target="tpu_custom_call" | custom-call | flops 8388608 | bytes 6291456 | tf_op jit(solution)/shard_map/edge_columns/pallas_call | solution.py:149
  7.9 0.0 collective-permute-done.above
  8.0 0.9 collective-permute-done.1.below
  8.8 0.1 iota.16.sides
  8.9 0.2 corners.1
  9.1 1.3 %collective-permute-start.2 = (f32[8,1536]{1,0:T(8,128)S(1)}, f32[8,1536]{1,0:T(8,128)S(1)}, u32[]{:S(2)}, u32[]{:S(2)}) collective-permute-start(f32[8,1536]{1,0:T(8,128)S(1)} %get-tuple-element.29.to_right), channel_id=1, source_target_pairs={{0,1},{1,2},{2,3},{3,4},{4,5},{5,6},{6,7},{7,8},{8,9},{9,10},{10,1... | collective-permute-start | bytes 147464 | tf_op jit(solution)/shard_map/ppermute | solution.py:806
  10.4 4.8 %collective-permute-start.3 = (f32[8,1536]{1,0:T(8,128)S(1)}, f32[8,1536]{1,0:T(8,128)S(1)}, u32[]{:S(2)}, u32[]{:S(2)}) collective-permute-start(f32[8,1536]{1,0:T(8,128)S(1)} %get-tuple-element.30.to_left), channel_id=1, source_target_pairs={{0,15},{1,0},{2,1},{3,2},{4,3},{5,4},{6,5},{7,6},{8,7},{9,8},{10,9... | collective-permute-start | bytes 147464 | tf_op jit(solution)/shard_map/ppermute | solution.py:806
  15.2 0.0 copy-done.1
  15.2 0.0 copy-done.2
  15.2 0.0 copy-done.7
  15.2 0.0 copy-done.8
  15.2 3.5 %slope.1.fields = f32[3,256,512]{2,1,0:T(8,128)S(1)} custom-call(f32[8,128]{1,0:T(8,128)S(1)} %iota.16.sides, f32[256,512]{1,0:T(8,128)S(1)} %copy-done.6, f32[2,256,512]{2,1,0:T(8,128)S(1)} %copy-done.1, f32[2,256,512]{2,1,0:T(8,128)S(1)} %copy-done.2, f32[256,512]{1,0:T(8,128)S(1)} %copy-done.7, s32[256,512]{1,0:T(8,128)S(1)} %copy-done.8, ...), custom_call_target="tpu_custom_call" | custom-call | flops 33554432 | bytes 6291456 | tf_op jit(solution)/shard_map/slope/pallas_call | solution.py:371
  18.8 0.0 collective-permute-done.2.from_left
  18.8 0.0 collective-permute-done.3.from_right
  18.8 0.0 copy-done.14
  18.8 3.1 %pack.1 = (f32[3,256,512]{2,1,0:T(8,128)}, f32[6272,128]{1,0:T(8,128)}) custom-call(f32[8,128]{1,0:T(8,128)S(1)} %iota.16.sides, f32[3,256,512]{2,1,0:T(8,128)S(1)} %slope.1.fields, f32[8,1536]{1,0:T(8,128)S(1)} %get-tuple-element.29.to_right, f32[8,1536]{1,0:T(8,128)S(1)} %get-tuple-element.30.to_left, f32[8,1536]{1,0:T(8,128)S(1)} %collective-permute-done.2.from_left, ...), custom_call_target="tpu_custom_call" | custom-call | tf_op jit(solution)/shard_map/pack/pallas_call | solution.py:478
  21.9 7.4 %all-to-all-start = ((f32[128,49,1,128]{3,2,1,0:T(1,128)}), f32[128,49,1,128]{3,2,1,0:T(1,128)S(1)}, u32[]{:S(2)}, u32[]{:S(2)}) async-start(f32[128,49,1,128]{3,2,1,0:T(1,128)} %bitcast.14), calls=%async_computation | async-start | bytes 6422528 | tf_op jit(solution)/shard_map/all_to_all | solution.py:810
  29.3 0.0 copy-start
  29.3 1.2 %copy-done = f32[512,512]{1,0:T(8,128)S(1)} copy-done((f32[512,512]{1,0:T(8,128)S(1)}, f32[512,512]{1,0:T(8,128)}, u32[]{:S(2)}) %copy-start) | copy-done | bytes 1048600
  30.5 1.6 %copy-done.3 = f32[2,512,512]{2,1,0:T(8,128)S(1)} copy-done((f32[2,512,512]{2,1,0:T(8,128)S(1)}, f32[2,512,512]{2,1,0:T(8,128)}, u32[]{:S(2)}) %copy-start.3) | copy-done | bytes 2097176
  32.1 0.8 lake_columns.1
  32.9 1.4 %collective-permute-start.4 = (f32[8,640]{1,0:T(8,128)S(1)}, f32[8,640]{1,0:T(8,128)S(1)}, u32[]{:S(2)}, u32[]{:S(2)}) collective-permute-start(f32[8,640]{1,0:T(8,128)S(1)} %get-tuple-element.38), channel_id=1, source_target_pairs={{0,1},{1,2},{2,3},{3,4},{4,5},{5,6},{6,7},{7,8},{8,9},{9,10},{10,1... | collective-permute-start | bytes 61448 | tf_op jit(solution)/shard_map/ppermute | solution.py:806
  34.3 4.1 %collective-permute-start.5 = (f32[8,640]{1,0:T(8,128)S(1)}, f32[8,640]{1,0:T(8,128)S(1)}, u32[]{:S(2)}, u32[]{:S(2)}) collective-permute-start(f32[8,640]{1,0:T(8,128)S(1)} %get-tuple-element.39), channel_id=1, source_target_pairs={{0,15},{1,0},{2,1},{3,2},{4,3},{5,4},{6,5},{7,6},{8,7},{9,8},{10,9... | collective-permute-start | bytes 61448 | tf_op jit(solution)/shard_map/ppermute | solution.py:806
  38.5 0.3 prepare.1
  38.7 0.0 copy-start.9
  38.7 1.3 %copy-done.9 = f32[2,4,512,128]{3,2,1,0:T(8,128)} copy-done((f32[2,4,512,128]{3,2,1,0:T(8,128)}, f32[2,4,512,128]{3,2,1,0:T(8,128)S(1)}, u32[]{:S(2)}) %copy-start.9) | copy-done | bytes 2097176
  40.0 1.0 copy-done.11
  41.1 27.5 %collective-permute-done.4.from_left = f32[8,640]{1,0:T(8,128)S(1)} collective-permute-done((f32[8,640]{1,0:T(8,128)S(1)}, f32[8,640]{1,0:T(8,128)S(1)}, u32[]{:S(2)}, u32[]{:S(2)}) %collective-permute-start.4) | collective-permute-done | bytes 20512 | tf_op jit(solution)/shard_map/ppermute | solution.py:806
  68.6 0.0 collective-permute-done.5.from_right
  68.6 2.1 %all-to-all-done = f32[128,49,1,128]{3,2,1,0:T(1,128)S(1)} async-done(((f32[128,49,1,128]{3,2,1,0:T(1,128)}), f32[128,49,1,128]{3,2,1,0:T(1,128)S(1)}, u32[]{:S(2)}, u32[]{:S(2)}) %all-to-all-start) | async-done | bytes 3211296 | tf_op jit(solution)/shard_map/all_to_all | solution.py:810
  70.7 2.9 %place.1 = (f32[2,5,512,128]{3,2,1,0:T(8,128)S(1)}, f32[2,5,8,128]{3,2,1,0:T(8,128)S(1)}, f32[2,5,8,128]{3,2,1,0:T(8,128)S(1)}) custom-call(f32[8,128]{1,0:T(8,128)S(1)} %iota.16.sides, f32[6272,128]{1,0:T(8,128)S(1)} %bitcast.8, f32[2,4,8,128]{3,2,1,0:T(8,128)S(1)} %get-tuple-element.36.first_momentum, ...), custom_call_target="tpu_custom_call" | custom-call | tf_op jit(solution)/shard_map/place/pallas_call | solution.py:585
  73.6 1.1 %collective-permute-start.6 = (f32[2,5,8,128]{3,2,1,0:T(8,128)S(1)}, f32[2,5,8,128]{3,2,1,0:T(8,128)S(1)}, u32[]{:S(2)}, u32[]{:S(2)}) collective-permute-start(f32[2,5,8,128]{3,2,1,0:T(8,128)S(1)} %get-tuple-element.44), channel_id=1, source_target_pairs={{0,16},{16,32},{32,48},{48,64},{64,80},{80,96},{96,112},{112,0},{1... | collective-permute-start | bytes 122888 | tf_op jit(solution)/shard_map/ppermute | solution.py:806
  74.8 0.0 collective-permute-start.7
  74.8 1.9 %raise_lake.1 = f32[512,512]{1,0:T(8,128)} custom-call(f32[6272,128]{1,0:T(8,128)S(1)} %bitcast.9, f32[512,512]{1,0:T(8,128)S(1)} %copy-done.13), custom_call_target="tpu_custom_call" | custom-call | flops 629145600 | bytes 6291456 | tf_op jit(solution)/shard_map/raise_lake/pallas_call | solution.py:601
  76.6 0.0 collective-permute-done.6.above
  76.6 1.8 %collective-permute-done.7.below = f32[2,5,8,128]{3,2,1,0:T(8,128)S(1)} collective-permute-done((f32[2,5,8,128]{3,2,1,0:T(8,128)S(1)}, f32[2,5,8,128]{3,2,1,0:T(8,128)S(1)}, u32[]{:S(2)}, u32[]{:S(2)}) %collective-permute-start.7) | collective-permute-done | bytes 40992 | tf_op jit(solution)/shard_map/ppermute | solution.py:806
  78.5 6.0 %krylov.1 = (f32[2,5,544,128]{3,2,1,0:T(8,128)S(1)}, f32[2,5,544,128]{3,2,1,0:T(8,128)S(1)}, f32[2,5,544,128]{3,2,1,0:T(8,128)S(1)}, f32[128,128]{1,0:T(8,128)S(1)}) custom-call(f32[8,128]{1,0:T(8,128)S(1)} %iota.16.sides, f32[2,5,512,128]{3,2,1,0:T(8,128)S(1)} %get-tuple-element.42.flow, f32[2,4,512,128]{3,2,1,0:T(8,128)S(1)} %copy-done.10, ...), custom_call_target="tpu_custom_call" | custom-call | tf_op jit(solution)/shard_map/krylov/pallas_call | solution.py:718
  84.5 16.4 %all_to_all.10 = f32[128,1,128]{2,1,0:T(1,128)S(1)} all-to-all(f32[128,1,128]{2,1,0:T(1,128)S(1)} %bitcast.11), channel_id=1, replica_groups=mesh['gx'=8,'gy'=16] {'gx','gy'}, dimensions={0} | all-to-all | bytes 131072 | tf_op jit(solution)/shard_map/all_to_all | solution.py:810
  100.9 1.6 %finish.1 = f32[2,512,512]{2,1,0:T(8,128)} custom-call(f32[128,128]{1,0:T(8,128)S(1)} %bitcast.10, f32[2,5,544,128]{3,2,1,0:T(8,128)S(1)} %get-tuple-element.48.b, f32[2,5,544,128]{3,2,1,0:T(8,128)S(1)} %get-tuple-element.49.w1, f32[2,5,544,128]{3,2,1,0:T(8,128)S(1)} %get-tuple-element.50.w2), custom_call_target="tpu_custom_call" | custom-call | tf_op jit(solution)/shard_map/finish/pallas_call | solution.py:793
  (16 shorter events, 0.0 us)
Async XLA Ops:
  0.6 1.0 %copy-start.5 = (f32[256,512]{1,0:T(8,128)S(1)}, f32[256,512]{1,0:T(8,128)}, u32[]{:S(2)}) copy-start(f32[256,512]{1,0:T(8,128)} %h.3) | copy-start | bytes 1572868
  1.7 3.9 %copy-start.6 = (f32[256,512]{1,0:T(8,128)S(1)}, f32[256,512]{1,0:T(8,128)}, u32[]{:S(2)}) copy-start(f32[256,512]{1,0:T(8,128)} %h.3) | copy-start | bytes 1572868
  2.8 12.4 %copy-start.1 = (f32[2,256,512]{2,1,0:T(8,128)S(1)}, f32[2,256,512]{2,1,0:T(8,128)}, u32[]{:S(2)}) copy-start(f32[2,256,512]{2,1,0:T(8,128)} %m.3) | copy-start | bytes 3145732
  2.8 12.4 %copy-start.2 = (f32[2,256,512]{2,1,0:T(8,128)S(1)}, f32[2,256,512]{2,1,0:T(8,128)}, u32[]{:S(2)}) copy-start(f32[2,256,512]{2,1,0:T(8,128)} %b.3) | copy-start | bytes 3145732
  2.8 12.4 %copy-start.7 = (f32[256,512]{1,0:T(8,128)S(1)}, f32[256,512]{1,0:T(8,128)}, u32[]{:S(2)}) copy-start(f32[256,512]{1,0:T(8,128)} %f.3) | copy-start | bytes 1572868
  2.8 5.1 %collective-permute-start = (f32[16,512]{1,0:T(8,128)S(1)}, f32[16,512]{1,0:T(8,128)S(1)}, u32[]{:S(2)}, u32[]{:S(2)}) collective-permute-start(f32[16,512]{1,0:T(8,128)S(1)} %get-tuple-element.27), channel_id=1, source_target_pairs={{0,16},{16,32},{32,48},{48,64},{64,80},{80,96},{96,112},{112,0},{1... | collective-permute-start | bytes 98312 | tf_op jit(solution)/shard_map/ppermute | solution.py:806
  5.5 3.3 %collective-permute-start.1 = (f32[16,512]{1,0:T(8,128)S(1)}, f32[16,512]{1,0:T(8,128)S(1)}, u32[]{:S(2)}, u32[]{:S(2)}) collective-permute-start(f32[16,512]{1,0:T(8,128)S(1)} %get-tuple-element.28), channel_id=1, source_target_pairs={{0,112},{16,0},{32,16},{48,32},{64,48},{80,64},{96,80},{112,96},{1... | collective-permute-start | bytes 98312 | tf_op jit(solution)/shard_map/ppermute | solution.py:806
  5.5 9.7 %copy-start.8 = (s32[256,512]{1,0:T(8,128)S(1)}, s32[256,512]{1,0:T(8,128)}, u32[]{:S(2)}) copy-start(s32[256,512]{1,0:T(8,128)} %a.3) | copy-start | bytes 1572868
  9.1 9.7 %collective-permute-start.2 = (f32[8,1536]{1,0:T(8,128)S(1)}, f32[8,1536]{1,0:T(8,128)S(1)}, u32[]{:S(2)}, u32[]{:S(2)}) collective-permute-start(f32[8,1536]{1,0:T(8,128)S(1)} %get-tuple-element.29.to_right), channel_id=1, source_target_pairs={{0,1},{1,2},{2,3},{3,4},{4,5},{5,6},{6,7},{7,8},{8,9},{9,10},{10,1... | collective-permute-start | bytes 147464 | tf_op jit(solution)/shard_map/ppermute | solution.py:806
  10.4 8.4 %copy-start.14 = (s32[1,1,256,1]{2,3,1,0:T(1,128)S(1)}, s32[1,1,256,1]{2,3,1,0:T(1,128)}, u32[]{:S(2)}) copy-start(s32[1,1,256,1]{2,3,1,0:T(1,128)} %param.15) | copy-start | bytes 3076
  10.4 8.4 %copy-start.15 = (s32[1,1,256]{2,1,0:T(1,128)S(1)}, s32[1,1,256]{2,1,0:T(1,128)}, u32[]{:S(2)}) copy-start(s32[1,1,256]{2,1,0:T(1,128)} %param.16) | copy-start | bytes 3076
  10.4 8.4 %collective-permute-start.3 = (f32[8,1536]{1,0:T(8,128)S(1)}, f32[8,1536]{1,0:T(8,128)S(1)}, u32[]{:S(2)}, u32[]{:S(2)}) collective-permute-start(f32[8,1536]{1,0:T(8,128)S(1)} %get-tuple-element.30.to_left), channel_id=1, source_target_pairs={{0,15},{1,0},{2,1},{3,2},{4,3},{5,4},{6,5},{7,6},{8,7},{9,8},{10,9... | collective-permute-start | bytes 147464 | tf_op jit(solution)/shard_map/ppermute | solution.py:806
  21.9 48.8 %all-to-all-start = ((f32[128,49,1,128]{3,2,1,0:T(1,128)}), f32[128,49,1,128]{3,2,1,0:T(1,128)S(1)}, u32[]{:S(2)}, u32[]{:S(2)}) async-start(f32[128,49,1,128]{3,2,1,0:T(1,128)} %bitcast.14), calls=%async_computation | async-start | bytes 6422528 | tf_op jit(solution)/shard_map/all_to_all | solution.py:810
  29.3 1.2 %copy-start = (f32[512,512]{1,0:T(8,128)S(1)}, f32[512,512]{1,0:T(8,128)}, u32[]{:S(2)}) copy-start(f32[512,512]{1,0:T(8,128)} %d.3) | copy-start | bytes 3145732
  30.5 1.6 %copy-start.3 = (f32[2,512,512]{2,1,0:T(8,128)S(1)}, f32[2,512,512]{2,1,0:T(8,128)}, u32[]{:S(2)}) copy-start(f32[2,512,512]{2,1,0:T(8,128)} %l) | copy-start | bytes 6291460
  32.1 6.4 %copy-start.4 = (f32[2,512,512]{2,1,0:T(8,128)S(1)}, f32[2,512,512]{2,1,0:T(8,128)}, u32[]{:S(2)}) copy-start(f32[2,512,512]{2,1,0:T(8,128)} %l) | copy-start | bytes 6291460
  32.9 35.7 %collective-permute-start.4 = (f32[8,640]{1,0:T(8,128)S(1)}, f32[8,640]{1,0:T(8,128)S(1)}, u32[]{:S(2)}, u32[]{:S(2)}) collective-permute-start(f32[8,640]{1,0:T(8,128)S(1)} %get-tuple-element.38), channel_id=1, source_target_pairs={{0,1},{1,2},{2,3},{3,4},{4,5},{5,6},{6,7},{7,8},{8,9},{9,10},{10,1... | collective-permute-start | bytes 61448 | tf_op jit(solution)/shard_map/ppermute | solution.py:806
  34.3 34.3 %collective-permute-start.5 = (f32[8,640]{1,0:T(8,128)S(1)}, f32[8,640]{1,0:T(8,128)S(1)}, u32[]{:S(2)}, u32[]{:S(2)}) collective-permute-start(f32[8,640]{1,0:T(8,128)S(1)} %get-tuple-element.39), channel_id=1, source_target_pairs={{0,15},{1,0},{2,1},{3,2},{4,3},{5,4},{6,5},{7,6},{8,7},{9,8},{10,9... | collective-permute-start | bytes 61448 | tf_op jit(solution)/shard_map/ppermute | solution.py:806
  38.7 1.3 %copy-start.9 = (f32[2,4,512,128]{3,2,1,0:T(8,128)}, f32[2,4,512,128]{3,2,1,0:T(8,128)S(1)}, u32[]{:S(2)}) copy-start(f32[2,4,512,128]{3,2,1,0:T(8,128)S(1)} %get-tuple-element.43.momentum) | copy-start | bytes 6291460
  40.0 1.0 %copy-start.11 = (f32[4,544,128]{2,1,0:T(8,128)}, f32[4,544,128]{2,1,0:T(8,128)S(1)}, u32[]{:S(2)}) copy-start(f32[4,544,128]{2,1,0:T(8,128)S(1)} %get-tuple-element.46.coef) | copy-start | bytes 3342340
  70.7 4.0 %copy-start.13 = (f32[512,512]{1,0:T(8,128)S(1)}, f32[512,512]{1,0:T(8,128)}, u32[]{:S(2)}) copy-start(f32[512,512]{1,0:T(8,128)} %height.1) | copy-start | bytes 3145732
  73.6 3.0 %collective-permute-start.6 = (f32[2,5,8,128]{3,2,1,0:T(8,128)S(1)}, f32[2,5,8,128]{3,2,1,0:T(8,128)S(1)}, u32[]{:S(2)}, u32[]{:S(2)}) collective-permute-start(f32[2,5,8,128]{3,2,1,0:T(8,128)S(1)} %get-tuple-element.44), channel_id=1, source_target_pairs={{0,16},{16,32},{32,48},{48,64},{64,80},{80,96},{96,112},{112,0},{1... | collective-permute-start | bytes 122888 | tf_op jit(solution)/shard_map/ppermute | solution.py:806
  74.8 3.7 %copy-start.10 = (f32[2,4,512,128]{3,2,1,0:T(8,128)S(1)}, f32[2,4,512,128]{3,2,1,0:T(8,128)}, u32[]{:S(2)}) copy-start(f32[2,4,512,128]{3,2,1,0:T(8,128)} %copy-done.9) | copy-start | bytes 6291460
  74.8 3.7 %copy-start.12 = (f32[4,544,128]{2,1,0:T(8,128)S(1)}, f32[4,544,128]{2,1,0:T(8,128)}, u32[]{:S(2)}) copy-start(f32[4,544,128]{2,1,0:T(8,128)} %copy-done.11) | copy-start | bytes 3342340
  74.8 3.7 %collective-permute-start.7 = (f32[2,5,8,128]{3,2,1,0:T(8,128)S(1)}, f32[2,5,8,128]{3,2,1,0:T(8,128)S(1)}, u32[]{:S(2)}, u32[]{:S(2)}) collective-permute-start(f32[2,5,8,128]{3,2,1,0:T(8,128)S(1)} %get-tuple-element.45), channel_id=1, source_target_pairs={{0,112},{16,0},{32,16},{48,32},{64,48},{80,64},{96,80},{112,96},{1... | collective-permute-start | bytes 122888 | tf_op jit(solution)/shard_map/ppermute | solution.py:806

commit v6 on v5

--- a/solution.py
+++ b/solution.py
@@ -526,18 +526,15 @@
     )(d, lm, above, below)
 
 
-def lake_turn(from_left, from_right, t):
-    gap, s = jnp.zeros((56, 128), F32), slice(128 * t, 128 * t + 128)
-    return jnp.concatenate([from_left[:, s], gap, from_right[:, s], gap], axis=0).T
-
-
-def lake_halo(sides, w, i):
+def lake_halo(sides, from_left, from_right, t, i):
     _, _, on_left, on_right = present(sides)
     at, wide = LAKE_CHANNELS[i]
-    lane = lanes(w.shape)
-    left = pltpu.roll(w, 128 - wide - at, 1)
-    right = pltpu.roll(w, 64 - at, 1)
-    return jnp.where(lane >= 128 - wide, on_left * left, jnp.where(lane < wide, on_right * right, 0.0))
+    s, row = slice(128 * t, 128 * t + 128), rows((8, 128))
+    right = from_right[:, s] if at == 0 else pltpu.roll(from_right[:, s], 8 - at, 0)
+    left = from_left[:, s] if at + wide == 8 else pltpu.roll(from_left[:, s], 8 - wide - at, 0)
+    right = jnp.where(row < wide, on_right * right, 0.0)
+    left = jnp.where(row >= 8 - wide, on_left * left, 0.0)
+    return jnp.concatenate([right, jnp.zeros((112, 128), F32), left], axis=0).T
 
 
 def one_hot(hot, tags, first):
@@ -574,11 +571,11 @@
         flow[c, 4, :, :] = pick(side, split2(jnp.concatenate(left + right, axis=0)))
     first[:, 0:4, :, :] = first_momentum[...] + flow[:, 0:4, 0:8, :]
     last[:, 0:4, :, :] = last_momentum[...] + flow[:, 0:4, L - 8 : L, :]
-    top = lake_turn(from_left, from_right, 0)[0:8, :]
-    bottom = lake_turn(from_left, from_right, L // 128 - 1)[120:128, :]
     for c in range(2):
-        first[c, 4, :, :] = lake_halo(sides, top, c + 1) + flow[c, 4, 0:8, :]
-        last[c, 4, :, :] = lake_halo(sides, bottom, c + 1) + flow[c, 4, L - 8 : L, :]
+        top = lake_halo(sides, from_left, from_right, 0, c + 1)
+        first[c, 4, :, :] = top[0:8, :] + flow[c, 4, 0:8, :]
+        bottom = lake_halo(sides, from_left, from_right, L // 128 - 1, c + 1)
+        last[c, 4, :, :] = bottom[120:128, :] + flow[c, 4, L - 8 : L, :]
 
 
 def place(sides, recv, first_momentum, last_momentum, from_left, from_right):
@@ -610,7 +607,7 @@
     )(recv, height)
 
 
-def krylov_kernel(sides, flow, momentum, above, below, coef, from_left, from_right, b, w1, w2, sums, turn, side_coef):
+def krylov_kernel(sides, flow, momentum, above, below, coef, from_left, from_right, b, w1, w2, sums, side_coef):
     for x in (b, w1, w2):
         x[:, :, 0 : LTOP - 8, :] = jnp.zeros((2, 5, LTOP - 8, 128), F32)
         x[:, :, LTOP + L + 8 :, :] = jnp.zeros((2, 5, LTOP - 8, 128), F32)
@@ -622,18 +619,19 @@
     def total_side(t, _):
         r = pl.multiple_of(t * 64, 64)
         s, to = pl.ds(r, 64), pl.ds(pl.multiple_of(LTOP + r, 8), 64)
-        w = turn[s, :]
-        side_coef[to, :] = 2.0 * lake_halo(sides, w, 0) - 2.0
         for i in range(2):
             for j in range(4):
                 b[i, j, to, :] = flow[i, j, s, :] + momentum[i, j, s, :]
-            b[i, 4, to, :] = flow[i, 4, s, :] + lake_halo(sides, w, i + 1)
         return 0
 
-    for t in range(5):
-        turn[128 * t : 128 * t + 128, :] = lake_turn(from_left, from_right, t)
-    side_coef[LTOP - 8 : LTOP, :] = 2.0 * lake_halo(sides, turn[L + 120 :, :], 0) - 2.0
-    side_coef[LTOP + L : LTOP + L + 8, :] = 2.0 * lake_halo(sides, turn[L : L + 8, :], 0) - 2.0
+    for t in range(4):
+        s, to = slice(128 * t, 128 * t + 128), slice(LTOP + 128 * t, LTOP + 128 * t + 128)
+        side_coef[to, :] = 2.0 * lake_halo(sides, from_left, from_right, t, 0) - 2.0
+        for i in range(2):
+            b[i, 4, to, :] = flow[i, 4, s, :] + lake_halo(sides, from_left, from_right, t, i + 1)
+    ends = 2.0 * lake_halo(sides, from_left, from_right, 4, 0) - 2.0
+    side_coef[LTOP - 8 : LTOP, :] = ends[120:128, :]
+    side_coef[LTOP + L : LTOP + L + 8, :] = ends[0:8, :]
     lax.fori_loop(0, L // 64, total_side, 0)
 
     def image(x, i, r, n):
@@ -720,7 +718,7 @@
         in_specs=[VMEM] * 8,
         out_specs=[VMEM] * 4,
         out_shape=[jax.ShapeDtypeStruct((2, 5, LROWS, 128), F32)] * 3 + [jax.ShapeDtypeStruct((DEV, 128), F32)],
-        scratch_shapes=[pltpu.VMEM((LAKE_WIDTH, 128), F32), pltpu.VMEM((LROWS, 128), F32)],
+        scratch_shapes=[pltpu.VMEM((LROWS, 128), F32)],
         compiler_params=params(24),
         name="krylov",
     )(sides, flow, momentum, above, below, coef, from_left, from_right)

time: 103 us -> 102 us (level)
  no operation moved by 1% of the time
where the time goes in v6:
time: 102 us
  waiting for transfers between devices  32.4 us (32%)
  Pallas kernels  22.9 us (22%)
  starting transfers between devices  22.8 us (22%)
  blocking collectives  16.4 us (16%)
  local copies, waits for them, and re-layouts  6.3 us (6%)
    ppermute x8, waiting for transfers between devices, shift(): return lax.ppermute(x, axis, [(i, (i + by) % n) for i in range(n)])  30.3 us
    all_to_all x1, blocking collectives, exchange(): return lax.all_to_all(x, AXES, split_axis=0, concat_axis=0, tiled=True)  16.4 us
    ppermute x8, starting transfers between devices, shift(): return lax.ppermute(x, axis, [(i, (i + by) % n) for i in range(n)])  15.5 us
    all_to_all x1, starting transfers between devices, exchange(): return lax.all_to_all(x, AXES, split_axis=0, concat_axis=0, tiled=True)  7.36 us
    unnamed x32, local copies, waits for them, and re-layouts  6.23 us
    pallas_call x1, Pallas kernels, krylov(): pl.pallas_call(krylov_kernel, in_specs=[VMEM] * 8, out_specs=[VMEM] * 4,...  5.12 us
    pallas_call x1, Pallas kernels, slope(): pl.pallas_call(slope_kernel, in_specs=[VMEM] * 8, out_shape=jax.ShapeDtyp...  3.55 us
    pallas_call x1, Pallas kernels, pack(): pl.pallas_call(pack_kernel, in_specs=[VMEM] * 8, out_specs=[HBM, HBM], ou...  3.08 us
  transfers between devices with their start and end apart: 9, of which 4 were waited for; matrix products, arithmetic and copies ran while one was open for 0% of the time, Pallas kernels for 9%

profile of v6, /device:TPU:1, one launch (start us, length us, event | category | flops | bytes accessed | tf_op | source)
XLA Modules:
  0.0 101.7 jit_solution(443124410426419221)
XLA Ops:
  0.6 0.0 copy-start.5
  0.6 1.0 %copy-done.5 = f32[256,512]{1,0:T(8,128)S(1)} copy-done((f32[256,512]{1,0:T(8,128)S(1)}, f32[256,512]{1,0:T(8,128)}, u32[]{:S(2)}) %copy-start.5) | copy-done | bytes 524312
  1.7 1.1 %edge_rows.1 = (f32[16,512]{1,0:T(8,128)S(1)}, f32[16,512]{1,0:T(8,128)S(1)}) custom-call(f32[256,512]{1,0:T(8,128)S(1)} %copy-done.5, f32[2,256,512]{2,1,0:T(8,128)} %m.3, f32[2,256,512]{2,1,0:T(8,128)} %b.3, f32[256,512]{1,0:T(8,128)} %f.3, s32[256,512]{1,0:T(8,128)} %a.3, f32[512,512]{1,0:T(8,128)} %d.3), custom_call_target="tpu_custom_call" | custom-call | tf_op jit(solution)/shard_map/edge_rows/pallas_call | solution.py:75
  2.8 0.0 copy-start.1
  2.8 0.0 copy-start.2
  2.8 0.0 copy-start.7
  2.8 2.7 %collective-permute-start = (f32[16,512]{1,0:T(8,128)S(1)}, f32[16,512]{1,0:T(8,128)S(1)}, u32[]{:S(2)}, u32[]{:S(2)}) collective-permute-start(f32[16,512]{1,0:T(8,128)S(1)} %get-tuple-element.27), channel_id=1, source_target_pairs={{0,16},{16,32},{32,48},{48,64},{64,80},{80,96},{96,112},{112,0},{1... | collective-permute-start | bytes 98312 | tf_op jit(solution)/shard_map/ppermute | solution.py:804
  5.5 0.0 collective-permute-start.1
  5.5 0.0 copy-done.6
  5.5 2.4 %edge_columns.1.both = f32[2,8,1536]{2,1,0:T(8,128)S(1)} custom-call(f32[256,512]{1,0:T(8,128)S(1)} %copy-done.6, f32[2,256,512]{2,1,0:T(8,128)} %m.3, f32[2,256,512]{2,1,0:T(8,128)} %b.3, f32[256,512]{1,0:T(8,128)} %f.3, s32[256,512]{1,0:T(8,128)} %a.3), custom_call_target="tpu_custom_call" | custom-call | flops 8388608 | bytes 6291456 | tf_op jit(solution)/shard_map/edge_columns/pallas_call | solution.py:149
  7.9 0.0 collective-permute-done.above
  8.0 0.9 collective-permute-done.1.below
  8.8 0.1 iota.16.sides
  8.9 0.2 corners.1
  9.1 1.3 %collective-permute-start.2 = (f32[8,1536]{1,0:T(8,128)S(1)}, f32[8,1536]{1,0:T(8,128)S(1)}, u32[]{:S(2)}, u32[]{:S(2)}) collective-permute-start(f32[8,1536]{1,0:T(8,128)S(1)} %get-tuple-element.29.to_right), channel_id=1, source_target_pairs={{0,1},{1,2},{2,3},{3,4},{4,5},{5,6},{6,7},{7,8},{8,9},{9,10},{10,1... | collective-permute-start | bytes 147464 | tf_op jit(solution)/shard_map/ppermute | solution.py:804
  10.4 4.8 %collective-permute-start.3 = (f32[8,1536]{1,0:T(8,128)S(1)}, f32[8,1536]{1,0:T(8,128)S(1)}, u32[]{:S(2)}, u32[]{:S(2)}) collective-permute-start(f32[8,1536]{1,0:T(8,128)S(1)} %get-tuple-element.30.to_left), channel_id=1, source_target_pairs={{0,15},{1,0},{2,1},{3,2},{4,3},{5,4},{6,5},{7,6},{8,7},{9,8},{10,9... | collective-permute-start | bytes 147464 | tf_op jit(solution)/shard_map/ppermute | solution.py:804
  15.2 0.0 copy-done.1
  15.2 0.0 copy-done.2
  15.2 0.0 copy-done.7
  15.2 0.0 copy-done.8
  15.2 3.5 %slope.1.fields = f32[3,256,512]{2,1,0:T(8,128)S(1)} custom-call(f32[8,128]{1,0:T(8,128)S(1)} %iota.16.sides, f32[256,512]{1,0:T(8,128)S(1)} %copy-done.6, f32[2,256,512]{2,1,0:T(8,128)S(1)} %copy-done.1, f32[2,256,512]{2,1,0:T(8,128)S(1)} %copy-done.2, f32[256,512]{1,0:T(8,128)S(1)} %copy-done.7, s32[256,512]{1,0:T(8,128)S(1)} %copy-done.8, ...), custom_call_target="tpu_custom_call" | custom-call | flops 33554432 | bytes 6291456 | tf_op jit(solution)/shard_map/slope/pallas_call | solution.py:371
  18.8 0.0 collective-permute-done.2.from_left
  18.8 0.0 collective-permute-done.3.from_right
  18.8 3.1 %pack.1 = (f32[3,256,512]{2,1,0:T(8,128)}, f32[6272,128]{1,0:T(8,128)}) custom-call(f32[8,128]{1,0:T(8,128)S(1)} %iota.16.sides, f32[3,256,512]{2,1,0:T(8,128)S(1)} %slope.1.fields, f32[8,1536]{1,0:T(8,128)S(1)} %get-tuple-element.29.to_right, f32[8,1536]{1,0:T(8,128)S(1)} %get-tuple-element.30.to_left, f32[8,1536]{1,0:T(8,128)S(1)} %collective-permute-done.2.from_left, ...), custom_call_target="tpu_custom_call" | custom-call | tf_op jit(solution)/shard_map/pack/pallas_call | solution.py:478
  21.9 7.4 %all-to-all-start = ((f32[128,49,1,128]{3,2,1,0:T(1,128)}), f32[128,49,1,128]{3,2,1,0:T(1,128)S(1)}, u32[]{:S(2)}, u32[]{:S(2)}) async-start(f32[128,49,1,128]{3,2,1,0:T(1,128)} %bitcast.14), calls=%async_computation | async-start | bytes 6422528 | tf_op jit(solution)/shard_map/all_to_all | solution.py:808
  29.3 0.0 copy-start
  29.3 1.2 %copy-done = f32[512,512]{1,0:T(8,128)S(1)} copy-done((f32[512,512]{1,0:T(8,128)S(1)}, f32[512,512]{1,0:T(8,128)}, u32[]{:S(2)}) %copy-start) | copy-done | bytes 1048600
  30.5 1.6 %copy-done.3 = f32[2,512,512]{2,1,0:T(8,128)S(1)} copy-done((f32[2,512,512]{2,1,0:T(8,128)S(1)}, f32[2,512,512]{2,1,0:T(8,128)}, u32[]{:S(2)}) %copy-start.3) | copy-done | bytes 2097176
  32.1 0.8 lake_columns.1
  32.9 1.4 %collective-permute-start.4 = (f32[8,640]{1,0:T(8,128)S(1)}, f32[8,640]{1,0:T(8,128)S(1)}, u32[]{:S(2)}, u32[]{:S(2)}) collective-permute-start(f32[8,640]{1,0:T(8,128)S(1)} %get-tuple-element.38), channel_id=1, source_target_pairs={{0,1},{1,2},{2,3},{3,4},{4,5},{5,6},{6,7},{7,8},{8,9},{9,10},{10,1... | collective-permute-start | bytes 61448 | tf_op jit(solution)/shard_map/ppermute | solution.py:804
  34.3 4.1 %collective-permute-start.5 = (f32[8,640]{1,0:T(8,128)S(1)}, f32[8,640]{1,0:T(8,128)S(1)}, u32[]{:S(2)}, u32[]{:S(2)}) collective-permute-start(f32[8,640]{1,0:T(8,128)S(1)} %get-tuple-element.39), channel_id=1, source_target_pairs={{0,15},{1,0},{2,1},{3,2},{4,3},{5,4},{6,5},{7,6},{8,7},{9,8},{10,9... | collective-permute-start | bytes 61448 | tf_op jit(solution)/shard_map/ppermute | solution.py:804
  38.5 0.3 prepare.1
  38.7 0.0 copy-start.9
  38.7 1.3 %copy-done.9 = f32[2,4,512,128]{3,2,1,0:T(8,128)} copy-done((f32[2,4,512,128]{3,2,1,0:T(8,128)}, f32[2,4,512,128]{3,2,1,0:T(8,128)S(1)}, u32[]{:S(2)}) %copy-start.9) | copy-done | bytes 2097176
  40.0 1.0 %copy-done.11 = f32[4,544,128]{2,1,0:T(8,128)} copy-done((f32[4,544,128]{2,1,0:T(8,128)}, f32[4,544,128]{2,1,0:T(8,128)S(1)}, u32[]{:S(2)}) %copy-start.11) | copy-done | bytes 1114136
  41.1 27.5 %collective-permute-done.4.from_left = f32[8,640]{1,0:T(8,128)S(1)} collective-permute-done((f32[8,640]{1,0:T(8,128)S(1)}, f32[8,640]{1,0:T(8,128)S(1)}, u32[]{:S(2)}, u32[]{:S(2)}) %collective-permute-start.4) | collective-permute-done | bytes 20512 | tf_op jit(solution)/shard_map/ppermute | solution.py:804
  68.6 0.0 collective-permute-done.5.from_right
  68.6 2.1 %all-to-all-done = f32[128,49,1,128]{3,2,1,0:T(1,128)S(1)} async-done(((f32[128,49,1,128]{3,2,1,0:T(1,128)}), f32[128,49,1,128]{3,2,1,0:T(1,128)S(1)}, u32[]{:S(2)}, u32[]{:S(2)}) %all-to-all-start) | async-done | bytes 3211296 | tf_op jit(solution)/shard_map/all_to_all | solution.py:808
  70.7 2.9 %place.1 = (f32[2,5,512,128]{3,2,1,0:T(8,128)S(1)}, f32[2,5,8,128]{3,2,1,0:T(8,128)S(1)}, f32[2,5,8,128]{3,2,1,0:T(8,128)S(1)}) custom-call(f32[8,128]{1,0:T(8,128)S(1)} %iota.16.sides, f32[6272,128]{1,0:T(8,128)S(1)} %bitcast.8, f32[2,4,8,128]{3,2,1,0:T(8,128)S(1)} %get-tuple-element.36.first_momentum, ...), custom_call_target="tpu_custom_call" | custom-call | tf_op jit(solution)/shard_map/place/pallas_call | solution.py:582
  73.6 1.1 %collective-permute-start.6 = (f32[2,5,8,128]{3,2,1,0:T(8,128)S(1)}, f32[2,5,8,128]{3,2,1,0:T(8,128)S(1)}, u32[]{:S(2)}, u32[]{:S(2)}) collective-permute-start(f32[2,5,8,128]{3,2,1,0:T(8,128)S(1)} %get-tuple-element.44), channel_id=1, source_target_pairs={{0,16},{16,32},{32,48},{48,64},{64,80},{80,96},{96,112},{112,0},{1... | collective-permute-start | bytes 122888 | tf_op jit(solution)/shard_map/ppermute | solution.py:804
  74.8 0.0 collective-permute-start.7
  74.8 1.9 %raise_lake.1 = f32[512,512]{1,0:T(8,128)} custom-call(f32[6272,128]{1,0:T(8,128)S(1)} %bitcast.9, f32[512,512]{1,0:T(8,128)S(1)} %copy-done.13), custom_call_target="tpu_custom_call" | custom-call | flops 629145600 | bytes 6291456 | tf_op jit(solution)/shard_map/raise_lake/pallas_call | solution.py:598
  76.6 0.0 collective-permute-done.6.above
  76.6 1.8 %collective-permute-done.7.below = f32[2,5,8,128]{3,2,1,0:T(8,128)S(1)} collective-permute-done((f32[2,5,8,128]{3,2,1,0:T(8,128)S(1)}, f32[2,5,8,128]{3,2,1,0:T(8,128)S(1)}, u32[]{:S(2)}, u32[]{:S(2)}) %collective-permute-start.7) | collective-permute-done | bytes 40992 | tf_op jit(solution)/shard_map/ppermute | solution.py:804
  78.5 0.0 copy-done.10
  78.5 5.1 %krylov.1 = (f32[2,5,544,128]{3,2,1,0:T(8,128)S(1)}, f32[2,5,544,128]{3,2,1,0:T(8,128)S(1)}, f32[2,5,544,128]{3,2,1,0:T(8,128)S(1)}, f32[128,128]{1,0:T(8,128)S(1)}) custom-call(f32[8,128]{1,0:T(8,128)S(1)} %iota.16.sides, f32[2,5,512,128]{3,2,1,0:T(8,128)S(1)} %get-tuple-element.42.flow, f32[2,4,512,128]{3,2,1,0:T(8,128)S(1)} %copy-done.10, ...), custom_call_target="tpu_custom_call" | custom-call | tf_op jit(solution)/shard_map/krylov/pallas_call | solution.py:716
  83.6 16.4 %all_to_all.10 = f32[128,1,128]{2,1,0:T(1,128)S(1)} all-to-all(f32[128,1,128]{2,1,0:T(1,128)S(1)} %bitcast.11), channel_id=1, replica_groups=mesh['gx'=8,'gy'=16] {'gx','gy'}, dimensions={0} | all-to-all | bytes 131072 | tf_op jit(solution)/shard_map/all_to_all | solution.py:808
  100.0 1.6 %finish.1 = f32[2,512,512]{2,1,0:T(8,128)} custom-call(f32[128,128]{1,0:T(8,128)S(1)} %bitcast.10, f32[2,5,544,128]{3,2,1,0:T(8,128)S(1)} %get-tuple-element.48.b, f32[2,5,544,128]{3,2,1,0:T(8,128)S(1)} %get-tuple-element.49.w1, f32[2,5,544,128]{3,2,1,0:T(8,128)S(1)} %get-tuple-element.50.w2), custom_call_target="tpu_custom_call" | custom-call | tf_op jit(solution)/shard_map/finish/pallas_call | solution.py:791
  (16 shorter events, 0.0 us)
Async XLA Ops:
  0.6 1.0 %copy-start.5 = (f32[256,512]{1,0:T(8,128)S(1)}, f32[256,512]{1,0:T(8,128)}, u32[]{:S(2)}) copy-start(f32[256,512]{1,0:T(8,128)} %h.3) | copy-start | bytes 1572868
  1.7 3.9 %copy-start.6 = (f32[256,512]{1,0:T(8,128)S(1)}, f32[256,512]{1,0:T(8,128)}, u32[]{:S(2)}) copy-start(f32[256,512]{1,0:T(8,128)} %h.3) | copy-start | bytes 1572868
  2.8 12.4 %copy-start.1 = (f32[2,256,512]{2,1,0:T(8,128)S(1)}, f32[2,256,512]{2,1,0:T(8,128)}, u32[]{:S(2)}) copy-start(f32[2,256,512]{2,1,0:T(8,128)} %m.3) | copy-start | bytes 3145732
  2.8 12.4 %copy-start.2 = (f32[2,256,512]{2,1,0:T(8,128)S(1)}, f32[2,256,512]{2,1,0:T(8,128)}, u32[]{:S(2)}) copy-start(f32[2,256,512]{2,1,0:T(8,128)} %b.3) | copy-start | bytes 3145732
  2.8 12.4 %copy-start.7 = (f32[256,512]{1,0:T(8,128)S(1)}, f32[256,512]{1,0:T(8,128)}, u32[]{:S(2)}) copy-start(f32[256,512]{1,0:T(8,128)} %f.3) | copy-start | bytes 1572868
  2.8 5.1 %collective-permute-start = (f32[16,512]{1,0:T(8,128)S(1)}, f32[16,512]{1,0:T(8,128)S(1)}, u32[]{:S(2)}, u32[]{:S(2)}) collective-permute-start(f32[16,512]{1,0:T(8,128)S(1)} %get-tuple-element.27), channel_id=1, source_target_pairs={{0,16},{16,32},{32,48},{48,64},{64,80},{80,96},{96,112},{112,0},{1... | collective-permute-start | bytes 98312 | tf_op jit(solution)/shard_map/ppermute | solution.py:804
  5.5 3.3 %collective-permute-start.1 = (f32[16,512]{1,0:T(8,128)S(1)}, f32[16,512]{1,0:T(8,128)S(1)}, u32[]{:S(2)}, u32[]{:S(2)}) collective-permute-start(f32[16,512]{1,0:T(8,128)S(1)} %get-tuple-element.28), channel_id=1, source_target_pairs={{0,112},{16,0},{32,16},{48,32},{64,48},{80,64},{96,80},{112,96},{1... | collective-permute-start | bytes 98312 | tf_op jit(solution)/shard_map/ppermute | solution.py:804
  5.5 9.7 %copy-start.8 = (s32[256,512]{1,0:T(8,128)S(1)}, s32[256,512]{1,0:T(8,128)}, u32[]{:S(2)}) copy-start(s32[256,512]{1,0:T(8,128)} %a.3) | copy-start | bytes 1572868
  9.1 9.7 %collective-permute-start.2 = (f32[8,1536]{1,0:T(8,128)S(1)}, f32[8,1536]{1,0:T(8,128)S(1)}, u32[]{:S(2)}, u32[]{:S(2)}) collective-permute-start(f32[8,1536]{1,0:T(8,128)S(1)} %get-tuple-element.29.to_right), channel_id=1, source_target_pairs={{0,1},{1,2},{2,3},{3,4},{4,5},{5,6},{6,7},{7,8},{8,9},{9,10},{10,1... | collective-permute-start | bytes 147464 | tf_op jit(solution)/shard_map/ppermute | solution.py:804
  10.4 8.4 %copy-start.14 = (s32[1,1,256,1]{2,3,1,0:T(1,128)S(1)}, s32[1,1,256,1]{2,3,1,0:T(1,128)}, u32[]{:S(2)}) copy-start(s32[1,1,256,1]{2,3,1,0:T(1,128)} %param.15) | copy-start | bytes 3076
  10.4 8.4 %copy-start.15 = (s32[1,1,256]{2,1,0:T(1,128)S(1)}, s32[1,1,256]{2,1,0:T(1,128)}, u32[]{:S(2)}) copy-start(s32[1,1,256]{2,1,0:T(1,128)} %param.16) | copy-start | bytes 3076
  10.4 8.4 %collective-permute-start.3 = (f32[8,1536]{1,0:T(8,128)S(1)}, f32[8,1536]{1,0:T(8,128)S(1)}, u32[]{:S(2)}, u32[]{:S(2)}) collective-permute-start(f32[8,1536]{1,0:T(8,128)S(1)} %get-tuple-element.30.to_left), channel_id=1, source_target_pairs={{0,15},{1,0},{2,1},{3,2},{4,3},{5,4},{6,5},{7,6},{8,7},{9,8},{10,9... | collective-permute-start | bytes 147464 | tf_op jit(solution)/shard_map/ppermute | solution.py:804
  21.9 48.8 %all-to-all-start = ((f32[128,49,1,128]{3,2,1,0:T(1,128)}), f32[128,49,1,128]{3,2,1,0:T(1,128)S(1)}, u32[]{:S(2)}, u32[]{:S(2)}) async-start(f32[128,49,1,128]{3,2,1,0:T(1,128)} %bitcast.14), calls=%async_computation | async-start | bytes 6422528 | tf_op jit(solution)/shard_map/all_to_all | solution.py:808
  29.3 1.2 %copy-start = (f32[512,512]{1,0:T(8,128)S(1)}, f32[512,512]{1,0:T(8,128)}, u32[]{:S(2)}) copy-start(f32[512,512]{1,0:T(8,128)} %d.3) | copy-start | bytes 3145732
  30.5 1.6 %copy-start.3 = (f32[2,512,512]{2,1,0:T(8,128)S(1)}, f32[2,512,512]{2,1,0:T(8,128)}, u32[]{:S(2)}) copy-start(f32[2,512,512]{2,1,0:T(8,128)} %l) | copy-start | bytes 6291460
  32.1 6.4 %copy-start.4 = (f32[2,512,512]{2,1,0:T(8,128)S(1)}, f32[2,512,512]{2,1,0:T(8,128)}, u32[]{:S(2)}) copy-start(f32[2,512,512]{2,1,0:T(8,128)} %l) | copy-start | bytes 6291460
  32.9 35.7 %collective-permute-start.4 = (f32[8,640]{1,0:T(8,128)S(1)}, f32[8,640]{1,0:T(8,128)S(1)}, u32[]{:S(2)}, u32[]{:S(2)}) collective-permute-start(f32[8,640]{1,0:T(8,128)S(1)} %get-tuple-element.38), channel_id=1, source_target_pairs={{0,1},{1,2},{2,3},{3,4},{4,5},{5,6},{6,7},{7,8},{8,9},{9,10},{10,1... | collective-permute-start | bytes 61448 | tf_op jit(solution)/shard_map/ppermute | solution.py:804
  34.3 34.3 %collective-permute-start.5 = (f32[8,640]{1,0:T(8,128)S(1)}, f32[8,640]{1,0:T(8,128)S(1)}, u32[]{:S(2)}, u32[]{:S(2)}) collective-permute-start(f32[8,640]{1,0:T(8,128)S(1)} %get-tuple-element.39), channel_id=1, source_target_pairs={{0,15},{1,0},{2,1},{3,2},{4,3},{5,4},{6,5},{7,6},{8,7},{9,8},{10,9... | collective-permute-start | bytes 61448 | tf_op jit(solution)/shard_map/ppermute | solution.py:804
  38.7 1.3 %copy-start.9 = (f32[2,4,512,128]{3,2,1,0:T(8,128)}, f32[2,4,512,128]{3,2,1,0:T(8,128)S(1)}, u32[]{:S(2)}) copy-start(f32[2,4,512,128]{3,2,1,0:T(8,128)S(1)} %get-tuple-element.43.momentum) | copy-start | bytes 6291460
  40.0 1.0 %copy-start.11 = (f32[4,544,128]{2,1,0:T(8,128)}, f32[4,544,128]{2,1,0:T(8,128)S(1)}, u32[]{:S(2)}) copy-start(f32[4,544,128]{2,1,0:T(8,128)S(1)} %get-tuple-element.46.coef) | copy-start | bytes 3342340
  70.7 4.0 %copy-start.13 = (f32[512,512]{1,0:T(8,128)S(1)}, f32[512,512]{1,0:T(8,128)}, u32[]{:S(2)}) copy-start(f32[512,512]{1,0:T(8,128)} %height.1) | copy-start | bytes 3145732
  73.6 3.0 %collective-permute-start.6 = (f32[2,5,8,128]{3,2,1,0:T(8,128)S(1)}, f32[2,5,8,128]{3,2,1,0:T(8,128)S(1)}, u32[]{:S(2)}, u32[]{:S(2)}) collective-permute-start(f32[2,5,8,128]{3,2,1,0:T(8,128)S(1)} %get-tuple-element.44), channel_id=1, source_target_pairs={{0,16},{16,32},{32,48},{48,64},{64,80},{80,96},{96,112},{112,0},{1... | collective-permute-start | bytes 122888 | tf_op jit(solution)/shard_map/ppermute | solution.py:804
  74.8 3.7 %copy-start.10 = (f32[2,4,512,128]{3,2,1,0:T(8,128)S(1)}, f32[2,4,512,128]{3,2,1,0:T(8,128)}, u32[]{:S(2)}) copy-start(f32[2,4,512,128]{3,2,1,0:T(8,128)} %copy-done.9) | copy-start | bytes 6291460
  74.8 3.7 %copy-start.12 = (f32[4,544,128]{2,1,0:T(8,128)S(1)}, f32[4,544,128]{2,1,0:T(8,128)}, u32[]{:S(2)}) copy-start(f32[4,544,128]{2,1,0:T(8,128)} %copy-done.11) | copy-start | bytes 3342340
  74.8 3.7 %collective-permute-start.7 = (f32[2,5,8,128]{3,2,1,0:T(8,128)S(1)}, f32[2,5,8,128]{3,2,1,0:T(8,128)S(1)}, u32[]{:S(2)}, u32[]{:S(2)}) collective-permute-start(f32[2,5,8,128]{3,2,1,0:T(8,128)S(1)} %get-tuple-element.45), channel_id=1, source_target_pairs={{0,112},{16,0},{32,16},{48,32},{64,48},{80,64},{96,80},{112,96},{1... | collective-permute-start | bytes 122888 | tf_op jit(solution)/shard_map/ppermute | solution.py:804
